TPU v7x, 32 devices: a whole 2x2x4 slice. The times are simulated.
32 devices in a mesh: groups: 2 (over x), tok: 8 (over z, y), head: 2 (over core).
Axes of the slice: x: 2, y: 2, z: 4, core: 2. Of those that a mesh axis runs over, the one named last changes fastest.
Arguments:
- video_query: bfloat16 [2, 4096, 4096], P('groups', ('tok', 'head')), parts along dimension 0, may hold values from -640 to 640
- video_key: bfloat16 [2, 4096, 4096], P('groups', ('tok', 'head')), parts along dimension 0, may hold values from -6 to 6
- video_value: bfloat16 [2, 4096, 4096], P('groups', ('tok', 'head')), parts along dimension 0, may hold values from -6 to 6
- audio_query: bfloat16 [2, 1024, 2048], P('groups', ('tok', 'head')), parts along dimension 0, may hold values from -640 to 640
- audio_key: bfloat16 [2, 1024, 2048], P('groups', ('tok', 'head')), parts along dimension 0, may hold values from -6 to 6
- audio_value: bfloat16 [2, 1024, 2048], P('groups', ('tok', 'head')), parts along dimension 0, may hold values from -6 to 6
- cross_audio_query: bfloat16 [2, 1024, 2048], P('groups', ('tok', 'head')), parts along dimension 0, may hold values from -640 to 640
- cross_video_key: bfloat16 [2, 4096, 2048], P('groups', ('tok', 'head')), parts along dimension 0, may hold values from -6 to 6
- cross_video_value: bfloat16 [2, 4096, 2048], P('groups', ('tok', 'head')), parts along dimension 0, may hold values from -6 to 6
- cross_video_query: bfloat16 [2, 4096, 2048], P('groups', ('tok', 'head')), parts along dimension 0, may hold values from -640 to 640
- cross_audio_key: bfloat16 [2, 1024, 2048], P('groups', ('tok', 'head')), parts along dimension 0, may hold values from -6 to 6
- cross_audio_value: bfloat16 [2, 1024, 2048], P('groups', ('tok', 'head')), parts along dimension 0, may hold values from -6 to 6
- audio_frames: int32 [2, 1024], P('groups', ('tok', 'head')), parts along dimension 0, may hold values from 0 to 15
- into_audio_slope: float32 [32], replicated, may hold values from 0.05 to 0.5
- into_video_slope: float32 [32], replicated, may hold values from 0.05 to 0.5
- timestep: int32 [2], P('groups'), parts along dimension 0, may hold values from 0 to 63
- video_gate: bfloat16 [64, 4096], replicated, may hold values from 2 to 12
- audio_gate: bfloat16 [64, 2048], replicated, may hold values from 2 to 12
- into_audio_gate: bfloat16 [64, 2048], replicated, may hold values from 2 to 12
- into_video_gate: bfloat16 [64, 2048], replicated, may hold values from 2 to 12
Outputs:
- video_self: bfloat16 [2, 4096, 4096], P('groups', ('tok', 'head')), parts along dimension 0
- audio_self: bfloat16 [2, 1024, 2048], P('groups', ('tok', 'head')), parts along dimension 0
- audio_cross: bfloat16 [2, 1024, 2048], P('groups', ('tok', 'head')), parts along dimension 0
- video_cross: bfloat16 [2, 4096, 2048], P('groups', ('tok', 'head')), parts along dimension 0
There are 2 independent parts, one for each index of `groups`. A program takes and returns all parts, laid end to end along the dimension named above; an argument that names none is the same for every part. Nothing has to cross between parts.
All inputs are finite; a program needn't handle non-finite values.
Results may differ from a plain program's by a relative error of at most 0.0075.
Values may be sent and summed in bfloat16 or wider, within the bound.
No kernel may reach another device: no remote copies, remote signals or barrier semaphores. Data moves between devices by JAX's collectives and lax.ppermute only.
A program may use at most 128 MiB of HBM per device.

v0:
```python
import math

import jax
import jax.numpy as jnp
from jax import lax
from jax.sharding import PartitionSpec as P

LV = 4096
FRAMES = 16
DHV = 128
DHA = 64


def partner(value, axis, stride):
    mask = 2**stride
    pairs = [(source, source ^ mask) for source in range(lax.axis_size(axis))]
    return lax.ppermute(value, axis, pairs)


def split_heads(tensor, head_width):
    samples, counted, columns = tensor.shape
    heads_here = columns // head_width
    return (
        tensor.reshape(samples, counted, heads_here, head_width)
        .transpose(0, 2, 1, 3)
        .reshape(samples * heads_here, counted, head_width)
    )


def join_heads(tensor, samples):
    folded, counted, head_width = tensor.shape
    heads_here = folded // samples
    return (
        tensor.reshape(samples, heads_here, counted, head_width)
        .transpose(0, 2, 1, 3)
        .reshape(samples, counted, heads_here * head_width)
    )


def spread(places, samples, heads_here):
    if places.ndim == 1:
        places = places[None, :]
    counted = places.shape[1]
    return jnp.broadcast_to(places[:, None, :], (samples, heads_here, counted)).reshape(
        samples * heads_here, counted
    )


def lane_rows(which_lane, counted, tok_count, head_count):
    tok_ids = jnp.arange(tok_count, dtype=jnp.int32)[:, None]
    return (tok_ids * head_count + which_lane) * counted + jnp.arange(counted, dtype=jnp.int32)[
        None, :
    ]


def key_order(my_lane, other_lane, counted, tok_count, head_count):
    own_rows = lane_rows(my_lane, counted, tok_count, head_count)
    their_rows = lane_rows(other_lane, counted, tok_count, head_count)
    return jnp.concatenate((own_rows.reshape(-1), their_rows.reshape(-1)))


def attend(queries, keyed, valued, slopes, query_places, key_places):
    folded, counted, head_width = queries.shape
    block_rows = math.gcd(counted, 512)
    blocks_count = counted // block_rows
    score_scale = 1.0 / math.sqrt(head_width)
    query_blocks = queries.reshape(folded, blocks_count, block_rows, head_width).transpose(
        1, 0, 2, 3
    )
    place_blocks = query_places.reshape(folded, blocks_count, block_rows).transpose(1, 0, 2)

    def one_block(packed):
        query_block, place_block = packed
        logit_scores = (
            jnp.einsum("fqd,fkd->fqk", query_block, keyed, preferred_element_type=jnp.float32)
            * score_scale
        )
        if slopes is not None:
            logit_scores = logit_scores - slopes[:, None, None] * jnp.abs(
                place_block[:, :, None] - key_places[:, None, :]
            )
        maxima = jnp.max(logit_scores, axis=2)
        exps = jnp.exp(logit_scores - maxima[:, :, None])
        totals = jnp.sum(exps, axis=2)
        weighted_sum = jnp.einsum(
            "fqk,fkd->fqd", exps.astype(jnp.bfloat16), valued, preferred_element_type=jnp.float32
        )
        return (weighted_sum, maxima, totals)

    weighted_sum, maxima, totals = lax.map(one_block, (query_blocks, place_blocks))
    return (
        weighted_sum.transpose(1, 0, 2, 3).reshape(folded, counted, head_width),
        maxima.transpose(1, 0, 2).reshape(folded, counted),
        totals.transpose(1, 0, 2).reshape(folded, counted),
    )


def finish(partials, gate_values, samples):
    weighted_sum, maxima, totals = partials
    gated = weighted_sum / totals[:, :, None] * gate_values
    return join_heads(gated.astype(jnp.bfloat16), samples)


def on_device(
    video_query,
    video_key,
    video_value,
    audio_query,
    audio_key,
    audio_value,
    cross_audio_query,
    cross_video_key,
    cross_video_value,
    cross_video_query,
    cross_audio_key,
    cross_audio_value,
    audio_frames,
    into_audio_slope,
    into_video_slope,
    timestep,
    video_gate,
    audio_gate,
    into_audio_gate,
    into_video_gate,
):
    samples, video_rows, video_columns = video_query.shape
    audio_rows = audio_query.shape[1]
    tok_count = lax.axis_size("tok")
    head_count = lax.axis_size("head")
    my_lane = lax.axis_index("head")
    other_lane = 1 - my_lane
    head_first = lax.axis_index("tok")
    patches = LV // FRAMES
    audio_times = lax.all_gather(audio_frames, ("tok", "head"), axis=1, tiled=True).astype(
        jnp.float32
    )
    levels = jnp.arange(video_gate.shape[0], dtype=jnp.int32)
    picker = (timestep[:, None] == levels[None, :]).astype(jnp.bfloat16)

    def video_places(row_ids):
        return (row_ids // patches).astype(jnp.float32)

    def audio_places(row_ids):
        return jnp.take(audio_times, row_ids, axis=1)

    def gate_columns(table, head_width, heads_here):
        row_values = jnp.dot(picker, table, preferred_element_type=jnp.float32)
        picked = lax.dynamic_slice_in_dim(
            row_values, head_first * heads_here * head_width, heads_here * head_width, 1
        )
        return picked.reshape(samples * heads_here, 1, head_width)

    def slope_columns(table, heads_here):
        picked = lax.dynamic_slice_in_dim(table, head_first * heads_here, heads_here, 0)
        return picked[None, :].reshape(-1)

    own_video = lane_rows(my_lane, video_rows, tok_count, head_count).reshape(-1)
    own_audio = lane_rows(my_lane, audio_rows, tok_count, head_count).reshape(-1)
    moved = (
        lax.all_to_all(video_query, "tok", split_axis=2, concat_axis=1, tiled=True),
        lax.all_to_all(video_key, "tok", split_axis=2, concat_axis=1, tiled=True),
        lax.all_to_all(video_value, "tok", split_axis=2, concat_axis=1, tiled=True),
        lax.all_to_all(audio_query, "tok", split_axis=2, concat_axis=1, tiled=True),
        lax.all_to_all(audio_key, "tok", split_axis=2, concat_axis=1, tiled=True),
        lax.all_to_all(audio_value, "tok", split_axis=2, concat_axis=1, tiled=True),
        lax.all_to_all(cross_audio_query, "tok", split_axis=2, concat_axis=1, tiled=True),
        lax.all_to_all(cross_video_key, "tok", split_axis=2, concat_axis=1, tiled=True),
        lax.all_to_all(cross_video_value, "tok", split_axis=2, concat_axis=1, tiled=True),
        lax.all_to_all(cross_video_query, "tok", split_axis=2, concat_axis=1, tiled=True),
        lax.all_to_all(cross_audio_key, "tok", split_axis=2, concat_axis=1, tiled=True),
        lax.all_to_all(cross_audio_value, "tok", split_axis=2, concat_axis=1, tiled=True),
    )
    (
        moved_video_query,
        moved_video_key,
        moved_video_value,
        moved_audio_query,
        moved_audio_key,
        moved_audio_value,
        moved_cross_audio_query,
        moved_cross_video_key,
        moved_cross_video_value,
        moved_cross_video_query,
        moved_cross_audio_key,
        moved_cross_audio_value,
    ) = moved
    partner_pieces = partner(
        (
            moved_video_key,
            moved_video_value,
            moved_audio_key,
            moved_audio_value,
            moved_cross_audio_key,
            moved_cross_audio_value,
            moved_cross_audio_query,
        ),
        "head",
        0,
    )
    full_video_key = jnp.concatenate((moved_video_key, partner_pieces[0]), axis=1)
    full_video_value = jnp.concatenate((moved_video_value, partner_pieces[1]), axis=1)
    full_audio_key = jnp.concatenate((moved_audio_key, partner_pieces[2]), axis=1)
    full_audio_value = jnp.concatenate((moved_audio_value, partner_pieces[3]), axis=1)
    full_cross_audio_key = jnp.concatenate((moved_cross_audio_key, partner_pieces[4]), axis=1)
    full_cross_audio_value = jnp.concatenate((moved_cross_audio_value, partner_pieces[5]), axis=1)
    partner_query = partner_pieces[6]
    video_heads = moved_video_query.shape[2] // DHV
    audio_heads = moved_audio_query.shape[2] // DHA
    audio_key_rows = key_order(my_lane, other_lane, audio_rows, tok_count, head_count)
    still_video = jnp.zeros((samples * video_heads, own_video.shape[0]), jnp.float32)
    still_audio = jnp.zeros((samples * audio_heads, own_audio.shape[0]), jnp.float32)
    video_self = finish(
        attend(
            split_heads(moved_video_query, DHV),
            split_heads(full_video_key, DHV),
            split_heads(full_video_value, DHV),
            None,
            still_video,
            None,
        ),
        gate_columns(video_gate, DHV, video_heads),
        samples,
    )
    audio_self = finish(
        attend(
            split_heads(moved_audio_query, DHA),
            split_heads(full_audio_key, DHA),
            split_heads(full_audio_value, DHA),
            None,
            still_audio,
            None,
        ),
        gate_columns(audio_gate, DHA, audio_heads),
        samples,
    )
    video_slopes = slope_columns(into_video_slope, audio_heads)
    video_cross = finish(
        attend(
            split_heads(moved_cross_video_query, DHA),
            split_heads(full_cross_audio_key, DHA),
            split_heads(full_cross_audio_value, DHA),
            video_slopes,
            spread(video_places(own_video), samples, audio_heads),
            spread(audio_places(audio_key_rows), samples, audio_heads),
        ),
        gate_columns(into_video_gate, DHA, audio_heads),
        samples,
    )
    audio_slopes = slope_columns(into_audio_slope, audio_heads)
    own_audio_places = spread(audio_places(own_audio), samples, audio_heads)
    own_keys = split_heads(moved_cross_video_key, DHA)
    own_values = split_heads(moved_cross_video_value, DHA)
    own_key_places = spread(video_places(own_video), samples, audio_heads)
    own_part = attend(
        split_heads(moved_cross_audio_query, DHA),
        own_keys,
        own_values,
        audio_slopes,
        own_audio_places,
        own_key_places,
    )
    partner_audio = lane_rows(other_lane, audio_rows, tok_count, head_count).reshape(-1)
    their_part = attend(
        split_heads(partner_query, DHA),
        own_keys,
        own_values,
        audio_slopes,
        spread(audio_places(partner_audio), samples, audio_heads),
        own_key_places,
    )
    returned = partner((their_part[0], their_part[1], their_part[2]), "head", 0)
    maxima = jnp.maximum(own_part[1], returned[1])
    own_factor = jnp.exp(own_part[1] - maxima)
    their_factor = jnp.exp(returned[1] - maxima)
    merged = (
        own_part[0] * own_factor[:, :, None] + returned[0] * their_factor[:, :, None],
        maxima,
        own_part[2] * own_factor + returned[2] * their_factor,
    )
    audio_cross = finish(merged, gate_columns(into_audio_gate, DHA, audio_heads), samples)
    return (
        lax.all_to_all(video_self, "tok", split_axis=1, concat_axis=2, tiled=True),
        lax.all_to_all(audio_self, "tok", split_axis=1, concat_axis=2, tiled=True),
        lax.all_to_all(audio_cross, "tok", split_axis=1, concat_axis=2, tiled=True),
        lax.all_to_all(video_cross, "tok", split_axis=1, concat_axis=2, tiled=True),
    )


def solution(mesh):
    placed = (
        P("groups", ("tok", "head"), None),
        P("groups", ("tok", "head"), None),
        P("groups", ("tok", "head"), None),
        P("groups", ("tok", "head"), None),
        P("groups", ("tok", "head"), None),
        P("groups", ("tok", "head"), None),
        P("groups", ("tok", "head"), None),
        P("groups", ("tok", "head"), None),
        P("groups", ("tok", "head"), None),
        P("groups", ("tok", "head"), None),
        P("groups", ("tok", "head"), None),
        P("groups", ("tok", "head"), None),
        P("groups", ("tok", "head")),
        P(),
        P(),
        P("groups"),
        P(),
        P(),
        P(),
        P(),
    )
    return jax.shard_map(
        on_device,
        mesh=mesh,
        in_specs=placed,
        out_specs=(
            P("groups", ("tok", "head"), None),
            P("groups", ("tok", "head"), None),
            P("groups", ("tok", "head"), None),
            P("groups", ("tok", "head"), None),
        ),
        check_vma=False,
    )
```

profile of v0, /device:TPU:0, one launch (start us, length us, event | category | flops | bytes accessed | tf_op | source)
XLA Modules:
  0.0 952.0 jit_solution(9676572812332082340)
XLA Ops:
  3.5 11.5 %reduce.4 = bf16[2048,64]{1,0:T(8,128)(2,1)S(1)} reduce(bf16[2048,1,64]{2,1,0:T(2,128)(2,1)S(1)} %bitcast.385, bf16[]{:T(256)} %broadcast.313), dimensions={1}, to_apply=%bitcast.262.reduce_sub_computation | reduce | bytes 524290
  16.1 7.3 all-to-all-start.6
  24.2 11.5 %reduce.5 = bf16[2048,64]{1,0:T(8,128)(2,1)S(1)} reduce(bf16[2048,1,64]{2,1,0:T(2,128)(2,1)S(1)} %bitcast.386, bf16[]{:T(256)} %broadcast.313), dimensions={1}, to_apply=%bitcast.264.reduce_sub_computation | reduce | bytes 524290
  36.8 6.2 all-to-all-start.4
  43.8 11.5 %reduce.6 = bf16[2048,64]{1,0:T(8,128)(2,1)S(1)} reduce(bf16[2048,1,64]{2,1,0:T(2,128)(2,1)S(1)} %bitcast.387, bf16[]{:T(256)} %broadcast.313), dimensions={1}, to_apply=%bitcast.266.reduce_sub_computation | reduce | bytes 524290
  56.4 6.0 all-to-all-start.5
  63.2 11.6 %reduce.8 = bf16[2048,64]{1,0:T(8,128)(2,1)S(1)} reduce(bf16[2048,1,64]{2,1,0:T(2,128)(2,1)S(1)} %bitcast.388, bf16[]{:T(256)} %broadcast.313), dimensions={1}, to_apply=%bitcast.270.reduce_sub_computation | reduce | bytes 524290
  75.8 6.4 all-to-all-start.8
  84.5 11.5 %reduce.13 = bf16[2048,64]{1,0:T(8,128)(2,1)S(1)} reduce(bf16[2048,1,64]{2,1,0:T(2,128)(2,1)S(1)} %bitcast.389, bf16[]{:T(256)} %broadcast.313), dimensions={1}, to_apply=%bitcast.280.reduce_sub_computation | reduce | bytes 524290
  97.1 6.0 all-to-all-start.13
  103.8 11.5 %reduce.14 = bf16[2048,64]{1,0:T(8,128)(2,1)S(1)} reduce(bf16[2048,1,64]{2,1,0:T(2,128)(2,1)S(1)} %bitcast.390, bf16[]{:T(256)} %broadcast.313), dimensions={1}, to_apply=%bitcast.282.reduce_sub_computation | reduce | bytes 524290
  117.1 6.2 all-to-all-start.14
  123.3 4.6 copy.188
  127.9 11.5 %reduce.9 = bf16[2048,256]{1,0:T(8,128)(2,1)} reduce(bf16[2048,1,256]{2,1,0:T(2,128)(2,1)S(1)} %bitcast.372, bf16[]{:T(256)} %broadcast.313), dimensions={1}, to_apply=%bitcast.272.reduce_sub_computation | reduce | bytes 2097154
  141.8 6.0 all-to-all-start.9
  148.3 7.2 copy.157
  155.6 21.6 %reduce = bf16[4096,256]{1,0:T(8,128)(2,1)S(1)} reduce(bf16[4096,1,256]{2,1,0:T(2,128)(2,1)} %bitcast.355, bf16[]{:T(256)} %broadcast.313), dimensions={1}, to_apply=%bitcast.254.reduce_sub_computation | reduce | bytes 4194306
  180.3 10.0 %copy.160 = bf16[1,256,4096]{1,0,2:T(2,128)(2,1)} copy(bf16[1,256,4096]{2,1,0:T(8,128)(2,1)} %param.27) | data formatting | bytes 4194304 | tf_op args[1]
  190.3 21.6 %reduce.1 = bf16[4096,256]{1,0:T(8,128)(2,1)S(1)} reduce(bf16[4096,1,256]{2,1,0:T(2,128)(2,1)} %bitcast.356, bf16[]{:T(256)} %broadcast.313), dimensions={1}, to_apply=%bitcast.256.reduce_sub_computation | reduce | bytes 4194306
  215.1 10.0 %copy.162 = bf16[1,256,4096]{1,0,2:T(2,128)(2,1)} copy(bf16[1,256,4096]{2,1,0:T(8,128)(2,1)} %param.28) | data formatting | bytes 4194304 | tf_op args[2]
  225.1 21.6 %reduce.2 = bf16[4096,256]{1,0:T(8,128)(2,1)S(1)} reduce(bf16[4096,1,256]{2,1,0:T(2,128)(2,1)} %bitcast.357, bf16[]{:T(256)} %broadcast.313), dimensions={1}, to_apply=%bitcast.258.reduce_sub_computation | reduce | bytes 4194306
  252.4 12.7 %all-reduce = s32[1024]{0:T(1024)S(1)} all-reduce(s32[1024]{0:T(1024)S(1)} %bitcast_dynamic-update-slice_fusion.2), channel_id=1, replica_groups=mesh['groups'=2,'tok'=8,'head'=2] {'tok','head'}, use_global_device_ids=true, to_apply=%add | all-reduce | flops 1024 | bytes 8192
  269.7 11.5 %reduce.10 = bf16[2048,256]{1,0:T(8,128)(2,1)} reduce(bf16[2048,1,256]{2,1,0:T(2,128)(2,1)S(1)} %bitcast.373, bf16[]{:T(256)} %broadcast.313), dimensions={1}, to_apply=%bitcast.274.reduce_sub_computation | reduce | bytes 2097154
  293.5 4.6 copy.197
  298.2 11.5 %reduce.12 = bf16[2048,256]{1,0:T(8,128)(2,1)} reduce(bf16[2048,1,256]{2,1,0:T(2,128)(2,1)S(1)} %bitcast.374, bf16[]{:T(256)} %broadcast.313), dimensions={1}, to_apply=%bitcast.278.reduce_sub_computation | reduce | bytes 2097154
  317.1 5.9 all-to-all-start.12
  329.4 16.9 %all-to-all-done.12 = bf16[8,2,32768]{2,1,0:T(2,128)(2,1)S(1)} async-done(((bf16[8,2,32768]{2,1,0:T(2,128)(2,1)}), bf16[8,2,32768]{2,1,0:T(2,128)(2,1)S(1)}, u32[]{:S(2)}, u32[]{:S(2)}) %all-to-all-start.12) | async-done | bytes 1048608 | tf_op jit(solution)/shard_map/all_to_all | solution.py:169
  389.4 8.9 all-to-all-done
  426.0 9.1 fusion.118
  435.2 9.3 fusion.35
  445.0 8.1 fusion.33
  460.8 6.6 all-to-all-start.2
  467.5 28.5 %while.6 = (s32[]{:T(128)}, f32[4,4,512,64]{2,3,1,0:T(8,128)S(1)}, f32[4,4,512]{2,1,0:T(4,128)S(1)}, bf16[4,4,512,64]{2,3,1,0:T(8,128)(2,1)}, bf16[4,1024,64]{1,...) while((s32[]{:T(128)}, f32[4,4,512,64]{2,3,1,0:T(8,128)S(1)}, ...), condition=%wide.region_13.15_spmd.clone, body=%wide.region_10.14_spmd.clone.sunk | while | flops 557838336 | bytes 27078796 | solution.py:90
  496.0 9.5 fusion.119
  505.4 6.8 reshape.515
  519.2 8.1 fusion.31
  538.1 5.9 copy.211
  544.1 12.8 %reduce.15 = bf16[2048,256]{1,0:T(8,128)(2,1)} reduce(bf16[2048,1,256]{2,1,0:T(2,128)(2,1)} %bitcast.369, bf16[]{:T(256)} %broadcast.313), dimensions={1}, to_apply=%bitcast.284.reduce_sub_computation | reduce | bytes 2097154
  559.0 8.8 multiply_convert_fusion.1
  571.2 6.8 reshape.513
  591.1 5.8 all-to-all-start.7
  596.9 6.8 reshape.517
  613.5 24.9 %fusion.47 = bf16[1,16384,128]{2,1,0:T(8,128)(2,1)} fusion(bf16[1,2048,512]{2,1,0:T(8,128)(2,1)} %collective-permute-done, bf16[1,2048,512]{2,1,0:T(8,128)(2,1)S(1)} %bitcast.346, bf16[1,4096,128]{2,1,0:T(8,128)(2,1)S(1)} %get-tuple-element.303, bf16[1,4096,128]{2,1,0:T(8,128)(2,1)S(1)} %get-tuple-element.302, bf16[1,4096,128]{2,1,0:T(8,128)(2,1)S(1)} %get-tuple-element.301), kind=kLoop, calls=%fused_computation.63 | loop fusion | flops 20971520 | bytes 11534336 | tf_op jit(solution)/shard_map/concatenate
  641.7 5.8 all-to-all-start.11
  647.5 12.7 %fusion.46 = bf16[1,16384,128]{2,1,0:T(8,128)(2,1)} fusion(bf16[1,2048,512]{2,1,0:T(8,128)(2,1)} %copy-done.6, bf16[1,2048,512]{2,1,0:T(8,128)(2,1)S(1)} %bitcast.349, bf16[1,4096,128]{2,1,0:T(8,128)(2,1)} %get-tuple-element.300, bf16[1,4096,128]{2,1,0:T(8,128)(2,1)} %get-tuple-element.299, bf16[1,4096,128]{2,1,0:T(8,128)(2,1)} %get-tuple-element.298), kind=kLoop, calls=%fused_computation.61 | loop fusion | flops 20971520 | bytes 11534336 | tf_op jit(solution)/shard_map/concatenate.1
  660.2 6.0 all-to-all-start.15
  666.3 185.7 %while.5 = (s32[]{:T(128)}, f32[4,4,512,128]{3,2,0,1:T(8,128)}, f32[4,4,512]{2,1,0:T(4,128)S(1)}, bf16[4,4,512,128]{3,2,0,1:T(8,128)(2,1)}, bf16[4,4096,128]{2,1...) while((s32[]{:T(128)}, f32[4,4,512,128]{3,2,0,1:T(8,128)}, f32[4,4,512]{2,1,0:T(4,128)S(1)}, ...), condition=%wide.region_3.4_spmd, body=%wide.region_0.3_spmd.sunk | while | flops 4362072064 | bytes 127451264 | solution.py:90
  666.3 18.1 %multiply_reduce_fusion.2 = (f32[4,512]{1,0:T(4,128)S(1)}, f32[4,512,4096]{2,1,0:T(8,128)}) fusion(bf16[4,4096,128]{2,1,0:T(8,128)(2,1)} %get-tuple-element.450, bf16[4,4,512,128]{3,2,0,1:T(8,128)(2,1)} %get-tuple-element.449, s32[]{:T(128)S(6)} %copy.259), kind=kOutput, calls=%fused_computation.5.clone.1 | convolution fusion | flops 2164258816 | bytes 38281220 | tf_op jit(solution)/shard_map/while/body/eval_jaxpr/fqd,fkd->fqk/dot_general | solution.py:75
  684.4 14.3 %fusion.145 = f32[4,4,512,128]{3,2,0,1:T(8,128)} fusion(f32[4,4,512,128]{3,2,0,1:T(8,128)} %get-tuple-element.440, s32[]{:T(128)S(6)} %copy.259, bf16[4,4096,128]{2,1,0:T(8,128)(2,1)S(1)} %copy-done.8, f32[4,512,4096]{2,1,0:T(8,128)} %get-tuple-element.419, f32[4,512]{1,0:T(4,128)S(1)} %get-tuple-element.420), kind=kOutput, calls=%fused_computation.10.clone.1 | convolution fusion | flops 2172649472 | bytes 38805508 | tf_op jit(solution)/shard_map/while/body/eval_jaxpr/fqk,fkd->fqd/dot_general | solution.py:85
  698.7 14.0 %fusion.146 = f32[4,512]{1,0:T(4,128)S(1)} fusion(f32[4,512,4096]{2,1,0:T(8,128)} %get-tuple-element.419, f32[4,512]{1,0:T(4,128)S(1)} %get-tuple-element.420), kind=kLoop, calls=%fused_computation.6.clone.1 | loop fusion | flops 25163776 | bytes 33570816 | tf_op jit(solution)/shard_map/while/body/eval_jaxpr/reduce_sum | solution.py:84
  712.7 18.1 %multiply_reduce_fusion.2 = (f32[4,512]{1,0:T(4,128)S(1)}, f32[4,512,4096]{2,1,0:T(8,128)}) fusion(bf16[4,4096,128]{2,1,0:T(8,128)(2,1)} %get-tuple-element.450, bf16[4,4,512,128]{3,2,0,1:T(8,128)(2,1)} %get-tuple-element.449, s32[]{:T(128)S(6)} %copy.259), kind=kOutput, calls=%fused_computation.5.clone.1 | convolution fusion | flops 2164258816 | bytes 38281220 | tf_op jit(solution)/shard_map/while/body/eval_jaxpr/fqd,fkd->fqk/dot_general | solution.py:75
  730.8 14.3 %fusion.145 = f32[4,4,512,128]{3,2,0,1:T(8,128)} fusion(f32[4,4,512,128]{3,2,0,1:T(8,128)} %get-tuple-element.440, s32[]{:T(128)S(6)} %copy.259, bf16[4,4096,128]{2,1,0:T(8,128)(2,1)S(1)} %copy-done.8, f32[4,512,4096]{2,1,0:T(8,128)} %get-tuple-element.419, f32[4,512]{1,0:T(4,128)S(1)} %get-tuple-element.420), kind=kOutput, calls=%fused_computation.10.clone.1 | convolution fusion | flops 2172649472 | bytes 38805508 | tf_op jit(solution)/shard_map/while/body/eval_jaxpr/fqk,fkd->fqd/dot_general | solution.py:85
  745.1 14.0 %fusion.146 = f32[4,512]{1,0:T(4,128)S(1)} fusion(f32[4,512,4096]{2,1,0:T(8,128)} %get-tuple-element.419, f32[4,512]{1,0:T(4,128)S(1)} %get-tuple-element.420), kind=kLoop, calls=%fused_computation.6.clone.1 | loop fusion | flops 25163776 | bytes 33570816 | tf_op jit(solution)/shard_map/while/body/eval_jaxpr/reduce_sum | solution.py:84
  759.1 18.1 %multiply_reduce_fusion.2 = (f32[4,512]{1,0:T(4,128)S(1)}, f32[4,512,4096]{2,1,0:T(8,128)}) fusion(bf16[4,4096,128]{2,1,0:T(8,128)(2,1)} %get-tuple-element.450, bf16[4,4,512,128]{3,2,0,1:T(8,128)(2,1)} %get-tuple-element.449, s32[]{:T(128)S(6)} %copy.259), kind=kOutput, calls=%fused_computation.5.clone.1 | convolution fusion | flops 2164258816 | bytes 38281220 | tf_op jit(solution)/shard_map/while/body/eval_jaxpr/fqd,fkd->fqk/dot_general | solution.py:75
  777.2 14.3 %fusion.145 = f32[4,4,512,128]{3,2,0,1:T(8,128)} fusion(f32[4,4,512,128]{3,2,0,1:T(8,128)} %get-tuple-element.440, s32[]{:T(128)S(6)} %copy.259, bf16[4,4096,128]{2,1,0:T(8,128)(2,1)S(1)} %copy-done.8, f32[4,512,4096]{2,1,0:T(8,128)} %get-tuple-element.419, f32[4,512]{1,0:T(4,128)S(1)} %get-tuple-element.420), kind=kOutput, calls=%fused_computation.10.clone.1 | convolution fusion | flops 2172649472 | bytes 38805508 | tf_op jit(solution)/shard_map/while/body/eval_jaxpr/fqk,fkd->fqd/dot_general | solution.py:85
  791.5 14.0 %fusion.146 = f32[4,512]{1,0:T(4,128)S(1)} fusion(f32[4,512,4096]{2,1,0:T(8,128)} %get-tuple-element.419, f32[4,512]{1,0:T(4,128)S(1)} %get-tuple-element.420), kind=kLoop, calls=%fused_computation.6.clone.1 | loop fusion | flops 25163776 | bytes 33570816 | tf_op jit(solution)/shard_map/while/body/eval_jaxpr/reduce_sum | solution.py:84
  805.6 18.1 %multiply_reduce_fusion.2 = (f32[4,512]{1,0:T(4,128)S(1)}, f32[4,512,4096]{2,1,0:T(8,128)}) fusion(bf16[4,4096,128]{2,1,0:T(8,128)(2,1)} %get-tuple-element.450, bf16[4,4,512,128]{3,2,0,1:T(8,128)(2,1)} %get-tuple-element.449, s32[]{:T(128)S(6)} %copy.259), kind=kOutput, calls=%fused_computation.5.clone.1 | convolution fusion | flops 2164258816 | bytes 38281220 | tf_op jit(solution)/shard_map/while/body/eval_jaxpr/fqd,fkd->fqk/dot_general | solution.py:75
  823.6 14.3 %fusion.145 = f32[4,4,512,128]{3,2,0,1:T(8,128)} fusion(f32[4,4,512,128]{3,2,0,1:T(8,128)} %get-tuple-element.440, s32[]{:T(128)S(6)} %copy.259, bf16[4,4096,128]{2,1,0:T(8,128)(2,1)S(1)} %copy-done.8, f32[4,512,4096]{2,1,0:T(8,128)} %get-tuple-element.419, f32[4,512]{1,0:T(4,128)S(1)} %get-tuple-element.420), kind=kOutput, calls=%fused_computation.10.clone.1 | convolution fusion | flops 2172649472 | bytes 38805508 | tf_op jit(solution)/shard_map/while/body/eval_jaxpr/fqk,fkd->fqd/dot_general | solution.py:85
  837.9 14.0 %fusion.146 = f32[4,512]{1,0:T(4,128)S(1)} fusion(f32[4,512,4096]{2,1,0:T(8,128)} %get-tuple-element.419, f32[4,512]{1,0:T(4,128)S(1)} %get-tuple-element.420), kind=kLoop, calls=%fused_computation.6.clone.1 | loop fusion | flops 25163776 | bytes 33570816 | tf_op jit(solution)/shard_map/while/body/eval_jaxpr/reduce_sum | solution.py:84
  858.7 7.5 copy.167
  866.3 14.1 %reduce.3 = bf16[2048,512]{1,0:T(8,128)(2,1)S(1)} reduce(bf16[2048,1,512]{2,1,0:T(2,128)(2,1)} %bitcast.350, bf16[]{:T(256)} %broadcast.313), dimensions={1}, to_apply=%bitcast.260.reduce_sub_computation | reduce | bytes 4194306
  884.1 6.1 all-to-all-start.3
  892.4 5.8 reshape.543
  905.4 32.6 %all-to-all-done.3 = bf16[8,2,65536]{2,1,0:T(2,128)(2,1)S(1)} async-done(((bf16[8,2,65536]{2,1,0:T(2,128)(2,1)}), bf16[8,2,65536]{2,1,0:T(2,128)(2,1)S(1)}, u32[]{:S(2)}, u32[]{:S(2)}) %all-to-all-start.3) | async-done | bytes 2097184 | tf_op jit(solution)/shard_map/all_to_all | solution.py:282
  (315 shorter events, 249.6 us)
Async XLA Ops:
  0.6 322.4 %copy-start = (bf16[64,4096]{1,0:T(8,128)(2,1)S(1)}, bf16[64,4096]{1,0:T(8,128)(2,1)}, u32[]{:S(2)}) copy-start(bf16[64,4096]{1,0:T(8,128)(2,1)} %param.42) | copy-start | bytes 1572868
  0.6 22.8 %copy-start.26 = (bf16[1,64,2048]{2,1,0:T(8,128)(2,1)S(1)}, bf16[1,64,2048]{2,1,0:T(8,128)(2,1)}, u32[]{:S(2)}) copy-start(bf16[1,64,2048]{2,1,0:T(8,128)(2,1)} %param.30) | copy-start | bytes 786436
  0.7 42.4 %copy-start.27 = (bf16[1,64,2048]{2,1,0:T(8,128)(2,1)S(1)}, bf16[1,64,2048]{2,1,0:T(8,128)(2,1)}, u32[]{:S(2)}) copy-start(bf16[1,64,2048]{2,1,0:T(8,128)(2,1)} %param.29) | copy-start | bytes 786436
  16.1 20.7 %all-to-all-start.6 = ((bf16[8,2,8192]{2,1,0:T(2,128)(2,1)}), bf16[8,2,8192]{2,1,0:T(2,128)(2,1)S(1)}, u32[]{:S(2)}, u32[]{:S(2)}) async-start(bf16[8,2,8192]{2,1,0:T(2,128)(2,1)} %reshape.520), calls=%async_computation.6 | async-start | bytes 524288 | tf_op jit(solution)/shard_map/all_to_all | solution.py:165
  23.5 38.9 %copy-start.28 = (bf16[1,64,2048]{2,1,0:T(8,128)(2,1)S(1)}, bf16[1,64,2048]{2,1,0:T(8,128)(2,1)}, u32[]{:S(2)}) copy-start(bf16[1,64,2048]{2,1,0:T(8,128)(2,1)} %param.32) | copy-start | bytes 786436
  36.8 19.6 %all-to-all-start.4 = ((bf16[8,2,8192]{2,1,0:T(2,128)(2,1)}), bf16[8,2,8192]{2,1,0:T(2,128)(2,1)S(1)}, u32[]{:S(2)}, u32[]{:S(2)}) async-start(bf16[8,2,8192]{2,1,0:T(2,128)(2,1)} %reshape.522), calls=%async_computation.4 | async-start | bytes 524288 | tf_op jit(solution)/shard_map/all_to_all | solution.py:164
  56.4 40.7 %copy-start.16 = (bf16[8,2,8192]{2,1,0:T(2,128)(2,1)}, bf16[8,2,8192]{2,1,0:T(2,128)(2,1)S(1)}, u32[]{:S(2)}) copy-start(bf16[8,2,8192]{2,1,0:T(2,128)(2,1)S(1)} %all-to-all-done.4) | copy-start | bytes 786436
  56.4 19.4 %all-to-all-start.5 = ((bf16[8,2,8192]{2,1,0:T(2,128)(2,1)}), bf16[8,2,8192]{2,1,0:T(2,128)(2,1)S(1)}, u32[]{:S(2)}, u32[]{:S(2)}) async-start(bf16[8,2,8192]{2,1,0:T(2,128)(2,1)} %reshape.524), calls=%async_computation.5 | async-start | bytes 524288 | tf_op jit(solution)/shard_map/all_to_all | solution.py:163
  63.1 39.9 %copy-start.29 = (bf16[1,64,2048]{2,1,0:T(8,128)(2,1)S(1)}, bf16[1,64,2048]{2,1,0:T(8,128)(2,1)}, u32[]{:S(2)}) copy-start(bf16[1,64,2048]{2,1,0:T(8,128)(2,1)} %param.37) | copy-start | bytes 786436
  75.8 21.3 %all-to-all-start.8 = ((bf16[8,2,8192]{2,1,0:T(2,128)(2,1)}), bf16[8,2,8192]{2,1,0:T(2,128)(2,1)S(1)}, u32[]{:S(2)}, u32[]{:S(2)}) async-start(bf16[8,2,8192]{2,1,0:T(2,128)(2,1)} %reshape.528), calls=%async_computation.8 | async-start | bytes 524288 | tf_op jit(solution)/shard_map/all_to_all | solution.py:166
  97.1 19.4 %copy-start.20 = (bf16[8,2,8192]{2,1,0:T(2,128)(2,1)}, bf16[8,2,8192]{2,1,0:T(2,128)(2,1)S(1)}, u32[]{:S(2)}) copy-start(bf16[8,2,8192]{2,1,0:T(2,128)(2,1)S(1)} %all-to-all-done.8) | copy-start | bytes 786436
  97.1 19.4 %all-to-all-start.13 = ((bf16[8,2,8192]{2,1,0:T(2,128)(2,1)}), bf16[8,2,8192]{2,1,0:T(2,128)(2,1)S(1)}, u32[]{:S(2)}, u32[]{:S(2)}) async-start(bf16[8,2,8192]{2,1,0:T(2,128)(2,1)} %reshape.538), calls=%async_computation.13 | async-start | bytes 524288 | tf_op jit(solution)/shard_map/all_to_all | solution.py:170
  117.1 24.7 %all-to-all-start.14 = ((bf16[8,2,8192]{2,1,0:T(2,128)(2,1)}), bf16[8,2,8192]{2,1,0:T(2,128)(2,1)S(1)}, u32[]{:S(2)}, u32[]{:S(2)}) async-start(bf16[8,2,8192]{2,1,0:T(2,128)(2,1)} %reshape.540), calls=%async_computation.14 | async-start | bytes 524288 | tf_op jit(solution)/shard_map/all_to_all | solution.py:171
  139.5 8.8 copy-start.9
  141.8 13.7 %copy-start.15 = (bf16[8,2,8192]{2,1,0:T(2,128)(2,1)}, bf16[8,2,8192]{2,1,0:T(2,128)(2,1)S(1)}, u32[]{:S(2)}) copy-start(bf16[8,2,8192]{2,1,0:T(2,128)(2,1)S(1)} %all-to-all-done.14) | copy-start | bytes 786436
  141.8 142.8 %all-to-all-start.9 = ((bf16[8,2,32768]{2,1,0:T(2,128)(2,1)}), bf16[8,2,32768]{2,1,0:T(2,128)(2,1)}, u32[]{:S(2)}, u32[]{:S(2)}) async-start(bf16[8,2,32768]{2,1,0:T(2,128)(2,1)} %reshape.530), calls=%async_computation.9 | async-start | bytes 2097152 | tf_op jit(solution)/shard_map/all_to_all | solution.py:167
  225.1 25.5 %copy-start.31 = (bf16[64,2048]{1,0:T(8,128)(2,1)S(1)}, bf16[64,2048]{1,0:T(8,128)(2,1)}, u32[]{:S(2)}) copy-start(bf16[64,2048]{1,0:T(8,128)(2,1)} %param.43) | copy-start | bytes 786436
  225.1 25.9 %copy-start.37 = (u32[32]{0:T(128)S(1)}, u32[32]{0:T(128)}, u32[]{:S(2)}) copy-start(u32[32]{0:T(128)} %constant.179) | copy-start | bytes 388
  225.1 27.2 %copy-start.34 = (s32[1,64]{1,0:T(1,128)S(1)}, s32[1,64]{1,0:T(1,128)}, u32[]{:S(2)}) copy-start(s32[1,64]{1,0:T(1,128)} %param.38) | copy-start | bytes 772
  284.6 32.5 %all-to-all-start.10 = ((bf16[8,2,32768]{2,1,0:T(2,128)(2,1)}), bf16[8,2,32768]{2,1,0:T(2,128)(2,1)}, u32[]{:S(2)}, u32[]{:S(2)}) async-start(bf16[8,2,32768]{2,1,0:T(2,128)(2,1)} %reshape.532), calls=%async_computation.10 | async-start | bytes 2097152 | tf_op jit(solution)/shard_map/all_to_all | solution.py:168
  293.5 18.4 %copy-start.35 = (f32[32]{0:T(128)S(1)}, f32[32]{0:T(128)}, u32[]{:S(2)}) copy-start(f32[32]{0:T(128)} %param.39) | copy-start | bytes 388
  293.5 18.5 %copy-start.36 = (f32[32]{0:T(128)S(1)}, f32[32]{0:T(128)}, u32[]{:S(2)}) copy-start(f32[32]{0:T(128)} %param.40) | copy-start | bytes 388
  309.7 7.1 copy-start.32
  316.8 8.6 copy-start.17
  317.1 29.2 %all-to-all-start.12 = ((bf16[8,2,32768]{2,1,0:T(2,128)(2,1)}), bf16[8,2,32768]{2,1,0:T(2,128)(2,1)S(1)}, u32[]{:S(2)}, u32[]{:S(2)}) async-start(bf16[8,2,32768]{2,1,0:T(2,128)(2,1)} %reshape.536), calls=%async_computation.12 | async-start | bytes 2097152 | tf_op jit(solution)/shard_map/all_to_all | solution.py:169
  324.6 2.8 copy-start.21
  325.4 52.4 %collective-permute-start.3 = (bf16[1,512,256]{2,1,0:T(8,128)(2,1)S(1)}, bf16[1,512,256]{2,1,0:T(8,128)(2,1)}, u32[]{:S(2)}, u32[]{:S(2)}) collective-permute-start(bf16[1,512,256]{2,1,0:T(8,128)(2,1)S(1)} %bitcast.400), channel_id=1, source_target_pairs={{0,1},{1,0},{2,3},{3,2},{4,5},{5,4},{6,7},{7,6},{8,9},{9,8},{10,11... | collective-permute-start | bytes 786440 | tf_op jit(solution)/shard_map/ppermute | solution.py:17
  326.9 52.1 %collective-permute-start.2 = (bf16[1,512,256]{2,1,0:T(8,128)(2,1)S(1)}, bf16[1,512,256]{2,1,0:T(8,128)(2,1)}, u32[]{:S(2)}, u32[]{:S(2)}) collective-permute-start(bf16[1,512,256]{2,1,0:T(8,128)(2,1)S(1)} %bitcast.403), channel_id=1, source_target_pairs={{0,1},{1,0},{2,3},{3,2},{4,5},{5,4},{6,7},{7,6},{8,9},{9,8},{10,11... | collective-permute-start | bytes 786440 | tf_op jit(solution)/shard_map/ppermute | solution.py:17
  329.4 28.6 %copy-start.19 = (bf16[8,2,8192]{2,1,0:T(2,128)(2,1)S(1)}, bf16[8,2,8192]{2,1,0:T(2,128)(2,1)}, u32[]{:S(2)}) copy-start(bf16[8,2,8192]{2,1,0:T(2,128)(2,1)} %copy-done.18) | copy-start | bytes 786436
  347.3 51.1 %all-to-all-start = ((bf16[8,2,65536]{2,1,0:T(2,128)(2,1)}), bf16[8,2,65536]{2,1,0:T(2,128)(2,1)S(1)}, u32[]{:S(2)}, u32[]{:S(2)}) async-start(bf16[8,2,65536]{2,1,0:T(2,128)(2,1)} %reshape.512), calls=%async_computation | async-start | bytes 4194304 | tf_op jit(solution)/shard_map/all_to_all | solution.py:160
  358.0 54.6 %collective-permute-start.4 = (bf16[1,512,256]{2,1,0:T(8,128)(2,1)}, bf16[1,512,256]{2,1,0:T(8,128)(2,1)}, u32[]{:S(2)}, u32[]{:S(2)}) collective-permute-start(bf16[1,512,256]{2,1,0:T(8,128)(2,1)} %bitcast.54), channel_id=1, source_target_pairs={{0,1},{1,0},{2,3},{3,2},{4,5},{5,4},{6,7},{7,6},{8,9},{9,8},{10,11... | collective-permute-start | bytes 786440 | tf_op jit(solution)/shard_map/ppermute | solution.py:17
  371.3 8.9 collective-permute-start.8
  377.5 5.8 copy-start.12
  377.7 34.1 %collective-permute-start.9 = (bf16[1,512,256]{2,1,0:T(8,128)(2,1)S(1)}, bf16[1,512,256]{2,1,0:T(8,128)(2,1)S(1)}, u32[]{:S(2)}, u32[]{:S(2)}) collective-permute-start(bf16[1,512,256]{2,1,0:T(8,128)(2,1)S(1)} %bitcast.406), channel_id=1, source_target_pairs={{0,1},{1,0},{2,3},{3,2},{4,5},{5,4},{6,7},{7,6},{8,9},{9,8},{10,11... | collective-permute-start | bytes 786440 | tf_op jit(solution)/shard_map/ppermute | solution.py:17
  389.4 13.5 %copy-start.13 = (bf16[1,1024,64]{2,1,0:T(8,128)(2,1)S(1)}, bf16[1,1024,64]{2,1,0:T(8,128)(2,1)}, u32[]{:S(2)}) copy-start(bf16[1,1024,64]{2,1,0:T(8,128)(2,1)} %get-tuple-element.307) | copy-start | bytes 393220
  389.4 13.5 %copy-start.14 = (bf16[1,1024,64]{2,1,0:T(8,128)(2,1)S(1)}, bf16[1,1024,64]{2,1,0:T(8,128)(2,1)}, u32[]{:S(2)}) copy-start(bf16[1,1024,64]{2,1,0:T(8,128)(2,1)} %get-tuple-element.308) | copy-start | bytes 393220
  398.4 11.1 %copy-start.5 = (bf16[8,2,65536]{2,1,0:T(2,128)(2,1)}, bf16[8,2,65536]{2,1,0:T(2,128)(2,1)S(1)}, u32[]{:S(2)}) copy-start(bf16[8,2,65536]{2,1,0:T(2,128)(2,1)S(1)} %all-to-all-done) | copy-start | bytes 6291460
  398.4 62.5 %all-to-all-start.1 = ((bf16[8,2,65536]{2,1,0:T(2,128)(2,1)}), bf16[8,2,65536]{2,1,0:T(2,128)(2,1)}, u32[]{:S(2)}, u32[]{:S(2)}) async-start(bf16[8,2,65536]{2,1,0:T(2,128)(2,1)} %reshape.514), calls=%async_computation.1 | async-start | bytes 4194304 | tf_op jit(solution)/shard_map/all_to_all | solution.py:161
  426.0 9.2 copy-start.4
  435.1 123.9 %collective-permute-start.5 = (f32[4,512]{1,0:T(4,128)S(1)}, f32[4,512]{1,0:T(4,128)S(1)}, u32[]{:S(2)}, u32[]{:S(2)}) collective-permute-start(f32[4,512]{1,0:T(4,128)S(1)} %get-tuple-element.326), channel_id=1, source_target_pairs={{0,1},{1,0},{2,3},{3,2},{4,5},{5,4},{6,7},{7,6},{8,9},{9,8},{10,11... | collective-permute-start | bytes 24584 | tf_op jit(solution)/shard_map/ppermute | solution.py:17
  444.5 114.5 %collective-permute-start.6 = (f32[4,512,64]{1,2,0:T(8,128)}, f32[4,512,64]{1,2,0:T(8,128)S(1)}, u32[]{:S(2)}, u32[]{:S(2)}) collective-permute-start(f32[4,512,64]{1,2,0:T(8,128)} %fusion.35), channel_id=1, source_target_pairs={{0,1},{1,0},{2,3},{3,2},{4,5},{5,4},{6,7},{7,6},{8,9},{9,8},{10,11... | collective-permute-start | bytes 1572872 | tf_op jit(solution)/shard_map/ppermute | solution.py:17
  453.1 105.8 %collective-permute-start.7 = (f32[4,512]{1,0:T(4,128)S(1)}, f32[4,512]{1,0:T(4,128)S(1)}, u32[]{:S(2)}, u32[]{:S(2)}) collective-permute-start(f32[4,512]{1,0:T(4,128)S(1)} %fusion.33), channel_id=1, source_target_pairs={{0,1},{1,0},{2,3},{3,2},{4,5},{5,4},{6,7},{7,6},{8,9},{9,8},{10,11... | collective-permute-start | bytes 24584 | tf_op jit(solution)/shard_map/ppermute | solution.py:17
  460.8 6.6 copy-start.10
  460.8 130.3 %all-to-all-start.2 = ((bf16[8,2,65536]{2,1,0:T(2,128)(2,1)}), bf16[8,2,65536]{2,1,0:T(2,128)(2,1)}, u32[]{:S(2)}, u32[]{:S(2)}) async-start(bf16[8,2,65536]{2,1,0:T(2,128)(2,1)} %reshape.516), calls=%async_computation.2 | async-start | bytes 4194304 | tf_op jit(solution)/shard_map/all_to_all | solution.py:162
  467.5 28.5 %copy-start.30 = (bf16[1,512,4,64]{1,3,2,0:T(8,128)(2,1)S(1)}, bf16[1,512,4,64]{1,3,2,0:T(8,128)(2,1)}, u32[]{:S(2)}) copy-start(bf16[1,512,4,64]{1,3,2,0:T(8,128)(2,1)} %reshape.444) | copy-start | bytes 786436
  495.9 9.5 copy-start.11
  519.0 92.8 %collective-permute-start = (bf16[1,2048,512]{2,1,0:T(8,128)(2,1)S(1)}, bf16[1,2048,512]{2,1,0:T(8,128)(2,1)}, u32[]{:S(2)}, u32[]{:S(2)}) collective-permute-start(bf16[1,2048,512]{2,1,0:T(8,128)(2,1)S(1)} %bitcast.344), channel_id=1, source_target_pairs={{0,1},{1,0},{2,3},{3,2},{4,5},{5,4},{6,7},{7,6},{8,9},{9,8},{10,11... | collective-permute-start | bytes 6291464 | tf_op jit(solution)/shard_map/ppermute | solution.py:17
  591.1 50.5 %all-to-all-start.7 = ((bf16[8,2,8192]{2,1,0:T(2,128)(2,1)}), bf16[8,2,8192]{2,1,0:T(2,128)(2,1)S(1)}, u32[]{:S(2)}, u32[]{:S(2)}) async-start(bf16[8,2,8192]{2,1,0:T(2,128)(2,1)} %reshape.526), calls=%async_computation.7 | async-start | bytes 524288 | tf_op jit(solution)/shard_map/all_to_all | solution.py:283
  611.5 26.9 %collective-permute-start.1 = (bf16[1,2048,512]{2,1,0:T(8,128)(2,1)}, bf16[1,2048,512]{2,1,0:T(8,128)(2,1)S(1)}, u32[]{:S(2)}, u32[]{:S(2)}) collective-permute-start(bf16[1,2048,512]{2,1,0:T(8,128)(2,1)} %bitcast.347), channel_id=1, source_target_pairs={{0,1},{1,0},{2,3},{3,2},{4,5},{5,4},{6,7},{7,6},{8,9},{9,8},{10,11... | collective-permute-start | bytes 6291464 | tf_op jit(solution)/shard_map/ppermute | solution.py:17
  613.5 26.3 %copy-start.2 = (bf16[1,8,256,512]{3,2,1,0:T(8,128)(2,1)S(1)}, bf16[1,8,256,512]{3,2,1,0:T(8,128)(2,1)}, u32[]{:S(2)}) copy-start(bf16[1,8,256,512]{3,2,1,0:T(8,128)(2,1)} %copy.163) | copy-start | bytes 6291460
  638.4 9.1 copy-start.3
  641.7 18.5 %copy-start.22 = (bf16[8,2,8192]{2,1,0:T(2,128)(2,1)}, bf16[8,2,8192]{2,1,0:T(2,128)(2,1)S(1)}, u32[]{:S(2)}) copy-start(bf16[8,2,8192]{2,1,0:T(2,128)(2,1)S(1)} %all-to-all-done.7) | copy-start | bytes 786436
  641.7 18.5 %all-to-all-start.11 = ((bf16[8,2,8192]{2,1,0:T(2,128)(2,1)}), bf16[8,2,8192]{2,1,0:T(2,128)(2,1)S(1)}, u32[]{:S(2)}, u32[]{:S(2)}) async-start(bf16[8,2,8192]{2,1,0:T(2,128)(2,1)} %reshape.534), calls=%async_computation.11 | async-start | bytes 524288 | tf_op jit(solution)/shard_map/all_to_all | solution.py:284
  660.2 6.0 copy-start.24
  660.2 223.9 %all-to-all-start.15 = ((bf16[8,2,32768]{2,1,0:T(2,128)(2,1)}), bf16[8,2,32768]{2,1,0:T(2,128)(2,1)}, u32[]{:S(2)}, u32[]{:S(2)}) async-start(bf16[8,2,32768]{2,1,0:T(2,128)(2,1)} %reshape.542), calls=%async_computation.15 | async-start | bytes 2097152 | tf_op jit(solution)/shard_map/all_to_all | solution.py:285
  666.2 185.7 %copy-start.33 = (f32[4,128]{1,0:T(4,128)S(1)}, f32[4,128]{1,0:T(4,128)}, u32[]{:S(2)}) copy-start(f32[4,128]{1,0:T(4,128)} %dynamic-slice_bitcast_fusion.1) | copy-start | bytes 6148
  666.3 18.1 %copy-start.8 = (bf16[4,4096,128]{2,1,0:T(8,128)(2,1)S(1)}, bf16[4,4096,128]{2,1,0:T(8,128)(2,1)}, u32[]{:S(2)}) copy-start(bf16[4,4096,128]{2,1,0:T(8,128)(2,1)} %get-tuple-element.451) | copy-start | bytes 12582916 | tf_op jit(solution)/shard_map/while
  712.7 18.1 %copy-start.8 = (bf16[4,4096,128]{2,1,0:T(8,128)(2,1)S(1)}, bf16[4,4096,128]{2,1,0:T(8,128)(2,1)}, u32[]{:S(2)}) copy-start(bf16[4,4096,128]{2,1,0:T(8,128)(2,1)} %get-tuple-element.451) | copy-start | bytes 12582916 | tf_op jit(solution)/shard_map/while
  759.1 18.1 %copy-start.8 = (bf16[4,4096,128]{2,1,0:T(8,128)(2,1)S(1)}, bf16[4,4096,128]{2,1,0:T(8,128)(2,1)}, u32[]{:S(2)}) copy-start(bf16[4,4096,128]{2,1,0:T(8,128)(2,1)} %get-tuple-element.451) | copy-start | bytes 12582916 | tf_op jit(solution)/shard_map/while
  805.6 18.1 %copy-start.8 = (bf16[4,4096,128]{2,1,0:T(8,128)(2,1)S(1)}, bf16[4,4096,128]{2,1,0:T(8,128)(2,1)}, u32[]{:S(2)}) copy-start(bf16[4,4096,128]{2,1,0:T(8,128)(2,1)} %get-tuple-element.451) | copy-start | bytes 12582916 | tf_op jit(solution)/shard_map/while
  880.3 9.9 %copy-start.23 = (bf16[8,2,8192]{2,1,0:T(2,128)(2,1)S(1)}, bf16[8,2,8192]{2,1,0:T(2,128)(2,1)}, u32[]{:S(2)}) copy-start(bf16[8,2,8192]{2,1,0:T(2,128)(2,1)} %copy-done.22) | copy-start | bytes 786436
  884.1 7.2 copy-start.25
  884.1 53.9 %all-to-all-start.3 = ((bf16[8,2,65536]{2,1,0:T(2,128)(2,1)}), bf16[8,2,65536]{2,1,0:T(2,128)(2,1)S(1)}, u32[]{:S(2)}, u32[]{:S(2)}) async-start(bf16[8,2,65536]{2,1,0:T(2,128)(2,1)} %reshape.518), calls=%async_computation.3 | async-start | bytes 4194304 | tf_op jit(solution)/shard_map/all_to_all | solution.py:282
  945.2 6.5 copy-start.1
  (3 other events, 3.0 us)
where the time goes:
time: 966 us; the launch traced here: 952 us
  other arithmetic  339 us (35%)
  local copies, waits for them, and re-layouts  251 us (26%)
  matrix products  192 us (20%)
  starting transfers between devices  95.5 us (10%)
  waiting for transfers between devices  58.6 us (6%)
  blocking collectives  12.7 us (1%)
    unnamed x19, other arithmetic  200 us
    unnamed x147, local copies, waits for them, and re-layouts  165 us
    dot_general x11, matrix products, one_block(): jnp.einsum('fqd,fkd->fqk', query_block, keyed, preferred_element_type=jnp...  106 us
    dot_general x11, matrix products, one_block(): jnp.einsum('fqk,fkd->fqd', exps.astype(jnp.bfloat16), valued, preferred_e...  84.6 us
    reduce_sum x11, other arithmetic, one_block(): totals = jnp.sum(exps, axis=2)  81.2 us
    all_to_all x1, waiting for transfers between devices, on_device(): lax.all_to_all(video_self, 'tok', split_axis=1, concat_axis=2, tiled=True)  32.6 us
    concatenate x1, other arithmetic  24.9 us
  transfers between devices with their start and end apart: 26, of which 3 were waited for; matrix products, arithmetic and copies ran while one was open for 79% of the time, Pallas kernels for 0%

commit v1 on v0

v1 whole, which is shorter than its diff:
```python
import math

import jax
import jax.numpy as jnp
from jax import lax
from jax.experimental import pallas as pl
from jax.experimental.pallas import tpu as pltpu
from jax.sharding import PartitionSpec as P


LV = 4096
FRAMES = 16
DHV = 128
DHA = 64
LANES = 128
LOG2E = 1.4426950408889634
VIDEO_PARTS = 2


BF16 = jnp.bfloat16
F32 = jnp.float32


def swap(value, axis, mask):
    count = lax.axis_size(axis)
    return lax.ppermute(value, axis, [(j, j ^ mask) for j in range(count)])


def cost(flops, exps, moved):
    return pl.CostEstimate(flops=int(flops), transcendentals=int(exps), bytes_accessed=int(moved))


def nt(a, b):
    return lax.dot_general(a, b, (((1,), (1,)), ((), ())), preferred_element_type=F32)


def pack(arrays, tok_count, parts):
    rows, columns = arrays[0].shape
    wide = columns // tok_count
    part = wide // parts
    n = len(arrays)
    if part % LANES:
        me = lax.axis_index("tok")
        return [
            jnp.stack(
                [lax.dynamic_slice_in_dim(a, (me ^ m) * wide + p * part, part, 1) for a in arrays]
            )
            for p in range(parts)
            for m in range(tok_count)
        ]
    high = min(32, rows)

    def body(*refs):
        ins, outs = refs[:n], refs[n:]
        me = lax.axis_index("tok")
        for p in range(parts):
            for m in range(tok_count):
                start = pl.multiple_of((me ^ m) * wide + p * part, part)
                for a in range(n):
                    outs[p * tok_count + m][a] = ins[a][:, pl.ds(start, part)]

    count = tok_count * parts
    return pl.pallas_call(
        body,
        grid=(rows // high,),
        out_shape=[jax.ShapeDtypeStruct((n, rows, part), BF16)] * count,
        in_specs=[pl.BlockSpec((high, columns), lambda i: (i, 0))] * n,
        out_specs=[pl.BlockSpec((n, high, part), lambda i: (0, i, 0))] * count,
        cost_estimate=cost(0, 0, 4 * n * rows * columns),
        name="pack",
    )(*arrays)


def assemble(blocks):
    count = len(blocks)
    _, rows, wide = blocks[0].shape
    high = min(64, rows)

    def body(*refs):
        for m in range(count):
            for a in range(2):
                refs[count][a, m] = refs[m][a]

    joined = pl.pallas_call(
        body,
        grid=(rows // high,),
        out_shape=jax.ShapeDtypeStruct((2, count, rows, wide), BF16),
        in_specs=[pl.BlockSpec((2, high, wide), lambda i: (0, i, 0))] * count,
        out_specs=pl.BlockSpec((2, count, high, wide), lambda i: (0, 0, i, 0)),
        cost_estimate=cost(0, 0, 8 * count * rows * wide),
        name="assemble",
    )(*blocks)
    return joined.reshape(2, count * rows, wide)


def unpack(parts, tok_count):
    count = len(parts)
    rows, part = parts[0][0].shape
    wide = part * count
    if part % LANES:
        me = lax.axis_index("tok")
        out = jnp.zeros((rows, wide * tok_count), BF16)
        for p in range(count):
            for m in range(tok_count):
                at = (me ^ m) * wide + p * part
                out = lax.dynamic_update_slice_in_dim(out, parts[p][m], at, 1)
        return out
    high = min(32, rows)

    def body(*refs):
        me = lax.axis_index("tok")
        out = refs[-1]
        for p in range(count):
            for m in range(tok_count):
                start = pl.multiple_of((me ^ m) * wide + p * part, part)
                out[:, pl.ds(start, part)] = refs[p * tok_count + m][...]

    return pl.pallas_call(
        body,
        grid=(rows // high,),
        out_shape=jax.ShapeDtypeStruct((rows, wide * tok_count), BF16),
        in_specs=[pl.BlockSpec((high, part), lambda i: (i, 0))] * (count * tok_count),
        out_specs=pl.BlockSpec((high, wide * tok_count), lambda i: (i, 0)),
        cost_estimate=cost(0, 0, 4 * rows * wide * tok_count),
        name="unpack",
    )(*[block for blocks in parts for block in blocks])


def stack_rows(first, second):
    rows, wide = first.shape

    def body(a_ref, b_ref, out_ref):
        out_ref[:rows] = a_ref[...]
        out_ref[rows:] = b_ref[...]

    return pl.pallas_call(
        body,
        out_shape=jax.ShapeDtypeStruct((2 * rows, wide), BF16),
        cost_estimate=cost(0, 0, 8 * rows * wide),
        name="stack_rows",
    )(first, second)


def lane_of(shape):
    return lax.broadcasted_iota(jnp.int32, shape, len(shape) - 1)


def one_head(queries, parts, scale):
    factor = scale * LOG2E
    top = total = summed = None
    for keys, values in parts:
        scores = nt(queries, keys)
        peak = jnp.max(scores, axis=1, keepdims=True)
        new_top = peak if top is None else jnp.maximum(top, peak)
        exps = jnp.exp2((scores - new_top) * factor)
        sums = jnp.sum(exps, axis=1, keepdims=True)
        part = jnp.dot(exps.astype(BF16), values, preferred_element_type=F32)
        if top is None:
            total, summed = sums, part
        else:
            fade = jnp.exp2((top - new_top) * factor)
            total = total * fade + sums
            summed = summed * fade + part
        top = new_top
    return total, summed


def pick(lanes, width, keys, index):
    if lanes == width:
        return keys
    here = (lane_of(keys.shape) // width) == index
    return jnp.where(here, keys, jnp.zeros_like(keys))


def self_attention(blocks, own, other, gate, width):
    tok_count = len(blocks)
    _, rows, columns = blocks[0].shape
    counted = rows * tok_count
    keyed = own.shape[1]
    lanes = min(LANES, columns)
    heads = lanes // width
    block = min(512, counted)
    chunk = min(1024, keyed)
    scale = 1.0 / math.sqrt(width)

    def body(*refs):
        q_refs, (own_ref, other_ref, gate_ref) = refs[:tok_count], refs[tok_count : tok_count + 3]
        outs, (q_held, held) = refs[tok_count + 3 : -2], refs[-2:]
        gates = gate_ref[...]
        for m in range(tok_count):
            q_held[m * rows : (m + 1) * rows, :] = q_refs[m][0]

        def step(b, carry):
            at = pl.multiple_of(b * block, block)
            q = q_held[pl.ds(at, block), :]
            result = None
            for head in range(heads):
                parts = []
                for ref in (own_ref, other_ref):
                    for c in range(keyed // chunk):
                        here = pl.ds(c * chunk, chunk)
                        keys = pick(lanes, width, ref[0, here, :], head)
                        parts.append((keys, ref[1, here, :]))
                total, summed = one_head(q, parts, scale)
                done = summed / total
                if result is None:
                    result = done
                else:
                    result = jnp.where(lane_of(done.shape) // width == head, done, result)
            held[pl.ds(at, block), :] = (result * gates).astype(BF16)
            return carry

        lax.fori_loop(0, counted // block, step, 0)
        for m in range(tok_count):
            outs[m][...] = held[m * rows : (m + 1) * rows, :]

    steps = columns // lanes
    scores = counted * keyed * 2 * (columns // width)
    return pl.pallas_call(
        body,
        grid=(steps,),
        out_shape=[jax.ShapeDtypeStruct((rows, columns), BF16)] * tok_count,
        in_specs=[pl.BlockSpec((1, rows, lanes), lambda i: (2, 0, i))] * tok_count
        + [
            pl.BlockSpec((2, keyed, lanes), lambda i: (0, 0, i)),
            pl.BlockSpec((2, keyed, lanes), lambda i: (0, 0, i)),
            pl.BlockSpec((1, lanes), lambda i: (0, i)),
        ],
        out_specs=[pl.BlockSpec((rows, lanes), lambda i: (0, i))] * tok_count,
        scratch_shapes=[pltpu.VMEM((counted, lanes), BF16)] * 2,
        cost_estimate=cost(scores * 4 * LANES, scores, 2 * columns * (2 * counted + 4 * keyed)),
        name="self_attention",
    )(*blocks, own, other, gate)


def video_cross_local(queries, pieces, slopes, gate, place, span):
    counted, columns = queries.shape
    keyed = pieces[0].shape[0]
    n = len(pieces)
    steps = columns // LANES
    heads = LANES // DHA
    factor = LOG2E / math.sqrt(DHA)

    def body(slope_ref, place_ref, q_ref, *refs):
        gate_ref, out_ref = refs[3 * n :]
        i = pl.program_id(0)
        q = q_ref[...]
        at = place_ref[0]
        if span % counted == 0:
            mine = (at // span).astype(F32)
        else:
            col = lax.broadcasted_iota(jnp.int32, (1, counted), 1)
            mine = ((at + col) // span).astype(F32)
        gaps, turned = [], []
        for p in range(n):
            frame = refs[3 * p + 2][...].astype(F32)
            if counted > LANES:
                frame = jnp.concatenate([frame] * (counted // LANES), axis=1)
            gaps.append(jnp.abs(frame[:, :counted] - mine))
            turned.append(jnp.transpose(refs[3 * p + 1][...]))
        results = []
        for head in range(heads):
            slope = slope_ref[i * heads + head] * LOG2E
            scores = [
                nt(pick(LANES, DHA, refs[3 * p][...], head), q) * factor - gaps[p] * slope
                for p in range(n)
            ]
            top = jnp.max(scores[0], axis=0, keepdims=True)
            for one in scores[1:]:
                top = jnp.maximum(top, jnp.max(one, axis=0, keepdims=True))
            total = summed = None
            for p in range(n):
                exps = jnp.exp2(scores[p] - top)
                sums = jnp.sum(exps, axis=0, keepdims=True)
                part = jnp.dot(
                    turned[p][head * DHA : (head + 1) * DHA],
                    exps.astype(BF16),
                    preferred_element_type=F32,
                )
                total = sums if total is None else total + sums
                summed = part if summed is None else summed + part
            results.append(summed / total)
        result = jnp.transpose(jnp.concatenate(results, axis=0))
        out_ref[...] = (result * gate_ref[...]).astype(BF16)

    piece = [
        pl.BlockSpec((keyed, LANES), lambda i: (0, steps + i)),
        pl.BlockSpec((keyed, LANES), lambda i: (0, 2 * steps + i)),
        pl.BlockSpec((keyed, LANES), lambda i: (0, 3 * steps)),
    ]
    scores = counted * keyed * n * steps * heads
    return pl.pallas_call(
        body,
        grid=(steps,),
        out_shape=jax.ShapeDtypeStruct((counted, columns), BF16),
        in_specs=[
            pl.BlockSpec(memory_space=pltpu.SMEM),
            pl.BlockSpec(memory_space=pltpu.SMEM),
            pl.BlockSpec((counted, LANES), lambda i: (0, i)),
        ]
        + piece * n
        + [pl.BlockSpec((1, LANES), lambda i: (0, i))],
        out_specs=pl.BlockSpec((counted, LANES), lambda i: (0, i)),
        cost_estimate=cost(scores * 4 * LANES, scores, 4 * columns * (counted + n * keyed)),
        name="video_cross",
    )(slopes, place, queries, *[a for piece in pieces for a in (piece, piece, piece)], gate)


def audio_cross_local(pieces, keys, values, slopes, place, span):
    counted = pieces[0].shape[0]
    n = len(pieces)
    keyed, columns = keys.shape
    steps = columns // LANES
    heads = LANES // DHA
    count = steps * heads
    factor = LOG2E / math.sqrt(DHA)

    def body(slope_ref, place_ref, k_ref, v_ref, *refs):
        q_refs, f_refs, o_refs = refs[:n], refs[n : 2 * n], refs[2 * n : 3 * n]
        stats, times = refs[3 * n :]
        i = pl.program_id(0)
        at = place_ref[0]

        @pl.when(i == 0)
        def _():
            stats[...] = jnp.zeros_like(stats)
            for p in range(n):
                times[p] = jnp.transpose(f_refs[p][...].astype(F32))[0:8, :]

        @pl.when(i < steps)
        def _():
            keys_here = k_ref[...]
            turned = jnp.transpose(v_ref[...])
            for p in range(n):
                q = q_refs[p][...]
                mine = times[p, 0:1, :]
                if span % keyed == 0:
                    gap = jnp.abs(mine - (at // span).astype(F32))
                else:
                    row = lax.broadcasted_iota(jnp.int32, (keyed, 1), 0)
                    gap = jnp.abs(mine - ((at + row) // span).astype(F32))
                results = []
                for head in range(heads):
                    index = i * heads + head
                    slope = slope_ref[index] * LOG2E
                    scores = nt(pick(LANES, DHA, keys_here, head), q)
                    if span % keyed == 0:
                        top = jnp.max(scores, axis=0, keepdims=True)
                        exps = jnp.exp2((scores - top) * factor)
                        top = top * factor - gap * slope
                    else:
                        scores = scores * factor - gap * slope
                        top = jnp.max(scores, axis=0, keepdims=True)
                        exps = jnp.exp2(scores - top)
                    total = jnp.sum(exps, axis=0, keepdims=True)
                    part = jnp.dot(
                        turned[head * DHA : (head + 1) * DHA],
                        exps.astype(BF16),
                        preferred_element_type=F32,
                    )
                    results.append(part / total)
                    stats[p, pl.ds(index, 1), :] = top + jnp.log2(total)
                result = jnp.concatenate(results, axis=0)
                o_refs[p][...] = jnp.transpose(result).astype(BF16)

        @pl.when(i == steps)
        def _():
            for p in range(n):
                o_refs[p][...] = spread_stats(jnp.transpose(stats[p]), count)

    def at_step(i):
        return jnp.minimum(i, steps - 1)

    scores = counted * keyed * n * count
    return pl.pallas_call(
        body,
        grid=(steps + 1,),
        out_shape=[jax.ShapeDtypeStruct((counted, columns + LANES), BF16)] * n,
        in_specs=[
            pl.BlockSpec(memory_space=pltpu.SMEM),
            pl.BlockSpec(memory_space=pltpu.SMEM),
        ]
        + [pl.BlockSpec((keyed, LANES), lambda i: (0, at_step(i)))] * 2
        + [pl.BlockSpec((counted, LANES), lambda i: (0, at_step(i)))] * n
        + [pl.BlockSpec((counted, LANES), lambda i: (0, 3 * steps))] * n,
        out_specs=[pl.BlockSpec((counted, LANES), lambda i: (0, i))] * n,
        scratch_shapes=[
            pltpu.VMEM((n, LANES, counted), F32),
            pltpu.VMEM((n, 8, counted), F32),
        ],
        cost_estimate=cost(scores * 4 * LANES, scores, 4 * columns * (n * counted + keyed)),
        name="audio_cross",
    )(slopes, place, keys, values, *pieces, *pieces)


def spread_stats(stats, count):
    lane = lane_of(stats.shape)
    first = stats.astype(BF16).astype(F32)
    rest = stats - first
    second = rest.astype(BF16).astype(F32)
    third = rest - second
    second = pltpu.roll(second, count, 1)
    third = pltpu.roll(third, 2 * count, 1)
    packed = jnp.where(lane < count, first, jnp.where(lane < 2 * count, second, third))
    return jnp.where(lane < 3 * count, packed, 0.0).astype(BF16)


def read_stats(packed, count):
    terms = packed.astype(F32)
    second = pltpu.roll(terms, LANES - count, 1)
    third = pltpu.roll(terms, LANES - 2 * count, 1)
    return terms + second + third


def merge(mine, theirs, form, gate=None):
    rows, wide = mine.shape
    columns = wide - LANES
    count = columns // DHA
    heads = LANES // DHA
    half = rows // 2

    def body(a_ref, b_ref, *refs):
        a_stat = read_stats(a_ref[:, columns:], count)
        b_stat = read_stats(b_ref[:, columns:], count)
        top = jnp.maximum(a_stat, b_stat)
        a_part = jnp.exp2(a_stat - top)
        b_part = jnp.exp2(b_stat - top)
        total = a_part + b_part
        a_share = a_part / total
        b_share = b_part / total
        lane = lane_of((rows, LANES)) // DHA

        def put(here, value):
            if form == "halves":
                refs[0][:, here] = value[:half]
                refs[1][:, here] = value[half:]
            else:
                refs[-1][:, here] = value

        for j in range(columns // LANES):
            here = slice(j * LANES, (j + 1) * LANES)
            a_weight = a_share[:, j * heads : j * heads + 1]
            b_weight = b_share[:, j * heads : j * heads + 1]
            for h in range(1, heads):
                at = j * heads + h
                a_weight = jnp.where(lane == h, a_share[:, at : at + 1], a_weight)
                b_weight = jnp.where(lane == h, b_share[:, at : at + 1], b_weight)
            joined = a_ref[:, here].astype(F32) * a_weight + b_ref[:, here].astype(F32) * b_weight
            if form == "last":
                joined = joined * refs[0][:, here]
            put(here, joined.astype(BF16))
        if form != "last":
            put(slice(columns, wide), spread_stats(top + jnp.log2(total), count))

    if form == "halves":
        shapes = [jax.ShapeDtypeStruct((half, wide), BF16)] * 2
    elif form == "last":
        shapes = jax.ShapeDtypeStruct((rows, columns), BF16)
    else:
        shapes = jax.ShapeDtypeStruct((rows, wide), BF16)
    extra = () if gate is None else (gate,)
    return pl.pallas_call(
        body,
        out_shape=shapes,
        cost_estimate=cost(0, rows * wide, 6 * rows * wide),
        name="merge",
    )(mine, theirs, *extra)


def on_device(
    video_query,
    video_key,
    video_value,
    audio_query,
    audio_key,
    audio_value,
    cross_audio_query,
    cross_video_key,
    cross_video_value,
    cross_video_query,
    cross_audio_key,
    cross_audio_value,
    audio_frames,
    into_audio_slope,
    into_video_slope,
    timestep,
    video_gate,
    audio_gate,
    into_audio_gate,
    into_video_gate,
):
    tok_count = lax.axis_size("tok")
    head_count = lax.axis_size("head")
    tok = lax.axis_index("tok")
    samples, video_rows, video_columns = video_query.shape
    audio_rows, _ = audio_query.shape[1:]
    patches = LV // FRAMES
    place = ((tok * head_count + lax.axis_index("head")) * video_rows).reshape(1)
    masks = [1 << b for b in reversed(range(tok_count.bit_length() - 1))]

    def gate_row(table, sample):
        return lax.dynamic_slice_in_dim(table, timestep[sample], 1, 0).astype(F32)

    def gate_part(row, part, parts):
        wide = row.shape[1] // tok_count
        piece = wide // parts
        return lax.dynamic_slice_in_dim(row, tok * wide + part * piece, piece, 1)

    def exchange(blocks):
        return [blocks[0]] + [swap(blocks[m], "tok", m) for m in range(1, tok_count)]

    def self_part(blocks, gate, width):
        blocks = exchange(blocks)
        own = assemble(blocks)
        other = swap(own, "head", 1)
        outs = self_attention(blocks, own, other, gate, width)
        return exchange(outs)

    results = []
    for s in range(samples):
        frames = jnp.broadcast_to(
            audio_frames[s][:, None].astype(F32), (audio_rows, LANES)
        ).astype(BF16)
        own = jnp.concatenate(
            (cross_audio_query[s], cross_audio_key[s], cross_audio_value[s], frames), axis=1
        )
        for step, mask in enumerate(masks):
            received = swap(own, "tok", mask)
            if step < len(masks) - 1:
                own = stack_rows(own, received)
        pieces = [own, received, swap(own, "head", 1), swap(received, "head", 1)]
        partial = audio_cross_local(
            pieces, cross_video_key[s], cross_video_value[s], into_audio_slope, place, patches
        )
        got = [swap(partial[2], "head", 1), swap(partial[3], "head", 1)]
        mine = merge(partial[0], got[0], "whole")
        send = merge(partial[1], got[1], "whole")
        for step, mask in enumerate(reversed(masks)):
            received = swap(send, "tok", mask)
            if step < len(masks) - 1:
                mine, send = merge(mine, received, "halves")
            else:
                audio_cross = merge(mine, received, "last", gate_row(into_audio_gate, s))
        blocks = pack((audio_key[s], audio_value[s], audio_query[s]), tok_count, 1)
        gate = gate_row(audio_gate, s)
        outs = self_part(blocks, gate_part(gate, 0, 1), DHA)
        audio_self = unpack([outs], tok_count)
        wide = video_columns // tok_count
        parts = VIDEO_PARTS if wide % (VIDEO_PARTS * LANES) == 0 else 1
        blocks = pack((video_key[s], video_value[s], video_query[s]), tok_count, parts)
        gate = gate_row(video_gate, s)
        outs = []
        for p in range(parts):
            mine = blocks[p * tok_count : (p + 1) * tok_count]
            outs.append(self_part(mine, gate_part(gate, p, parts), DHV))
        video_self = unpack(outs, tok_count)
        video_cross = video_cross_local(
            cross_video_query[s],
            pieces,
            into_video_slope,
            gate_row(into_video_gate, s),
            place,
            patches,
        )
        results.append((video_self, audio_self, audio_cross, video_cross))
    return tuple(jnp.stack(parts) for parts in zip(*results))


def solution(mesh):
    rows = P("groups", ("tok", "head"), None)
    placed = (rows,) * 12 + (
        P("groups", ("tok", "head")),
        P(),
        P(),
        P("groups"),
        P(),
        P(),
        P(),
        P(),
    )

    return jax.shard_map(
        on_device, mesh=mesh, in_specs=placed, out_specs=(rows,) * 4, check_vma=False
    )
```

time: 966 us -> 560 us (0.58); the launches traced: 952 us -> 558 us
  other arithmetic: 339 us -> 6.7 us
  local copies, waits for them, and re-layouts: 251 us -> 7.99 us
  waiting for transfers between devices: 58.6 us -> 257 us
  matrix products: 192 us -> 0 us
  Pallas kernels: 0 us -> 182 us
  blocking collectives: 12.7 us -> 0 us
    ppermute x10 -> x55, waiting for transfers between devices: 0.03 us -> 257 us  [swap(): return lax.ppermute(value, axis, [(j, j ^ mask) for j in range(count)])]
    unnamed x19 -> x0, other arithmetic: 200 us -> none
    dot_general x26 -> x0, matrix products: 192 us -> none  [the longest x11 106 us: one_block(): jnp.einsum('fqd,fkd->fqk', query_block, keyed, preferred_element_type=jnp...]
    pallas_call x0 -> x19, Pallas kernels: none -> 182 us  [the longest x3 57.9 us: self_attention(): pl.pallas_call(body, grid=(steps,), out_shape=[jax.ShapeDtypeStruct((rows...]
    unnamed x147 -> x98, local copies, waits for them, and re-layouts: 165 us -> 7.35 us
    ppermute x10 -> x55, starting transfers between devices: 2.4 us -> 103 us  [swap(): return lax.ppermute(value, axis, [(j, j ^ mask) for j in range(count)])]
    all_to_all x16 -> x0, starting transfers between devices: 93.1 us -> none  [the longest x1 7.31 us: on_device(): lax.all_to_all(audio_value, 'tok', split_axis=2, concat_axis=1, tiled=True)]
    reduce_sum x11 -> x0, other arithmetic: 81.2 us -> none  [one_block(): totals = jnp.sum(exps, axis=2)]
  transfers between devices with their start and end apart: 26 -> 55, of which waited for: 3 -> 15; matrix products, arithmetic and copies ran while one was open for 79% -> 1% of each run, Pallas kernels for 0% -> 30%
where the time goes in v1:
time: 560 us; the launch traced here: 558 us
  waiting for transfers between devices  257 us (46%)
  Pallas kernels  182 us (32%)
  starting transfers between devices  103 us (18%)
  local copies, waits for them, and re-layouts  7.99 us (1%)
  other arithmetic  6.7 us (1%)
    ppermute x55, waiting for transfers between devices, swap(): return lax.ppermute(value, axis, [(j, j ^ mask) for j in range(count)])  257 us
    ppermute x55, starting transfers between devices, swap(): return lax.ppermute(value, axis, [(j, j ^ mask) for j in range(count)])  103 us
    pallas_call x3, Pallas kernels, self_attention(): pl.pallas_call(body, grid=(steps,), out_shape=[jax.ShapeDtypeStruct((rows...  57.9 us
    pallas_call x1, Pallas kernels, audio_cross_local(): pl.pallas_call(body, grid=(steps + 1,), out_shape=[jax.ShapeDtypeStruct((...  44.6 us
    pallas_call x1, Pallas kernels, video_cross_local(): pl.pallas_call(body, grid=(steps,), out_shape=jax.ShapeDtypeStruct((count...  24.6 us
    pallas_call x5, Pallas kernels, merge(): pl.pallas_call(body, out_shape=shapes, cost_estimate=cost(0, rows * wide,...  21.5 us
  transfers between devices with their start and end apart: 55, of which 15 were waited for; matrix products, arithmetic and copies ran while one was open for 1% of the time, Pallas kernels for 30%

profile of v1, /device:TPU:0, one launch (start us, length us, event | category | flops | bytes accessed | tf_op | source)
XLA Modules:
  0.0 558.1 jit_solution(17128166331084413562)
XLA Ops:
  2.5 4.1 collective-permute-start.45
  6.7 35.1 %collective-permute-done.45.b_ref = bf16[64,6272]{1,0:T(8,128)(2,1)S(1)} collective-permute-done((bf16[64,6272]{1,0:T(8,128)(2,1)S(1)}, bf16[64,6272]{1,0:T(8,128)(2,1)S(1)}, u32[]{:S(2)}, u32[]{:S(2)}) %collective-permute-start.45) | collective-permute-done | bytes 802848 | tf_op jit(solution)/shard_map/ppermute | solution.py:26
  42.7 2.6 stack_rows.2.a_ref
  46.0 35.8 %collective-permute-done.46.b_ref = bf16[128,6272]{1,0:T(8,128)(2,1)S(1)} collective-permute-done((bf16[128,6272]{1,0:T(8,128)(2,1)}, bf16[128,6272]{1,0:T(8,128)(2,1)S(1)}, u32[]{:S(2)}, u32[]{:S(2)}) %collective-permute-start.46) | collective-permute-done | bytes 1605664 | tf_op jit(solution)/shard_map/ppermute | solution.py:26
  83.0 3.8 stack_rows.3.refs_0_.refs_4_.refs_1_.refs_2_
  86.8 1.3 collective-permute-start.47
  88.1 68.7 %collective-permute-done.47.refs_1_.refs_5_.refs_3_.refs_4_ = bf16[256,6272]{1,0:T(8,128)(2,1)S(1)} collective-permute-done((bf16[256,6272]{1,0:T(8,128)(2,1)}, bf16[256,6272]{1,0:T(8,128)(2,1)S(1)}, u32[]{:S(2)}, u32[]{:S(2)}) %collective-permute-start.47) | collective-permute-done | bytes 3211296 | tf_op jit(solution)/shard_map/ppermute | solution.py:26
  156.8 8.1 %pack.2 = (bf16[3,256,256]{2,1,0:T(8,128)(2,1)}, bf16[3,256,256]{2,1,0:T(8,128)(2,1)}, bf16[3,256,256]{2,1,0:T(8,128)(2,1)}, bf16[3,256,256]{2,1,0:T(8,128)(2,1)...) custom-call(bf16[256,4096]{1,0:T(8,128)(2,1)} %bitcast.26, ...), custom_call_target="tpu_custom_call" | custom-call | bytes 12582912 | tf_op jit(solution)/shard_map/pack/pallas_call | solution.py:63
  164.9 1.4 collective-permute-start
  166.4 2.0 pack.3
  169.1 2.2 collective-permute-start.31
  171.3 7.2 %collective-permute-done.30.refs_1_ = bf16[3,64,256]{2,1,0:T(8,128)(2,1)S(1)} collective-permute-done((bf16[3,64,256]{2,1,0:T(8,128)(2,1)}, bf16[3,64,256]{2,1,0:T(8,128)(2,1)S(1)}, u32[]{:S(2)}, u32[]{:S(2)}) %collective-permute-start.30) | collective-permute-done | bytes 98336 | tf_op jit(solution)/shard_map/ppermute | solution.py:26
  178.5 3.2 collective-permute-start.32
  181.7 3.4 collective-permute-start.33
  185.1 1.4 collective-permute-start.1
  186.5 2.1 collective-permute-done.33.refs_4_
  188.6 1.4 collective-permute-start.2
  190.1 2.0 collective-permute-start.3
  192.0 13.8 %collective-permute-done.1.refs_2_ = bf16[3,256,256]{2,1,0:T(8,128)(2,1)} collective-permute-done((bf16[3,256,256]{2,1,0:T(8,128)(2,1)}, bf16[3,256,256]{2,1,0:T(8,128)(2,1)}, u32[]{:S(2)}, u32[]{:S(2)}) %collective-permute-start.1) | collective-permute-done | bytes 393248 | tf_op jit(solution)/shard_map/ppermute | solution.py:26
  205.8 3.7 collective-permute-start.4
  209.6 4.5 collective-permute-done.2.refs_3_
  214.0 2.7 collective-permute-start.5
  216.8 2.1 collective-permute-start.6
  218.9 30.1 %collective-permute-done.4.refs_5_ = bf16[3,256,256]{2,1,0:T(8,128)(2,1)} collective-permute-done((bf16[3,256,256]{2,1,0:T(8,128)(2,1)}, bf16[3,256,256]{2,1,0:T(8,128)(2,1)}, u32[]{:S(2)}, u32[]{:S(2)}) %collective-permute-start.4) | collective-permute-done | bytes 393248 | tf_op jit(solution)/shard_map/ppermute | solution.py:26
  249.0 1.5 collective-permute-start.35
  250.5 2.9 collective-permute-start.36
  253.3 3.8 assemble.3
  257.1 17.1 %collective-permute-done.34.refs_5_ = bf16[3,64,256]{2,1,0:T(8,128)(2,1)} collective-permute-done((bf16[3,64,256]{2,1,0:T(8,128)(2,1)}, bf16[3,64,256]{2,1,0:T(8,128)(2,1)}, u32[]{:S(2)}, u32[]{:S(2)}) %collective-permute-start.34) | collective-permute-done | bytes 98336 | tf_op jit(solution)/shard_map/ppermute | solution.py:26
  275.4 3.4 collective-permute-start.16
  279.3 2.8 collective-permute-start.18
  282.2 44.6 %audio_cross.1 = (bf16[256,2176]{1,0:T(8,128)(2,1)}, bf16[256,2176]{1,0:T(8,128)(2,1)}, bf16[256,2176]{1,0:T(8,128)(2,1)}, bf16[256,2176]{1,0:T(8,128)(2,1)}) custom-call(f32[32]{0:T(128)} %slope_ref.2, s32[1]{0:T(128)} %bitcast.12.place_ref, bf16[256,2048]{1,0:T(8,128)(2,1)} %bitcast.34, bf16[256,2048]{1,0:T(8,128)(2,1)} %bitcast.35, ...), custom_call_target="tpu_custom_call" | custom-call | flops 4294967296 | bytes 10485760 | tf_op jit(solution)/shard_map/audio_cross/pallas_call | solution.py:375
  327.4 2.3 collective-permute-start.20
  329.7 2.0 collective-permute-start.21
  331.7 1.9 assemble.5
  333.6 31.4 %collective-permute-done.19.refs_5_ = bf16[3,256,256]{2,1,0:T(8,128)(2,1)S(1)} collective-permute-done((bf16[3,256,256]{2,1,0:T(8,128)(2,1)S(1)}, bf16[3,256,256]{2,1,0:T(8,128)(2,1)S(1)}, u32[]{:S(2)}, u32[]{:S(2)}) %collective-permute-start.19) | collective-permute-done | bytes 393248 | tf_op jit(solution)/shard_map/ppermute | solution.py:26
  366.1 3.9 assemble.4
  373.1 5.1 self_attention.5
  379.2 16.7 %collective-permute-start.39 = (bf16[64,256]{1,0:T(8,128)(2,1)}, bf16[64,256]{1,0:T(8,128)(2,1)S(1)}, u32[]{:S(2)}, u32[]{:S(2)}) collective-permute-start(bf16[64,256]{1,0:T(8,128)(2,1)} %get-tuple-element.102), channel_id=1, source_target_pairs={{0,4},{2,6},{4,0},{6,2},{8,12},{10,14},{12,8},{14,10},{1,5},{3,7},... | collective-permute-start | bytes 98312 | tf_op jit(solution)/shard_map/ppermute | solution.py:26
  397.1 5.2 merge.6
  405.3 4.0 collective-permute-done.40.refs_3_
  409.3 3.3 collective-permute-start.42
  412.6 26.5 %self_attention.3 = (bf16[256,256]{1,0:T(8,128)(2,1)}, bf16[256,256]{1,0:T(8,128)(2,1)}, bf16[256,256]{1,0:T(8,128)(2,1)}, bf16[256,256]{1,0:T(8,128)(2,1)}, bf1...) custom-call(bf16[3,256,256]{2,1,0:T(8,128)(2,1)} %get-tuple-element.60.re, ...), custom_call_target="tpu_custom_call" | custom-call | flops 8589934592 | bytes 6291456 | tf_op jit(solution)/shard_map/self_attention/pallas_call | solution.py:219
  440.3 1.6 collective-permute-start.43
  441.9 2.7 collective-permute-start.44
  444.6 5.1 merge.5.a_ref
  449.8 5.2 merge.7
  455.7 1.9 collective-permute-start.11
  457.7 1.4 collective-permute-start.12
  459.1 1.6 collective-permute-start.13
  461.6 26.3 %self_attention.4 = (bf16[256,256]{1,0:T(8,128)(2,1)}, bf16[256,256]{1,0:T(8,128)(2,1)}, bf16[256,256]{1,0:T(8,128)(2,1)}, bf16[256,256]{1,0:T(8,128)(2,1)}, bf1...) custom-call(bf16[3,256,256]{2,1,0:T(8,128)(2,1)} %get-tuple-element.76.re, ...), custom_call_target="tpu_custom_call" | custom-call | flops 8589934592 | bytes 6291456 | tf_op jit(solution)/shard_map/self_attention/pallas_call | solution.py:219
  488.0 2.9 collective-permute-start.14
  492.1 2.4 collective-permute-start.25
  494.4 1.4 dynamic-slice_convert_fusion.2.refs_0_
  496.8 4.6 collective-permute-start.26
  502.3 1.7 collective-permute-done.25.refs_11_
  504.0 4.3 collective-permute-start.29
  508.3 1.4 dynamic-slice_convert_fusion.1.refs_12_
  509.7 1.6 unpack.3
  512.3 3.2 collective-permute-done.27.refs_13_
  516.2 5.4 unpack.2
  522.5 3.4 merge.8
  525.9 4.2 collective-permute-start.54
  530.1 24.6 %video_cross.1 = bf16[256,2048]{1,0:T(8,128)(2,1)} custom-call(f32[32]{0:T(128)} %slope_ref.3, s32[1]{0:T(128)} %bitcast.12.place_ref, bf16[256,2048]{1,0:T(8,128)(2,1)} %bitcast.36, bf16[256,6272]{1,0:T(8,128)(2,1)} %stack_rows.3.refs_0_.refs_4_.refs_1_.refs_2_, bf16[256,6272]{1,0:T(8,128)(2,1)} %stack_rows.3.refs_0_.refs_4_.refs_1_.refs_2_, ...), custom_call_target="tpu_custom_call" | custom-call | flops 4294967296 | bytes 10485760 | tf_op jit(solution)/shard_map/video_cross/pallas_call | solution.py:292
  555.5 2.6 merge.9
  (171 shorter events, 25.7 us)
Async XLA Ops:
  2.5 39.2 %copy-start.1 = (bf16[64,6272]{1,0:T(8,128)(2,1)}, bf16[64,6272]{1,0:T(8,128)(2,1)S(1)}, u32[]{:S(2)}) copy-start(bf16[64,6272]{1,0:T(8,128)(2,1)S(1)} %pad_maximum_fusion.a_ref) | copy-start | bytes 2408452
  2.5 39.2 %collective-permute-start.45 = (bf16[64,6272]{1,0:T(8,128)(2,1)S(1)}, bf16[64,6272]{1,0:T(8,128)(2,1)S(1)}, u32[]{:S(2)}, u32[]{:S(2)}) collective-permute-start(bf16[64,6272]{1,0:T(8,128)(2,1)S(1)} %pad_maximum_fusion.a_ref), channel_id=1, source_target_pairs={{0,8},{2,10},{4,12},{6,14},{8,0},{10,2},{12,4},{14,6},{1,9},{3,11}... | collective-permute-start | bytes 2408456 | tf_op jit(solution)/shard_map/ppermute | solution.py:26
  45.3 36.5 %collective-permute-start.46 = (bf16[128,6272]{1,0:T(8,128)(2,1)}, bf16[128,6272]{1,0:T(8,128)(2,1)S(1)}, u32[]{:S(2)}, u32[]{:S(2)}) collective-permute-start(bf16[128,6272]{1,0:T(8,128)(2,1)} %stack_rows.2.a_ref), channel_id=1, source_target_pairs={{0,4},{2,6},{4,0},{6,2},{8,12},{10,14},{12,8},{14,10},{1,5},{3,7},... | collective-permute-start | bytes 4816904 | tf_op jit(solution)/shard_map/ppermute | solution.py:26
  86.8 70.0 %collective-permute-start.47 = (bf16[256,6272]{1,0:T(8,128)(2,1)}, bf16[256,6272]{1,0:T(8,128)(2,1)S(1)}, u32[]{:S(2)}, u32[]{:S(2)}) collective-permute-start(bf16[256,6272]{1,0:T(8,128)(2,1)} %stack_rows.3.refs_0_.refs_4_.refs_1_.refs_2_), channel_id=1, source_target_pairs={{0,2},{2,0},{4,6},{6,4},{8,10},{10,8},{12,14},{14,12},{1,3},{3,1},... | collective-permute-start | bytes 9633800 | tf_op jit(solution)/shard_map/ppermute | solution.py:26
  88.1 190.7 %collective-permute-start.48 = (bf16[256,6272]{1,0:T(8,128)(2,1)}, bf16[256,6272]{1,0:T(8,128)(2,1)}, u32[]{:S(2)}, u32[]{:S(2)}) collective-permute-start(bf16[256,6272]{1,0:T(8,128)(2,1)} %stack_rows.3.refs_0_.refs_4_.refs_1_.refs_2_), channel_id=1, source_target_pairs={{0,1},{1,0},{2,3},{3,2},{4,5},{5,4},{6,7},{7,6},{8,9},{9,8},{10,11... | collective-permute-start | bytes 9633800 | tf_op jit(solution)/shard_map/ppermute | solution.py:26
  156.8 122.5 %collective-permute-start.49 = (bf16[256,6272]{1,0:T(8,128)(2,1)S(1)}, bf16[256,6272]{1,0:T(8,128)(2,1)}, u32[]{:S(2)}, u32[]{:S(2)}) collective-permute-start(bf16[256,6272]{1,0:T(8,128)(2,1)S(1)} %collective-permute-done.47.refs_1_.refs_5_.refs_3_.refs_4_), channel_id=1, source_target_pairs={{0,1},{1,0},{2,3},{3,2},{4,5},{5,4},{6,7},{7,6},{8,9},{9,8},{10,11... | collective-permute-start | bytes 9633800 | tf_op jit(solution)/shard_map/ppermute | solution.py:26
  164.9 25.1 %collective-permute-start = (bf16[3,256,256]{2,1,0:T(8,128)(2,1)}, bf16[3,256,256]{2,1,0:T(8,128)(2,1)}, u32[]{:S(2)}, u32[]{:S(2)}) collective-permute-start(bf16[3,256,256]{2,1,0:T(8,128)(2,1)} %get-tuple-element.61), channel_id=1, source_target_pairs={{0,2},{2,0},{4,6},{6,4},{8,10},{10,8},{12,14},{14,12},{1,3},{3,1},... | collective-permute-start | bytes 1179656 | tf_op jit(solution)/shard_map/ppermute | solution.py:26
  168.4 10.1 %collective-permute-start.30 = (bf16[3,64,256]{2,1,0:T(8,128)(2,1)}, bf16[3,64,256]{2,1,0:T(8,128)(2,1)S(1)}, u32[]{:S(2)}, u32[]{:S(2)}) collective-permute-start(bf16[3,64,256]{2,1,0:T(8,128)(2,1)} %get-tuple-element.93), channel_id=1, source_target_pairs={{0,2},{2,0},{4,6},{6,4},{8,10},{10,8},{12,14},{14,12},{1,3},{3,1},... | collective-permute-start | bytes 294920 | tf_op jit(solution)/shard_map/ppermute | solution.py:26
  169.1 12.6 %collective-permute-start.31 = (bf16[3,64,256]{2,1,0:T(8,128)(2,1)}, bf16[3,64,256]{2,1,0:T(8,128)(2,1)S(1)}, u32[]{:S(2)}, u32[]{:S(2)}) collective-permute-start(bf16[3,64,256]{2,1,0:T(8,128)(2,1)} %get-tuple-element.94), channel_id=1, source_target_pairs={{0,4},{2,6},{4,0},{6,2},{8,12},{10,14},{12,8},{14,10},{1,5},{3,7},... | collective-permute-start | bytes 294920 | tf_op jit(solution)/shard_map/ppermute | solution.py:26
  178.5 78.6 %copy-start.27 = (bf16[3,64,256]{2,1,0:T(8,128)(2,1)}, bf16[3,64,256]{2,1,0:T(8,128)(2,1)S(1)}, u32[]{:S(2)}) copy-start(bf16[3,64,256]{2,1,0:T(8,128)(2,1)S(1)} %collective-permute-done.30.refs_1_) | copy-start | bytes 294916
  178.5 6.6 %collective-permute-start.32 = (bf16[3,64,256]{2,1,0:T(8,128)(2,1)}, bf16[3,64,256]{2,1,0:T(8,128)(2,1)S(1)}, u32[]{:S(2)}, u32[]{:S(2)}) collective-permute-start(bf16[3,64,256]{2,1,0:T(8,128)(2,1)} %get-tuple-element.95), channel_id=1, source_target_pairs={{0,6},{2,4},{4,2},{6,0},{8,14},{10,12},{12,10},{14,8},{1,7},{3,5},... | collective-permute-start | bytes 294920 | tf_op jit(solution)/shard_map/ppermute | solution.py:26
  181.7 75.4 %copy-start.28 = (bf16[3,64,256]{2,1,0:T(8,128)(2,1)}, bf16[3,64,256]{2,1,0:T(8,128)(2,1)S(1)}, u32[]{:S(2)}) copy-start(bf16[3,64,256]{2,1,0:T(8,128)(2,1)S(1)} %collective-permute-done.31.refs_2_) | copy-start | bytes 294916
  181.7 6.9 %collective-permute-start.33 = (bf16[3,64,256]{2,1,0:T(8,128)(2,1)}, bf16[3,64,256]{2,1,0:T(8,128)(2,1)}, u32[]{:S(2)}, u32[]{:S(2)}) collective-permute-start(bf16[3,64,256]{2,1,0:T(8,128)(2,1)} %get-tuple-element.96), channel_id=1, source_target_pairs={{0,8},{2,10},{4,12},{6,14},{8,0},{10,2},{12,4},{14,6},{1,9},{3,11}... | collective-permute-start | bytes 294920 | tf_op jit(solution)/shard_map/ppermute | solution.py:26
  185.1 72.0 %copy-start.29 = (bf16[3,64,256]{2,1,0:T(8,128)(2,1)}, bf16[3,64,256]{2,1,0:T(8,128)(2,1)S(1)}, u32[]{:S(2)}) copy-start(bf16[3,64,256]{2,1,0:T(8,128)(2,1)S(1)} %collective-permute-done.32.refs_3_) | copy-start | bytes 294916
  185.1 20.7 %collective-permute-start.1 = (bf16[3,256,256]{2,1,0:T(8,128)(2,1)}, bf16[3,256,256]{2,1,0:T(8,128)(2,1)}, u32[]{:S(2)}, u32[]{:S(2)}) collective-permute-start(bf16[3,256,256]{2,1,0:T(8,128)(2,1)} %get-tuple-element.62), channel_id=1, source_target_pairs={{0,4},{2,6},{4,0},{6,2},{8,12},{10,14},{12,8},{14,10},{1,5},{3,7},... | collective-permute-start | bytes 1179656 | tf_op jit(solution)/shard_map/ppermute | solution.py:26
  188.6 25.4 %collective-permute-start.2 = (bf16[3,256,256]{2,1,0:T(8,128)(2,1)}, bf16[3,256,256]{2,1,0:T(8,128)(2,1)}, u32[]{:S(2)}, u32[]{:S(2)}) collective-permute-start(bf16[3,256,256]{2,1,0:T(8,128)(2,1)} %get-tuple-element.63), channel_id=1, source_target_pairs={{0,6},{2,4},{4,2},{6,0},{8,14},{10,12},{12,10},{14,8},{1,7},{3,5},... | collective-permute-start | bytes 1179656 | tf_op jit(solution)/shard_map/ppermute | solution.py:26
  190.1 26.7 %collective-permute-start.3 = (bf16[3,256,256]{2,1,0:T(8,128)(2,1)}, bf16[3,256,256]{2,1,0:T(8,128)(2,1)}, u32[]{:S(2)}, u32[]{:S(2)}) collective-permute-start(bf16[3,256,256]{2,1,0:T(8,128)(2,1)} %get-tuple-element.64), channel_id=1, source_target_pairs={{0,8},{2,10},{4,12},{6,14},{8,0},{10,2},{12,4},{14,6},{1,9},{3,11}... | collective-permute-start | bytes 1179656 | tf_op jit(solution)/shard_map/ppermute | solution.py:26
  205.8 43.1 %collective-permute-start.4 = (bf16[3,256,256]{2,1,0:T(8,128)(2,1)}, bf16[3,256,256]{2,1,0:T(8,128)(2,1)}, u32[]{:S(2)}, u32[]{:S(2)}) collective-permute-start(bf16[3,256,256]{2,1,0:T(8,128)(2,1)} %get-tuple-element.65), channel_id=1, source_target_pairs={{0,10},{2,8},{4,14},{6,12},{8,2},{10,0},{12,6},{14,4},{1,11},{3,9}... | collective-permute-start | bytes 1179656 | tf_op jit(solution)/shard_map/ppermute | solution.py:26
  214.0 34.9 %collective-permute-start.5 = (bf16[3,256,256]{2,1,0:T(8,128)(2,1)}, bf16[3,256,256]{2,1,0:T(8,128)(2,1)}, u32[]{:S(2)}, u32[]{:S(2)}) collective-permute-start(bf16[3,256,256]{2,1,0:T(8,128)(2,1)} %get-tuple-element.66), channel_id=1, source_target_pairs={{0,12},{2,14},{4,8},{6,10},{8,4},{10,6},{12,0},{14,2},{1,13},{3,15... | collective-permute-start | bytes 1179656 | tf_op jit(solution)/shard_map/ppermute | solution.py:26
  216.8 33.7 %collective-permute-start.6 = (bf16[3,256,256]{2,1,0:T(8,128)(2,1)}, bf16[3,256,256]{2,1,0:T(8,128)(2,1)}, u32[]{:S(2)}, u32[]{:S(2)}) collective-permute-start(bf16[3,256,256]{2,1,0:T(8,128)(2,1)} %get-tuple-element.67), channel_id=1, source_target_pairs={{0,14},{2,12},{4,10},{6,8},{8,6},{10,4},{12,2},{14,0},{1,15},{3,13... | collective-permute-start | bytes 1179656 | tf_op jit(solution)/shard_map/ppermute | solution.py:26
  249.0 25.3 %collective-permute-start.34 = (bf16[3,64,256]{2,1,0:T(8,128)(2,1)}, bf16[3,64,256]{2,1,0:T(8,128)(2,1)}, u32[]{:S(2)}, u32[]{:S(2)}) collective-permute-start(bf16[3,64,256]{2,1,0:T(8,128)(2,1)} %get-tuple-element.97), channel_id=1, source_target_pairs={{0,10},{2,8},{4,14},{6,12},{8,2},{10,0},{12,6},{14,4},{1,11},{3,9}... | collective-permute-start | bytes 294920 | tf_op jit(solution)/shard_map/ppermute | solution.py:26
  249.0 25.3 %collective-permute-start.35 = (bf16[3,64,256]{2,1,0:T(8,128)(2,1)}, bf16[3,64,256]{2,1,0:T(8,128)(2,1)}, u32[]{:S(2)}, u32[]{:S(2)}) collective-permute-start(bf16[3,64,256]{2,1,0:T(8,128)(2,1)} %get-tuple-element.98), channel_id=1, source_target_pairs={{0,12},{2,14},{4,8},{6,10},{8,4},{10,6},{12,0},{14,2},{1,13},{3,15... | collective-permute-start | bytes 294920 | tf_op jit(solution)/shard_map/ppermute | solution.py:26
  250.5 24.9 %collective-permute-start.36 = (bf16[3,64,256]{2,1,0:T(8,128)(2,1)}, bf16[3,64,256]{2,1,0:T(8,128)(2,1)}, u32[]{:S(2)}, u32[]{:S(2)}) collective-permute-start(bf16[3,64,256]{2,1,0:T(8,128)(2,1)} %get-tuple-element.99), channel_id=1, source_target_pairs={{0,14},{2,12},{4,10},{6,8},{8,6},{10,4},{12,2},{14,0},{1,15},{3,13... | collective-permute-start | bytes 294920 | tf_op jit(solution)/shard_map/ppermute | solution.py:26
  274.3 135.0 %collective-permute-start.7 = (bf16[2,2048,256]{2,1,0:T(8,128)(2,1)}, bf16[2,2048,256]{2,1,0:T(8,128)(2,1)}, u32[]{:S(2)}, u32[]{:S(2)}) collective-permute-start(bf16[2,2048,256]{2,1,0:T(8,128)(2,1)} %bitcast.29), channel_id=1, source_target_pairs={{0,1},{1,0},{2,3},{3,2},{4,5},{5,4},{6,7},{7,6},{8,9},{9,8},{10,11... | collective-permute-start | bytes 6291464 | tf_op jit(solution)/shard_map/ppermute | solution.py:26
  274.3 52.5 %collective-permute-start.15 = (bf16[3,256,256]{2,1,0:T(8,128)(2,1)}, bf16[3,256,256]{2,1,0:T(8,128)(2,1)}, u32[]{:S(2)}, u32[]{:S(2)}) collective-permute-start(bf16[3,256,256]{2,1,0:T(8,128)(2,1)} %get-tuple-element.77), channel_id=1, source_target_pairs={{0,2},{2,0},{4,6},{6,4},{8,10},{10,8},{12,14},{14,12},{1,3},{3,1},... | collective-permute-start | bytes 1179656 | tf_op jit(solution)/shard_map/ppermute | solution.py:26
  275.4 51.5 %collective-permute-start.16 = (bf16[3,256,256]{2,1,0:T(8,128)(2,1)}, bf16[3,256,256]{2,1,0:T(8,128)(2,1)}, u32[]{:S(2)}, u32[]{:S(2)}) collective-permute-start(bf16[3,256,256]{2,1,0:T(8,128)(2,1)} %get-tuple-element.78), channel_id=1, source_target_pairs={{0,4},{2,6},{4,0},{6,2},{8,12},{10,14},{12,8},{14,10},{1,5},{3,7},... | collective-permute-start | bytes 1179656 | tf_op jit(solution)/shard_map/ppermute | solution.py:26
  278.7 48.6 %collective-permute-start.17 = (bf16[3,256,256]{2,1,0:T(8,128)(2,1)}, bf16[3,256,256]{2,1,0:T(8,128)(2,1)}, u32[]{:S(2)}, u32[]{:S(2)}) collective-permute-start(bf16[3,256,256]{2,1,0:T(8,128)(2,1)} %get-tuple-element.79), channel_id=1, source_target_pairs={{0,6},{2,4},{4,2},{6,0},{8,14},{10,12},{12,10},{14,8},{1,7},{3,5},... | collective-permute-start | bytes 1179656 | tf_op jit(solution)/shard_map/ppermute | solution.py:26
  279.3 50.4 %collective-permute-start.18 = (bf16[3,256,256]{2,1,0:T(8,128)(2,1)}, bf16[3,256,256]{2,1,0:T(8,128)(2,1)S(1)}, u32[]{:S(2)}, u32[]{:S(2)}) collective-permute-start(bf16[3,256,256]{2,1,0:T(8,128)(2,1)} %get-tuple-element.80), channel_id=1, source_target_pairs={{0,8},{2,10},{4,12},{6,14},{8,0},{10,2},{12,4},{14,6},{1,9},{3,11}... | collective-permute-start | bytes 1179656 | tf_op jit(solution)/shard_map/ppermute | solution.py:26
  282.2 44.7 %copy-start.38 = (bf16[3,256,256]{2,1,0:T(8,128)(2,1)S(1)}, bf16[3,256,256]{2,1,0:T(8,128)(2,1)}, u32[]{:S(2)}) copy-start(bf16[3,256,256]{2,1,0:T(8,128)(2,1)} %get-tuple-element.81) | copy-start | bytes 1179652
  326.7 69.2 %collective-permute-start.51 = (bf16[256,2176]{1,0:T(8,128)(2,1)}, bf16[256,2176]{1,0:T(8,128)(2,1)S(1)}, u32[]{:S(2)}, u32[]{:S(2)}) collective-permute-start(bf16[256,2176]{1,0:T(8,128)(2,1)} %get-tuple-element.111), channel_id=1, source_target_pairs={{0,1},{1,0},{2,3},{3,2},{4,5},{5,4},{6,7},{7,6},{8,9},{9,8},{10,11... | collective-permute-start | bytes 3342344 | tf_op jit(solution)/shard_map/ppermute | solution.py:26
  326.8 38.1 %collective-permute-start.19 = (bf16[3,256,256]{2,1,0:T(8,128)(2,1)S(1)}, bf16[3,256,256]{2,1,0:T(8,128)(2,1)S(1)}, u32[]{:S(2)}, u32[]{:S(2)}) collective-permute-start(bf16[3,256,256]{2,1,0:T(8,128)(2,1)S(1)} %copy-done.38), channel_id=1, source_target_pairs={{0,10},{2,8},{4,14},{6,12},{8,2},{10,0},{12,6},{14,4},{1,11},{3,9}... | collective-permute-start | bytes 1179656 | tf_op jit(solution)/shard_map/ppermute | solution.py:26
  327.4 37.6 %collective-permute-start.20 = (bf16[3,256,256]{2,1,0:T(8,128)(2,1)}, bf16[3,256,256]{2,1,0:T(8,128)(2,1)S(1)}, u32[]{:S(2)}, u32[]{:S(2)}) collective-permute-start(bf16[3,256,256]{2,1,0:T(8,128)(2,1)} %get-tuple-element.82), channel_id=1, source_target_pairs={{0,12},{2,14},{4,8},{6,10},{8,4},{10,6},{12,0},{14,2},{1,13},{3,15... | collective-permute-start | bytes 1179656 | tf_op jit(solution)/shard_map/ppermute | solution.py:26
  329.7 35.3 %copy-start.8 = (bf16[3,256,256]{2,1,0:T(8,128)(2,1)}, bf16[3,256,256]{2,1,0:T(8,128)(2,1)S(1)}, u32[]{:S(2)}) copy-start(bf16[3,256,256]{2,1,0:T(8,128)(2,1)S(1)} %collective-permute-done.18.refs_4_) | copy-start | bytes 1179652
  329.7 35.3 %collective-permute-start.21 = (bf16[3,256,256]{2,1,0:T(8,128)(2,1)}, bf16[3,256,256]{2,1,0:T(8,128)(2,1)S(1)}, u32[]{:S(2)}, u32[]{:S(2)}) collective-permute-start(bf16[3,256,256]{2,1,0:T(8,128)(2,1)} %get-tuple-element.83), channel_id=1, source_target_pairs={{0,14},{2,12},{4,10},{6,8},{8,6},{10,4},{12,2},{14,0},{1,15},{3,13... | collective-permute-start | bytes 1179656 | tf_op jit(solution)/shard_map/ppermute | solution.py:26
  365.0 7.3 %collective-permute-start.37 = (bf16[2,512,256]{2,1,0:T(8,128)(2,1)}, bf16[2,512,256]{2,1,0:T(8,128)(2,1)S(1)}, u32[]{:S(2)}, u32[]{:S(2)}) collective-permute-start(bf16[2,512,256]{2,1,0:T(8,128)(2,1)} %bitcast.38), channel_id=1, source_target_pairs={{0,1},{1,0},{2,3},{3,2},{4,5},{5,4},{6,7},{7,6},{8,9},{9,8},{10,11... | collective-permute-start | bytes 1572872 | tf_op jit(solution)/shard_map/ppermute | solution.py:26
  369.9 87.7 %collective-permute-start.22 = (bf16[2,2048,256]{2,1,0:T(8,128)(2,1)}, bf16[2,2048,256]{2,1,0:T(8,128)(2,1)}, u32[]{:S(2)}, u32[]{:S(2)}) collective-permute-start(bf16[2,2048,256]{2,1,0:T(8,128)(2,1)} %bitcast.31), channel_id=1, source_target_pairs={{0,1},{1,0},{2,3},{3,2},{4,5},{5,4},{6,7},{7,6},{8,9},{9,8},{10,11... | collective-permute-start | bytes 6291464 | tf_op jit(solution)/shard_map/ppermute | solution.py:26
  378.3 24.0 %collective-permute-start.38 = (bf16[64,256]{1,0:T(8,128)(2,1)}, bf16[64,256]{1,0:T(8,128)(2,1)S(1)}, u32[]{:S(2)}, u32[]{:S(2)}) collective-permute-start(bf16[64,256]{1,0:T(8,128)(2,1)} %get-tuple-element.101), channel_id=1, source_target_pairs={{0,2},{2,0},{4,6},{6,4},{8,10},{10,8},{12,14},{14,12},{1,3},{3,1},... | collective-permute-start | bytes 98312 | tf_op jit(solution)/shard_map/ppermute | solution.py:26
  379.2 25.0 %collective-permute-start.39 = (bf16[64,256]{1,0:T(8,128)(2,1)}, bf16[64,256]{1,0:T(8,128)(2,1)S(1)}, u32[]{:S(2)}, u32[]{:S(2)}) collective-permute-start(bf16[64,256]{1,0:T(8,128)(2,1)} %get-tuple-element.102), channel_id=1, source_target_pairs={{0,4},{2,6},{4,0},{6,2},{8,12},{10,14},{12,8},{14,10},{1,5},{3,7},... | collective-permute-start | bytes 98312 | tf_op jit(solution)/shard_map/ppermute | solution.py:26
  396.0 44.3 %collective-permute-start.50 = (bf16[256,2176]{1,0:T(8,128)(2,1)}, bf16[256,2176]{1,0:T(8,128)(2,1)S(1)}, u32[]{:S(2)}, u32[]{:S(2)}) collective-permute-start(bf16[256,2176]{1,0:T(8,128)(2,1)} %get-tuple-element.109), channel_id=1, source_target_pairs={{0,1},{1,0},{2,3},{3,2},{4,5},{5,4},{6,7},{7,6},{8,9},{9,8},{10,11... | collective-permute-start | bytes 3342344 | tf_op jit(solution)/shard_map/ppermute | solution.py:26
  402.3 36.8 %copy-start.30 = (bf16[64,256]{1,0:T(8,128)(2,1)}, bf16[64,256]{1,0:T(8,128)(2,1)S(1)}, u32[]{:S(2)}) copy-start(bf16[64,256]{1,0:T(8,128)(2,1)S(1)} %collective-permute-done.38.refs_1_) | copy-start | bytes 98308
  402.3 39.6 %collective-permute-start.52 = (bf16[256,2176]{1,0:T(8,128)(2,1)}, bf16[256,2176]{1,0:T(8,128)(2,1)S(1)}, u32[]{:S(2)}, u32[]{:S(2)}) collective-permute-start(bf16[256,2176]{1,0:T(8,128)(2,1)} %merge.6), channel_id=1, source_target_pairs={{0,2},{2,0},{4,6},{6,4},{8,10},{10,8},{12,14},{14,12},{1,3},{3,1},... | collective-permute-start | bytes 3342344 | tf_op jit(solution)/shard_map/ppermute | solution.py:26
  404.3 5.0 collective-permute-start.40
  409.3 29.8 %collective-permute-start.41 = (bf16[64,256]{1,0:T(8,128)(2,1)S(1)}, bf16[64,256]{1,0:T(8,128)(2,1)S(1)}, u32[]{:S(2)}, u32[]{:S(2)}) collective-permute-start(bf16[64,256]{1,0:T(8,128)(2,1)S(1)} %copy-done.47), channel_id=1, source_target_pairs={{0,8},{2,10},{4,12},{6,14},{8,0},{10,2},{12,4},{14,6},{1,9},{3,11}... | collective-permute-start | bytes 98312 | tf_op jit(solution)/shard_map/ppermute | solution.py:26
  409.3 30.9 %collective-permute-start.42 = (bf16[64,256]{1,0:T(8,128)(2,1)S(1)}, bf16[64,256]{1,0:T(8,128)(2,1)S(1)}, u32[]{:S(2)}, u32[]{:S(2)}) collective-permute-start(bf16[64,256]{1,0:T(8,128)(2,1)S(1)} %copy-done.46), channel_id=1, source_target_pairs={{0,10},{2,8},{4,14},{6,12},{8,2},{10,0},{12,6},{14,4},{1,11},{3,9}... | collective-permute-start | bytes 98312 | tf_op jit(solution)/shard_map/ppermute | solution.py:26
  439.1 48.9 %copy-start.33 = (bf16[64,256]{1,0:T(8,128)(2,1)}, bf16[64,256]{1,0:T(8,128)(2,1)S(1)}, u32[]{:S(2)}) copy-start(bf16[64,256]{1,0:T(8,128)(2,1)S(1)} %collective-permute-done.41.refs_4_) | copy-start | bytes 98308
  439.1 20.0 %collective-permute-start.8 = (bf16[256,256]{1,0:T(8,128)(2,1)}, bf16[256,256]{1,0:T(8,128)(2,1)S(1)}, u32[]{:S(2)}, u32[]{:S(2)}) collective-permute-start(bf16[256,256]{1,0:T(8,128)(2,1)} %get-tuple-element.69), channel_id=1, source_target_pairs={{0,2},{2,0},{4,6},{6,4},{8,10},{10,8},{12,14},{14,12},{1,3},{3,1},... | collective-permute-start | bytes 393224 | tf_op jit(solution)/shard_map/ppermute | solution.py:26
  440.2 47.7 %copy-start.34 = (bf16[64,256]{1,0:T(8,128)(2,1)}, bf16[64,256]{1,0:T(8,128)(2,1)S(1)}, u32[]{:S(2)}) copy-start(bf16[64,256]{1,0:T(8,128)(2,1)S(1)} %collective-permute-done.42.refs_5_) | copy-start | bytes 98308
  440.2 20.4 %collective-permute-start.9 = (bf16[256,256]{1,0:T(8,128)(2,1)}, bf16[256,256]{1,0:T(8,128)(2,1)S(1)}, u32[]{:S(2)}, u32[]{:S(2)}) collective-permute-start(bf16[256,256]{1,0:T(8,128)(2,1)} %get-tuple-element.70), channel_id=1, source_target_pairs={{0,4},{2,6},{4,0},{6,2},{8,12},{10,14},{12,8},{14,10},{1,5},{3,7},... | collective-permute-start | bytes 393224 | tf_op jit(solution)/shard_map/ppermute | solution.py:26
  440.3 14.6 %collective-permute-start.43 = (bf16[64,256]{1,0:T(8,128)(2,1)S(1)}, bf16[64,256]{1,0:T(8,128)(2,1)S(1)}, u32[]{:S(2)}, u32[]{:S(2)}) collective-permute-start(bf16[64,256]{1,0:T(8,128)(2,1)S(1)} %copy-done.45), channel_id=1, source_target_pairs={{0,12},{2,14},{4,8},{6,10},{8,4},{10,6},{12,0},{14,2},{1,13},{3,15... | collective-permute-start | bytes 98312 | tf_op jit(solution)/shard_map/ppermute | solution.py:26
  441.9 13.9 %collective-permute-start.44 = (bf16[64,256]{1,0:T(8,128)(2,1)S(1)}, bf16[64,256]{1,0:T(8,128)(2,1)S(1)}, u32[]{:S(2)}, u32[]{:S(2)}) collective-permute-start(bf16[64,256]{1,0:T(8,128)(2,1)S(1)} %copy-done.44), channel_id=1, source_target_pairs={{0,14},{2,12},{4,10},{6,8},{8,6},{10,4},{12,2},{14,0},{1,15},{3,13... | collective-permute-start | bytes 98312 | tf_op jit(solution)/shard_map/ppermute | solution.py:26
  454.9 33.0 %collective-permute-start.10 = (bf16[256,256]{1,0:T(8,128)(2,1)S(1)}, bf16[256,256]{1,0:T(8,128)(2,1)S(1)}, u32[]{:S(2)}, u32[]{:S(2)}) collective-permute-start(bf16[256,256]{1,0:T(8,128)(2,1)S(1)} %copy-done.43), channel_id=1, source_target_pairs={{0,6},{2,4},{4,2},{6,0},{8,14},{10,12},{12,10},{14,8},{1,7},{3,5},... | collective-permute-start | bytes 393224 | tf_op jit(solution)/shard_map/ppermute | solution.py:26
  455.7 35.2 %collective-permute-start.11 = (bf16[256,256]{1,0:T(8,128)(2,1)S(1)}, bf16[256,256]{1,0:T(8,128)(2,1)S(1)}, u32[]{:S(2)}, u32[]{:S(2)}) collective-permute-start(bf16[256,256]{1,0:T(8,128)(2,1)S(1)} %copy-done.42), channel_id=1, source_target_pairs={{0,8},{2,10},{4,12},{6,14},{8,0},{10,2},{12,4},{14,6},{1,9},{3,11}... | collective-permute-start | bytes 393224 | tf_op jit(solution)/shard_map/ppermute | solution.py:26
  457.7 34.2 %collective-permute-start.12 = (bf16[256,256]{1,0:T(8,128)(2,1)S(1)}, bf16[256,256]{1,0:T(8,128)(2,1)S(1)}, u32[]{:S(2)}, u32[]{:S(2)}) collective-permute-start(bf16[256,256]{1,0:T(8,128)(2,1)S(1)} %copy-done.41), channel_id=1, source_target_pairs={{0,10},{2,8},{4,14},{6,12},{8,2},{10,0},{12,6},{14,4},{1,11},{3,9}... | collective-permute-start | bytes 393224 | tf_op jit(solution)/shard_map/ppermute | solution.py:26
  459.1 33.0 %collective-permute-start.13 = (bf16[256,256]{1,0:T(8,128)(2,1)S(1)}, bf16[256,256]{1,0:T(8,128)(2,1)S(1)}, u32[]{:S(2)}, u32[]{:S(2)}) collective-permute-start(bf16[256,256]{1,0:T(8,128)(2,1)S(1)} %copy-done.40), channel_id=1, source_target_pairs={{0,12},{2,14},{4,8},{6,10},{8,4},{10,6},{12,0},{14,2},{1,13},{3,15... | collective-permute-start | bytes 393224 | tf_op jit(solution)/shard_map/ppermute | solution.py:26
  460.7 61.0 %collective-permute-start.53 = (bf16[128,2176]{1,0:T(8,128)(2,1)}, bf16[128,2176]{1,0:T(8,128)(2,1)S(1)}, u32[]{:S(2)}, u32[]{:S(2)}) collective-permute-start(bf16[128,2176]{1,0:T(8,128)(2,1)} %get-tuple-element.113), channel_id=1, source_target_pairs={{0,4},{2,6},{4,0},{6,2},{8,12},{10,14},{12,8},{14,10},{1,5},{3,7},... | collective-permute-start | bytes 1671176 | tf_op jit(solution)/shard_map/ppermute | solution.py:26
  488.0 8.8 %collective-permute-start.14 = (bf16[256,256]{1,0:T(8,128)(2,1)S(1)}, bf16[256,256]{1,0:T(8,128)(2,1)S(1)}, u32[]{:S(2)}, u32[]{:S(2)}) collective-permute-start(bf16[256,256]{1,0:T(8,128)(2,1)S(1)} %copy-done.39), channel_id=1, source_target_pairs={{0,14},{2,12},{4,10},{6,8},{8,6},{10,4},{12,2},{14,0},{1,15},{3,13... | collective-permute-start | bytes 393224 | tf_op jit(solution)/shard_map/ppermute | solution.py:26
  490.9 10.5 %collective-permute-start.23 = (bf16[256,256]{1,0:T(8,128)(2,1)}, bf16[256,256]{1,0:T(8,128)(2,1)S(1)}, u32[]{:S(2)}, u32[]{:S(2)}) collective-permute-start(bf16[256,256]{1,0:T(8,128)(2,1)} %get-tuple-element.85), channel_id=1, source_target_pairs={{0,2},{2,0},{4,6},{6,4},{8,10},{10,8},{12,14},{14,12},{1,3},{3,1},... | collective-permute-start | bytes 393224 | tf_op jit(solution)/shard_map/ppermute | solution.py:26
  491.9 10.5 %collective-permute-start.24 = (bf16[256,256]{1,0:T(8,128)(2,1)}, bf16[256,256]{1,0:T(8,128)(2,1)S(1)}, u32[]{:S(2)}, u32[]{:S(2)}) collective-permute-start(bf16[256,256]{1,0:T(8,128)(2,1)} %get-tuple-element.86), channel_id=1, source_target_pairs={{0,4},{2,6},{4,0},{6,2},{8,12},{10,14},{12,8},{14,10},{1,5},{3,7},... | collective-permute-start | bytes 393224 | tf_op jit(solution)/shard_map/ppermute | solution.py:26
  492.1 12.0 %collective-permute-start.25 = (bf16[256,256]{1,0:T(8,128)(2,1)}, bf16[256,256]{1,0:T(8,128)(2,1)S(1)}, u32[]{:S(2)}, u32[]{:S(2)}) collective-permute-start(bf16[256,256]{1,0:T(8,128)(2,1)} %get-tuple-element.87), channel_id=1, source_target_pairs={{0,6},{2,4},{4,2},{6,0},{8,14},{10,12},{12,10},{14,8},{1,7},{3,5},... | collective-permute-start | bytes 393224 | tf_op jit(solution)/shard_map/ppermute | solution.py:26
  496.8 15.4 %collective-permute-start.26 = (bf16[256,256]{1,0:T(8,128)(2,1)}, bf16[256,256]{1,0:T(8,128)(2,1)S(1)}, u32[]{:S(2)}, u32[]{:S(2)}) collective-permute-start(bf16[256,256]{1,0:T(8,128)(2,1)} %get-tuple-element.88), channel_id=1, source_target_pairs={{0,8},{2,10},{4,12},{6,14},{8,0},{10,2},{12,4},{14,6},{1,9},{3,11}... | collective-permute-start | bytes 393224 | tf_op jit(solution)/shard_map/ppermute | solution.py:26
  501.4 14.0 %collective-permute-start.27 = (bf16[256,256]{1,0:T(8,128)(2,1)}, bf16[256,256]{1,0:T(8,128)(2,1)S(1)}, u32[]{:S(2)}, u32[]{:S(2)}) collective-permute-start(bf16[256,256]{1,0:T(8,128)(2,1)} %get-tuple-element.89), channel_id=1, source_target_pairs={{0,10},{2,8},{4,14},{6,12},{8,2},{10,0},{12,6},{14,4},{1,11},{3,9}... | collective-permute-start | bytes 393224 | tf_op jit(solution)/shard_map/ppermute | solution.py:26
  502.3 13.1 %collective-permute-start.28 = (bf16[256,256]{1,0:T(8,128)(2,1)}, bf16[256,256]{1,0:T(8,128)(2,1)S(1)}, u32[]{:S(2)}, u32[]{:S(2)}) collective-permute-start(bf16[256,256]{1,0:T(8,128)(2,1)} %get-tuple-element.90), channel_id=1, source_target_pairs={{0,12},{2,14},{4,8},{6,10},{8,4},{10,6},{12,0},{14,2},{1,13},{3,15... | collective-permute-start | bytes 393224 | tf_op jit(solution)/shard_map/ppermute | solution.py:26
  504.0 11.4 %collective-permute-start.29 = (bf16[256,256]{1,0:T(8,128)(2,1)}, bf16[256,256]{1,0:T(8,128)(2,1)S(1)}, u32[]{:S(2)}, u32[]{:S(2)}) collective-permute-start(bf16[256,256]{1,0:T(8,128)(2,1)} %get-tuple-element.91), channel_id=1, source_target_pairs={{0,14},{2,12},{4,10},{6,8},{8,6},{10,4},{12,2},{14,0},{1,15},{3,13... | collective-permute-start | bytes 393224 | tf_op jit(solution)/shard_map/ppermute | solution.py:26
  525.9 28.9 %collective-permute-start.54 = (bf16[64,2176]{1,0:T(8,128)(2,1)}, bf16[64,2176]{1,0:T(8,128)(2,1)S(1)}, u32[]{:S(2)}, u32[]{:S(2)}) collective-permute-start(bf16[64,2176]{1,0:T(8,128)(2,1)} %get-tuple-element.115), channel_id=1, source_target_pairs={{0,8},{2,10},{4,12},{6,14},{8,0},{10,2},{12,4},{14,6},{1,9},{3,11}... | collective-permute-start | bytes 835592 | tf_op jit(solution)/shard_map/ppermute | solution.py:26
  (40 other events, 520.0 us)

commit v2 on v1

v2 whole, which is shorter than its diff:
```python
import math

import jax
import jax.numpy as jnp
from jax import lax
from jax.experimental import pallas as pl
from jax.experimental.pallas import tpu as pltpu
from jax.sharding import PartitionSpec as P


LV = 4096
FRAMES = 16
DHV = 128
DHA = 64
LANES = 128
LOG2E = 1.4426950408889634
VIDEO_PARTS = 2


BF16 = jnp.bfloat16
F32 = jnp.float32


def swap(value, axis, mask):
    count = lax.axis_size(axis)
    return lax.ppermute(value, axis, [(j, j ^ mask) for j in range(count)])


def cost(flops, exps, moved):
    return pl.CostEstimate(flops=int(flops), transcendentals=int(exps), bytes_accessed=int(moved))


def nt(a, b):
    return lax.dot_general(a, b, (((1,), (1,)), ((), ())), preferred_element_type=F32)


def pack(entries, tok_count):
    rows = [a.shape[0] for a, _, _ in entries]
    wide = entries[0][0].shape[1] // tok_count // entries[0][2]
    n = len(entries)
    if wide % LANES:
        cut = [
            a.reshape(a.shape[0], tok_count, parts, wide)[:, :, part].transpose(1, 0, 2)
            for a, part, parts in entries
        ]
        return jnp.concatenate(cut, axis=1)

    def body(*refs):
        at = 0
        for a in range(n):
            refs[n][0, at : at + rows[a], :] = refs[a][...]
            at += rows[a]

    total = sum(rows)
    return pl.pallas_call(
        body,
        grid=(tok_count,),
        out_shape=jax.ShapeDtypeStruct((tok_count, total, wide), BF16),
        in_specs=[
            pl.BlockSpec((a.shape[0], wide), lambda m, p=part, q=parts: (0, m * q + p))
            for a, part, parts in entries
        ],
        out_specs=pl.BlockSpec((1, total, wide), lambda m: (m, 0, 0)),
        cost_estimate=cost(0, 0, 4 * total * tok_count * wide),
        name="pack",
    )(*[a for a, _, _ in entries])


def unpack(sources, rows):
    tok_count = sources[0][0][0].shape[0]
    wides = [entry[0][0].shape[2] for entry in sources]
    parts = [len(entry) for entry in sources]
    if any(w % LANES for w in wides):
        outs = []
        for entry, r, w in zip(sources, rows, wides):
            cut = [array[:, at : at + r].transpose(1, 0, 2) for array, at in entry]
            outs.append(jnp.stack(cut, axis=2).reshape(r, tok_count * len(entry) * w))
        return outs

    def body(*refs):
        at = 0
        for e, (w, count) in enumerate(zip(wides, parts)):
            out = refs[sum(parts) + e]
            for p in range(count):
                out[:, p * w : (p + 1) * w] = refs[at][0]
                at += 1

    flat = [(array, at, r) for entry, r in zip(sources, rows) for array, at in entry]
    for _, at, r in flat:
        assert at % r == 0
    return pl.pallas_call(
        body,
        grid=(tok_count,),
        out_shape=[
            jax.ShapeDtypeStruct((r, tok_count * w * count), BF16)
            for r, w, count in zip(rows, wides, parts)
        ],
        in_specs=[
            pl.BlockSpec((1, r, array.shape[2]), lambda m, k=at // r: (m, k, 0))
            for array, at, r in flat
        ],
        out_specs=[
            pl.BlockSpec((r, w * count), lambda m: (0, m))
            for r, w, count in zip(rows, wides, parts)
        ],
        cost_estimate=cost(0, 0, 4 * sum(r * w for r, w in zip(rows, wides)) * tok_count),
        name="unpack",
    )(*[array for array, _, _ in flat])


def stack_rows(first, second):
    rows, wide = first.shape

    def body(a_ref, b_ref, out_ref):
        out_ref[:rows] = a_ref[...]
        out_ref[rows:] = b_ref[...]

    return pl.pallas_call(
        body,
        out_shape=jax.ShapeDtypeStruct((2 * rows, wide), BF16),
        cost_estimate=cost(0, 0, 8 * rows * wide),
        name="stack_rows",
    )(first, second)


def lane_of(shape):
    return lax.broadcasted_iota(jnp.int32, shape, len(shape) - 1)


def one_head(queries, parts, scale):
    factor = scale * LOG2E
    top = total = summed = None
    for keys, values in parts:
        scores = nt(queries, keys)
        peak = jnp.max(scores, axis=1, keepdims=True)
        new_top = peak if top is None else jnp.maximum(top, peak)
        exps = jnp.exp2((scores - new_top) * factor)
        sums = jnp.sum(exps, axis=1, keepdims=True)
        part = jnp.dot(exps.astype(BF16), values, preferred_element_type=F32)
        if top is None:
            total, summed = sums, part
        else:
            fade = jnp.exp2((top - new_top) * factor)
            total = total * fade + sums
            summed = summed * fade + part
        top = new_top
    return total, summed


def pick(lanes, width, keys, index):
    if lanes == width:
        return keys
    here = (lane_of(keys.shape) // width) == index
    return jnp.where(here, keys, jnp.zeros_like(keys))


def self_attention(own, other, segments):
    tok_count, total, columns = own.shape
    lanes = min(LANES, columns)

    def body(*refs):
        out_ref = refs[-1]
        row_at = 0
        for g, (rows, width, _) in enumerate(segments):
            key_a, value_a, q_ref, key_b, value_b, gate_ref = refs[6 * g : 6 * g + 6]
            gates = gate_ref[...]
            heads = lanes // width
            scale = 1.0 / math.sqrt(width)
            some = max(1, min(tok_count, 512 // rows))
            span = max(1, min(tok_count, 1024 // rows))
            here = slice(row_at, row_at + rows)
            row_at += rows

            def step(b, carry):
                at = b * some
                q = q_ref[pl.ds(at, some)].reshape(some * rows, lanes)
                result = None
                for head in range(heads):
                    parts = []
                    for keys, values in ((key_a, value_a), (key_b, value_b)):
                        for c in range(0, tok_count, span):
                            k = keys[c : c + span].reshape(span * rows, lanes)
                            v = values[c : c + span].reshape(span * rows, lanes)
                            parts.append((pick(lanes, width, k, head), v))
                    whole, summed = one_head(q, parts, scale)
                    done = summed / whole
                    if result is None:
                        result = done
                    else:
                        result = jnp.where(lane_of(done.shape) // width == head, done, result)
                result = (result * gates).astype(BF16)
                out_ref[pl.ds(at, some), here, :] = result.reshape(some, rows, lanes)
                return carry

            lax.fori_loop(0, tok_count // some, step, 0)

    in_specs, operands = [], []
    scores = base = 0
    for rows, width, gate in segments:
        assert base % rows == 0
        first = base // rows
        for array, which in ((own, 0), (own, 1), (own, 2), (other, 0), (other, 1)):
            in_specs.append(
                pl.BlockSpec((tok_count, rows, lanes), lambda i, k=first + which: (0, k, i))
            )
            operands.append(array)
        in_specs.append(pl.BlockSpec((1, lanes), lambda i: (0, i)))
        operands.append(gate)
        scores += (tok_count * rows) ** 2 * 2 * (columns // width)
        base += 3 * rows
    out_rows = sum(rows for rows, _, _ in segments)
    return pl.pallas_call(
        body,
        grid=(columns // lanes,),
        out_shape=jax.ShapeDtypeStruct((tok_count, out_rows, columns), BF16),
        in_specs=in_specs,
        out_specs=pl.BlockSpec((tok_count, out_rows, lanes), lambda i: (0, 0, i)),
        cost_estimate=cost(scores * 4 * LANES, scores, 10 * tok_count * total * columns),
        name="self_attention",
    )(*operands)


def video_cross_local(queries, pieces, marks, slopes, gate, place, span):
    counted, columns = queries.shape
    keyed = pieces[0].shape[0]
    n = len(pieces)
    steps = columns // LANES
    heads = LANES // DHA
    factor = LOG2E / math.sqrt(DHA)

    def body(slope_ref, place_ref, q_ref, *refs):
        gate_ref, out_ref = refs[3 * n :]
        i = pl.program_id(0)
        q = q_ref[...]
        at = place_ref[0]
        if span % counted == 0:
            mine = (at // span).astype(F32)
        else:
            col = lax.broadcasted_iota(jnp.int32, (1, counted), 1)
            mine = ((at + col) // span).astype(F32)
        gaps, turned = [], []
        for p in range(n):
            frame = refs[3 * p + 2][...].astype(F32)
            if counted > LANES:
                frame = jnp.concatenate([frame] * (counted // LANES), axis=1)
            gaps.append(jnp.abs(frame[:, :counted] - mine))
            turned.append(jnp.transpose(refs[3 * p + 1][...]))
        results = []
        for head in range(heads):
            slope = slope_ref[i * heads + head] * LOG2E
            scores = [
                nt(pick(LANES, DHA, refs[3 * p][...], head), q) * factor - gaps[p] * slope
                for p in range(n)
            ]
            top = jnp.max(scores[0], axis=0, keepdims=True)
            for one in scores[1:]:
                top = jnp.maximum(top, jnp.max(one, axis=0, keepdims=True))
            total = summed = None
            for p in range(n):
                exps = jnp.exp2(scores[p] - top)
                sums = jnp.sum(exps, axis=0, keepdims=True)
                part = jnp.dot(
                    turned[p][head * DHA : (head + 1) * DHA],
                    exps.astype(BF16),
                    preferred_element_type=F32,
                )
                total = sums if total is None else total + sums
                summed = part if summed is None else summed + part
            results.append(summed / total)
        result = jnp.transpose(jnp.concatenate(results, axis=0))
        out_ref[...] = (result * gate_ref[...]).astype(BF16)

    piece = [
        pl.BlockSpec((keyed, LANES), lambda i: (0, i)),
        pl.BlockSpec((keyed, LANES), lambda i: (0, steps + i)),
        pl.BlockSpec((keyed, LANES), lambda i: (0, steps)),
    ]
    scores = counted * keyed * n * steps * heads
    return pl.pallas_call(
        body,
        grid=(steps,),
        out_shape=jax.ShapeDtypeStruct((counted, columns), BF16),
        in_specs=[
            pl.BlockSpec(memory_space=pltpu.SMEM),
            pl.BlockSpec(memory_space=pltpu.SMEM),
            pl.BlockSpec((counted, LANES), lambda i: (0, i)),
        ]
        + piece * n
        + [pl.BlockSpec((1, LANES), lambda i: (0, i))],
        out_specs=pl.BlockSpec((counted, LANES), lambda i: (0, i)),
        cost_estimate=cost(scores * 4 * LANES, scores, 4 * columns * (counted + n * keyed)),
        name="video_cross",
    )(slopes, place, queries, *[a for k, f in zip(pieces, marks) for a in (k, k, f)], gate)


def audio_cross_local(pieces, keys, values, slopes, place, span):
    counted = pieces[0].shape[0]
    n = len(pieces)
    keyed, columns = keys.shape
    steps = columns // LANES
    heads = LANES // DHA
    count = steps * heads
    factor = LOG2E / math.sqrt(DHA)

    def body(slope_ref, place_ref, k_ref, v_ref, *refs):
        q_refs, f_refs, o_refs = refs[:n], refs[n : 2 * n], refs[2 * n : 3 * n]
        stats, times = refs[3 * n :]
        i = pl.program_id(0)
        at = place_ref[0]

        @pl.when(i == 0)
        def _():
            stats[...] = jnp.zeros_like(stats)
            for p in range(n):
                here = slice(p * counted, (p + 1) * counted)
                times[:, here] = jnp.transpose(f_refs[p][...].astype(F32))[0:8, :]

        @pl.when(i < steps)
        def _():
            keys_here = k_ref[...]
            turned = jnp.transpose(v_ref[...])
            q = jnp.concatenate([r[...] for r in q_refs], axis=0)
            mine = times[0:1, :]
            if span % keyed == 0:
                gap = jnp.abs(mine - (at // span).astype(F32))
            else:
                row = lax.broadcasted_iota(jnp.int32, (keyed, 1), 0)
                gap = jnp.abs(mine - ((at + row) // span).astype(F32))
            results = []
            for head in range(heads):
                index = i * heads + head
                slope = slope_ref[index] * LOG2E
                scores = nt(pick(LANES, DHA, keys_here, head), q)
                if span % keyed == 0:
                    top = jnp.max(scores, axis=0, keepdims=True)
                    exps = jnp.exp2((scores - top) * factor)
                    top = top * factor - gap * slope
                else:
                    scores = scores * factor - gap * slope
                    top = jnp.max(scores, axis=0, keepdims=True)
                    exps = jnp.exp2(scores - top)
                total = jnp.sum(exps, axis=0, keepdims=True)
                part = jnp.dot(
                    turned[head * DHA : (head + 1) * DHA],
                    exps.astype(BF16),
                    preferred_element_type=F32,
                )
                results.append(part * (1.0 / total))
                stats[pl.ds(index, 1), :] = top + jnp.log2(total)
            result = jnp.transpose(jnp.concatenate(results, axis=0).astype(BF16))
            for p in range(n):
                o_refs[p][...] = result[p * counted : (p + 1) * counted]

        @pl.when(i == steps)
        def _():
            for p in range(n):
                here = slice(p * counted, (p + 1) * counted)
                o_refs[p][...] = spread_stats(jnp.transpose(stats[:, here]), count)

    def at_step(i):
        return jnp.minimum(i, steps - 1)

    scores = counted * keyed * n * count
    return pl.pallas_call(
        body,
        grid=(steps + 1,),
        out_shape=[jax.ShapeDtypeStruct((counted, columns + LANES), BF16)] * n,
        in_specs=[
            pl.BlockSpec(memory_space=pltpu.SMEM),
            pl.BlockSpec(memory_space=pltpu.SMEM),
        ]
        + [pl.BlockSpec((keyed, LANES), lambda i: (0, at_step(i)))] * 2
        + [pl.BlockSpec((counted, LANES), lambda i: (0, at_step(i)))] * n
        + [pl.BlockSpec((counted, LANES), lambda i: (0, steps))] * n,
        out_specs=[pl.BlockSpec((counted, LANES), lambda i: (0, i))] * n,
        scratch_shapes=[
            pltpu.VMEM((LANES, n * counted), F32),
            pltpu.VMEM((8, n * counted), F32),
        ],
        cost_estimate=cost(scores * 4 * LANES, scores, 4 * columns * (n * counted + keyed)),
        name="audio_cross",
    )(slopes, place, keys, values, *pieces, *pieces)


def spread_stats(stats, count):
    lane = lane_of(stats.shape)
    first = stats.astype(BF16).astype(F32)
    rest = stats - first
    second = rest.astype(BF16).astype(F32)
    third = rest - second
    second = pltpu.roll(second, count, 1)
    third = pltpu.roll(third, 2 * count, 1)
    packed = jnp.where(lane < count, first, jnp.where(lane < 2 * count, second, third))
    return jnp.where(lane < 3 * count, packed, 0.0).astype(BF16)


def read_stats(packed, count):
    terms = packed.astype(F32)
    second = pltpu.roll(terms, LANES - count, 1)
    third = pltpu.roll(terms, LANES - 2 * count, 1)
    return terms + second + third


def merge(mine, theirs, form, gate=None):
    rows, wide = mine.shape
    columns = wide - LANES
    count = columns // DHA
    heads = LANES // DHA
    half = rows // 2

    def body(a_ref, b_ref, *refs):
        a_stat = read_stats(a_ref[:, columns:], count)
        b_stat = read_stats(b_ref[:, columns:], count)
        top = jnp.maximum(a_stat, b_stat)
        a_part = jnp.exp2(a_stat - top)
        total = a_part + jnp.exp2(b_stat - top)
        share = a_part / total
        high = share.astype(BF16)
        low = (share - high.astype(F32)).astype(BF16)

        def put(here, value):
            if form == "halves":
                refs[0][:, here] = value[:half]
                refs[1][:, here] = value[half:]
            else:
                refs[-1][:, here] = value

        for j in range(columns // LANES):
            here = slice(j * LANES, (j + 1) * LANES)
            row = lax.broadcasted_iota(jnp.int32, (LANES, LANES), 0)
            spot = (row == j * heads + lane_of((LANES, LANES)) // DHA).astype(F32).astype(BF16)
            weight = jnp.dot(high, spot, preferred_element_type=F32)
            weight = weight + jnp.dot(low, spot, preferred_element_type=F32)
            theirs_here = b_ref[:, here].astype(F32)
            joined = theirs_here + (a_ref[:, here].astype(F32) - theirs_here) * weight
            if form == "last":
                joined = joined * refs[0][:, here]
            put(here, joined.astype(BF16))
        if form != "last":
            put(slice(columns, wide), spread_stats(top + jnp.log2(total), count))

    if form == "halves":
        shapes = [jax.ShapeDtypeStruct((half, wide), BF16)] * 2
    elif form == "last":
        shapes = jax.ShapeDtypeStruct((rows, columns), BF16)
    else:
        shapes = jax.ShapeDtypeStruct((rows, wide), BF16)
    extra = () if gate is None else (gate,)
    return pl.pallas_call(
        body,
        out_shape=shapes,
        cost_estimate=cost(0, rows * wide, 6 * rows * wide),
        name="merge",
    )(mine, theirs, *extra)


def video_parts(wide):
    return VIDEO_PARTS if wide % (VIDEO_PARTS * LANES) == 0 else 1


def on_device(
    video_query,
    video_key,
    video_value,
    audio_query,
    audio_key,
    audio_value,
    cross_audio_query,
    cross_video_key,
    cross_video_value,
    cross_video_query,
    cross_audio_key,
    cross_audio_value,
    audio_frames,
    into_audio_slope,
    into_video_slope,
    timestep,
    video_gate,
    audio_gate,
    into_audio_gate,
    into_video_gate,
):
    tok_count = lax.axis_size("tok")
    head_count = lax.axis_size("head")
    tok = lax.axis_index("tok")
    samples, video_rows, video_columns = video_query.shape
    audio_rows, audio_columns = audio_query.shape[1:]
    patches = LV // FRAMES
    place = ((tok * head_count + lax.axis_index("head")) * video_rows).reshape(1)
    masks = [1 << b for b in reversed(range(tok_count.bit_length() - 1))]

    def gate_row(table, sample):
        return lax.dynamic_slice_in_dim(table, timestep[sample], 1, 0).astype(F32)

    def gate_part(row, part, parts):
        wide = row.shape[1] // tok_count
        piece = wide // parts
        return lax.dynamic_slice_in_dim(row, tok * wide + part * piece, piece, 1)

    def collect(own):
        for step, mask in enumerate(masks):
            received = swap(own, "tok", mask)
            if step < len(masks) - 1:
                own = stack_rows(own, received)
        return [own, received, swap(own, "head", 1), swap(received, "head", 1)]

    def across(blocks):
        return lax.all_to_all(blocks, "tok", split_axis=0, concat_axis=0, tiled=True)

    def self_part(members):
        entries = [(a, part, parts) for arrays, _, _, part, parts in members for a in arrays]
        bundle = pack(entries, tok_count)
        own = across(bundle)
        other = swap(own, "head", 1)
        segments = [
            (arrays[0].shape[0], width, gate_part(gate, part, parts))
            for arrays, width, gate, part, parts in members
        ]
        outs = self_attention(own, other, segments)
        return across(outs)

    results = []
    for s in range(samples):
        frames = jnp.broadcast_to(
            audio_frames[s][:, None].astype(F32), (audio_rows, LANES)
        ).astype(BF16)
        asked = collect(jnp.concatenate((cross_audio_query[s], frames), axis=1))
        kept = collect(jnp.concatenate((cross_audio_key[s], cross_audio_value[s]), axis=1))
        partial = audio_cross_local(
            asked, cross_video_key[s], cross_video_value[s], into_audio_slope, place, patches
        )
        got = [swap(partial[2], "head", 1), swap(partial[3], "head", 1)]
        mine = merge(partial[0], got[0], "whole")
        send = merge(partial[1], got[1], "whole")
        for step, mask in enumerate(reversed(masks)):
            received = swap(send, "tok", mask)
            if step < len(masks) - 1:
                mine, send = merge(mine, received, "halves")
            else:
                audio_cross = merge(mine, received, "last", gate_row(into_audio_gate, s))
        video = ((video_key[s], video_value[s], video_query[s]), DHV, gate_row(video_gate, s))
        audio = ((audio_key[s], audio_value[s], audio_query[s]), DHA, gate_row(audio_gate, s))
        parts = video_parts(video_columns // tok_count)
        if video_columns // parts == audio_columns:
            outs = [self_part([video + (0, parts), audio + (0, 1)])]
            sound = (outs[0], video_rows)
        else:
            outs = [self_part([video + (0, parts)])]
            sound = (self_part([audio + (0, 1)]), 0)
        for p in range(1, parts):
            outs.append(self_part([video + (p, parts)]))
        video_self, audio_self = unpack(
            [[(array, 0) for array in outs], [sound]], [video_rows, audio_rows]
        )
        video_cross = video_cross_local(
            cross_video_query[s],
            kept,
            asked,
            into_video_slope,
            gate_row(into_video_gate, s),
            place,
            patches,
        )
        results.append((video_self, audio_self, audio_cross, video_cross))
    return tuple(jnp.stack(parts) for parts in zip(*results))


def solution(mesh):
    rows = P("groups", ("tok", "head"), None)
    placed = (rows,) * 12 + (
        P("groups", ("tok", "head")),
        P(),
        P(),
        P("groups"),
        P(),
        P(),
        P(),
        P(),
    )

    return jax.shard_map(
        on_device, mesh=mesh, in_specs=placed, out_specs=(rows,) * 4, check_vma=False
    )
```

time: 560 us -> 448 us (0.80)
  starting transfers between devices: 103 us -> 38.4 us
  Pallas kernels: 182 us -> 147 us
  waiting for transfers between devices: 257 us -> 250 us
    ppermute x55 -> x17, waiting for transfers between devices: 257 us -> 88.2 us  [swap(): return lax.ppermute(value, axis, [(j, j ^ mask) for j in range(count)])]
    all_to_all x0 -> x4, waiting for transfers between devices: none -> 161 us  [across(): lax.all_to_all(blocks, 'tok', split_axis=0, concat_axis=0, tiled=True)]
    ppermute x55 -> x17, starting transfers between devices: 103 us -> 15.9 us  [swap(): return lax.ppermute(value, axis, [(j, j ^ mask) for j in range(count)])]
    all_to_all x0 -> x4, starting transfers between devices: none -> 22.4 us  [across(): lax.all_to_all(blocks, 'tok', split_axis=0, concat_axis=0, tiled=True)]
    pallas_call x1, Pallas kernels: 44.6 us -> 23.1 us  [audio_cross_local(): pl.pallas_call(body, grid=(steps + 1,), out_shape=[jax.ShapeDtypeStruct((...]
    pallas_call x10 -> x5, Pallas kernels: 84.6 us -> 74.2 us  [the longest x2 55.5 us: self_attention(): pl.pallas_call(body, grid=(columns // lanes,), out_shape=jax.ShapeDtypeSt...]
    pallas_call x5, Pallas kernels: 21.5 us -> 15.7 us  [merge(): pl.pallas_call(body, out_shape=shapes, cost_estimate=cost(0, rows * wide,...]
  transfers between devices with their start and end apart: 55 -> 21, of which waited for: 15 -> 7; matrix products, arithmetic and copies ran while one was open for 1% -> 1% of each run, Pallas kernels for 30% -> 30%
where the time goes in v2:
time: 448 us; the launch traced here: 446 us
  waiting for transfers between devices  250 us (56%)
  Pallas kernels  147 us (33%)
  starting transfers between devices  38.4 us (9%)
  local copies, waits for them, and re-layouts  5.05 us (1%)
  other arithmetic  4.96 us (1%)
    all_to_all x4, waiting for transfers between devices, across(): lax.all_to_all(blocks, 'tok', split_axis=0, concat_axis=0, tiled=True)  161 us
    ppermute x17, waiting for transfers between devices, swap(): return lax.ppermute(value, axis, [(j, j ^ mask) for j in range(count)])  88.2 us
    pallas_call x2, Pallas kernels, self_attention(): pl.pallas_call(body, grid=(columns // lanes,), out_shape=jax.ShapeDtypeSt...  55.5 us
    pallas_call x1, Pallas kernels, video_cross_local(): pl.pallas_call(body, grid=(steps,), out_shape=jax.ShapeDtypeStruct((count...  24.4 us
    pallas_call x1, Pallas kernels, audio_cross_local(): pl.pallas_call(body, grid=(steps + 1,), out_shape=[jax.ShapeDtypeStruct((...  23.1 us
    all_to_all x4, starting transfers between devices, across(): lax.all_to_all(blocks, 'tok', split_axis=0, concat_axis=0, tiled=True)  22.4 us
    ppermute x17, starting transfers between devices, swap(): return lax.ppermute(value, axis, [(j, j ^ mask) for j in range(count)])  15.9 us
    pallas_call x5, Pallas kernels, merge(): pl.pallas_call(body, out_shape=shapes, cost_estimate=cost(0, rows * wide,...  15.7 us
  transfers between devices with their start and end apart: 21, of which 7 were waited for; matrix products, arithmetic and copies ran while one was open for 1% of the time, Pallas kernels for 30%

profile of v2, /device:TPU:0, one launch (start us, length us, event | category | flops | bytes accessed | tf_op | source)
XLA Modules:
  0.0 446.2 jit_solution(14807171596657626564)
XLA Ops:
  0.6 6.3 %pack.3 = bf16[8,768,256]{2,1,0:T(8,128)(2,1)} custom-call(bf16[256,4096]{1,0:T(8,128)(2,1)} %bitcast.23, bf16[256,4096]{1,0:T(8,128)(2,1)} %bitcast.25, bf16[256,4096]{1,0:T(8,128)(2,1)} %bitcast.27), custom_call_target="tpu_custom_call" | custom-call | bytes 6291456 | tf_op jit(solution)/shard_map/pack/pallas_call | solution.py:55
  6.9 7.3 %all-to-all-start.2 = ((bf16[8,768,256]{2,1,0:T(8,128)(2,1)}), bf16[8,768,256]{2,1,0:T(8,128)(2,1)}, u32[]{:S(2)}, u32[]{:S(2)}) async-start(bf16[8,768,256]{2,1,0:T(8,128)(2,1)} %pack.3), calls=%async_computation.2 | async-start | bytes 6291456 | tf_op jit(solution)/shard_map/all_to_all | solution.py:508
  14.2 6.6 %pack.2 = bf16[8,960,256]{2,1,0:T(8,128)(2,1)} custom-call(bf16[256,4096]{1,0:T(8,128)(2,1)} %bitcast.24, bf16[256,4096]{1,0:T(8,128)(2,1)} %bitcast.26, bf16[256,4096]{1,0:T(8,128)(2,1)} %bitcast.28, bf16[64,2048]{1,0:T(8,128)(2,1)} %bitcast.31, bf16[64,2048]{1,0:T(8,128)(2,1)} %bitcast.32, bf16[64,2048]{1,0:T(8,128)(2,1)} %bitcast.33), custom_call_target="tpu_custom_call" | custom-call | bytes 7864320 | tf_op jit(solution)/shard_map/pack/pallas_call | solution.py:55
  20.8 0.0 copy-start.12
  20.8 0.0 copy-start.9
  20.8 64.2 %all-to-all-done.2.refs_0_.refs_1_.refs_2_ = bf16[8,768,256]{2,1,0:T(8,128)(2,1)} async-done(((bf16[8,768,256]{2,1,0:T(8,128)(2,1)}), bf16[8,768,256]{2,1,0:T(8,128)(2,1)}, u32[]{:S(2)}, u32[]{:S(2)}) %all-to-all-start.2) | async-done | bytes 3145760 | tf_op jit(solution)/shard_map/all_to_all | solution.py:508
  85.0 4.5 %all-to-all-start = ((bf16[8,960,256]{2,1,0:T(8,128)(2,1)}), bf16[8,960,256]{2,1,0:T(8,128)(2,1)}, u32[]{:S(2)}, u32[]{:S(2)}) async-start(bf16[8,960,256]{2,1,0:T(8,128)(2,1)} %pack.2), calls=%async_computation | async-start | bytes 7864320 | tf_op jit(solution)/shard_map/all_to_all | solution.py:508
  89.6 0.1 collective-permute-start.1
  89.7 2.8 collective-permute-start.12
  92.5 97.2 %all-to-all-done.refs_0_.refs_1_.refs_2_.refs_6_.refs_7_.refs_8_ = bf16[8,960,256]{2,1,0:T(8,128)(2,1)} async-done(((bf16[8,960,256]{2,1,0:T(8,128)(2,1)}), bf16[8,960,256]{2,1,0:T(8,128)(2,1)}, u32[]{:S(2)}, u32[]{:S(2)}) %all-to-all-start) | async-done | bytes 3932192 | tf_op jit(solution)/shard_map/all_to_all | solution.py:508
  189.7 0.0 collective-permute-start
  189.7 0.1 broadcast_in_dim.2
  189.8 0.0 copy-start.4
  189.8 0.1 collective-permute-start.2
  189.9 20.9 %collective-permute-done.2.b_ref = bf16[64,2176]{1,0:T(8,128)(2,1)S(1)} collective-permute-done((bf16[64,2176]{1,0:T(8,128)(2,1)S(1)}, bf16[64,2176]{1,0:T(8,128)(2,1)S(1)}, u32[]{:S(2)}, u32[]{:S(2)}) %collective-permute-start.2) | collective-permute-done | bytes 278560 | tf_op jit(solution)/shard_map/ppermute | solution.py:26
  210.8 0.7 copy-done.8
  211.5 1.9 stack_rows.4.a_ref
  213.4 0.8 copy-done.7
  214.2 2.2 stack_rows.6.a_ref
  216.5 2.0 collective-permute-start.13
  218.5 10.6 %collective-permute-done.3.b_ref = bf16[128,2176]{1,0:T(8,128)(2,1)S(1)} collective-permute-done((bf16[128,2176]{1,0:T(8,128)(2,1)}, bf16[128,2176]{1,0:T(8,128)(2,1)S(1)}, u32[]{:S(2)}, u32[]{:S(2)}) %collective-permute-start.3) | collective-permute-done | bytes 557088 | tf_op jit(solution)/shard_map/ppermute | solution.py:26
  229.1 0.8 copy-done.6
  229.9 2.3 stack_rows.5.refs_0_.refs_4_.refs_2_
  232.2 1.4 collective-permute-start.4
  234.3 14.4 %collective-permute-done.13.b_ref = bf16[128,4096]{1,0:T(8,128)(2,1)S(1)} collective-permute-done((bf16[128,4096]{1,0:T(8,128)(2,1)}, bf16[128,4096]{1,0:T(8,128)(2,1)S(1)}, u32[]{:S(2)}, u32[]{:S(2)}) %collective-permute-start.13) | collective-permute-done | bytes 1048608 | tf_op jit(solution)/shard_map/ppermute | solution.py:26
  248.8 1.0 copy-done.5
  249.8 3.0 stack_rows.7.refs_0_.refs_1_
  252.8 2.4 collective-permute-start.14
  255.2 0.9 dynamic-slice_convert_fusion
  256.0 0.6 constant_dynamic-slice_fusion
  256.6 0.0 collective-permute-start.5
  256.6 0.0 collective-permute-done.4.refs_1_.refs_5_
  256.6 0.5 collective-permute-start.6
  257.1 0.0 collective-permute-done.1.refs_3_.refs_4_
  257.1 26.0 %self_attention.3 = bf16[8,256,256]{2,1,0:T(8,128)(2,1)} custom-call(bf16[8,768,256]{2,1,0:T(8,128)(2,1)} %all-to-all-done.2.refs_0_.refs_1_.refs_2_, bf16[8,768,256]{2,1,0:T(8,128)(2,1)} %all-to-all-done.2.refs_0_.refs_1_.refs_2_, bf16[8,768,256]{2,1,0:T(8,128)(2,1)} %all-to-all-done.2.refs_0_.refs_1_.refs_2_, ...), custom_call_target="tpu_custom_call" | custom-call | flops 8589934592 | bytes 15728640 | tf_op jit(solution)/shard_map/self_attention/pallas_call | solution.py:212
  283.1 4.6 %all-to-all-start.3 = ((bf16[8,256,256]{2,1,0:T(8,128)(2,1)}), bf16[8,256,256]{2,1,0:T(8,128)(2,1)}, u32[]{:S(2)}, u32[]{:S(2)}) async-start(bf16[8,256,256]{2,1,0:T(8,128)(2,1)} %self_attention.3), calls=%async_computation.3 | async-start | bytes 2097152 | tf_op jit(solution)/shard_map/all_to_all | solution.py:508
  287.7 1.3 dynamic-slice_convert_fusion.3.refs_11_
  289.1 0.0 collective-permute-start.15
  289.1 0.0 collective-permute-done.5.refs_2_.refs_6_.refs_8_
  289.1 23.1 %audio_cross.1 = (bf16[256,2176]{1,0:T(8,128)(2,1)}, bf16[256,2176]{1,0:T(8,128)(2,1)}, bf16[256,2176]{1,0:T(8,128)(2,1)}, bf16[256,2176]{1,0:T(8,128)(2,1)}) custom-call(f32[32]{0:T(128)} %slope_ref.2, s32[1]{0:T(128)} %bitcast.9.place_ref, bf16[256,2048]{1,0:T(8,128)(2,1)} %bitcast.39, bf16[256,2048]{1,0:T(8,128)(2,1)} %bitcast.40, ...), custom_call_target="tpu_custom_call" | custom-call | flops 4294967296 | bytes 10485760 | tf_op jit(solution)/shard_map/audio_cross/pallas_call | solution.py:364
  312.1 0.5 collective-permute-start.8
  312.7 0.1 collective-permute-start.16
  312.8 29.5 %self_attention.2 = bf16[8,320,256]{2,1,0:T(8,128)(2,1)} custom-call(bf16[8,960,256]{2,1,0:T(8,128)(2,1)} %all-to-all-done.refs_0_.refs_1_.refs_2_.refs_6_.refs_7_.refs_8_, bf16[8,960,256]{2,1,0:T(8,128)(2,1)} %all-to-all-done.refs_0_.refs_1_.refs_2_.refs_6_.refs_7_.refs_8_, ...), custom_call_target="tpu_custom_call" | custom-call | flops 9663676416 | bytes 19660800 | tf_op jit(solution)/shard_map/self_attention/pallas_call | solution.py:212
  342.3 6.0 %all-to-all-start.1 = ((bf16[8,320,256]{2,1,0:T(8,128)(2,1)}), bf16[8,320,256]{2,1,0:T(8,128)(2,1)S(1)}, u32[]{:S(2)}, u32[]{:S(2)}) async-start(bf16[8,320,256]{2,1,0:T(8,128)(2,1)} %self_attention.2), calls=%async_computation.1 | async-start | bytes 2621440 | tf_op jit(solution)/shard_map/all_to_all | solution.py:508
  348.3 0.1 collective-permute-start.7
  348.5 0.0 collective-permute-done.8.b_ref
  348.5 3.7 merge.6
  352.1 1.9 collective-permute-start.9
  354.0 3.6 merge.5.a_ref
  357.6 31.7 %collective-permute-done.9.b_ref = bf16[256,2176]{1,0:T(8,128)(2,1)} collective-permute-done((bf16[256,2176]{1,0:T(8,128)(2,1)}, bf16[256,2176]{1,0:T(8,128)(2,1)}, u32[]{:S(2)}, u32[]{:S(2)}) %collective-permute-start.9) | collective-permute-done | bytes 1114144 | tf_op jit(solution)/shard_map/ppermute | solution.py:26
  389.3 3.6 merge.7
  392.8 1.5 collective-permute-start.10
  394.3 1.4 dynamic-slice_convert_fusion.2.refs_0_
  395.7 1.4 dynamic-slice_convert_fusion.1.refs_12_
  397.0 10.6 %collective-permute-done.10.b_ref = bf16[128,2176]{1,0:T(8,128)(2,1)} collective-permute-done((bf16[128,2176]{1,0:T(8,128)(2,1)}, bf16[128,2176]{1,0:T(8,128)(2,1)}, u32[]{:S(2)}, u32[]{:S(2)}) %collective-permute-start.10) | collective-permute-done | bytes 557088 | tf_op jit(solution)/shard_map/ppermute | solution.py:26
  407.6 2.6 merge.8
  410.2 2.5 collective-permute-start.11
  412.7 0.0 collective-permute-done.15.refs_6_.refs_7_
  412.7 0.0 collective-permute-done.16.refs_9_.refs_10_
  412.7 24.4 %video_cross.1 = bf16[256,2048]{1,0:T(8,128)(2,1)} custom-call(f32[32]{0:T(128)} %slope_ref.3, s32[1]{0:T(128)} %bitcast.9.place_ref, bf16[256,2048]{1,0:T(8,128)(2,1)} %bitcast.29, bf16[256,4096]{1,0:T(8,128)(2,1)} %stack_rows.7.refs_0_.refs_1_, bf16[256,4096]{1,0:T(8,128)(2,1)} %stack_rows.7.refs_0_.refs_1_, ...), custom_call_target="tpu_custom_call" | custom-call | flops 4294967296 | bytes 10485760 | tf_op jit(solution)/shard_map/video_cross/pallas_call | solution.py:279
  437.1 0.0 collective-permute-done.11.b_ref
  437.1 2.2 merge.9
  439.4 1.0 copy-done.1
  440.4 5.8 %unpack.1 = (bf16[256,4096]{1,0:T(8,128)(2,1)}, bf16[64,2048]{1,0:T(8,128)(2,1)}) custom-call(bf16[8,320,256]{2,1,0:T(8,128)(2,1)} %copy-done.1, bf16[8,256,256]{2,1,0:T(8,128)(2,1)} %all-to-all-done.3.refs_1_, bf16[8,320,256]{2,1,0:T(8,128)(2,1)} %copy-done.1), custom_call_target="tpu_custom_call" | custom-call | bytes 2621440 | tf_op jit(solution)/shard_map/unpack/pallas_call | solution.py:91
  (29 shorter events, 0.1 us)
Async XLA Ops:
  6.9 78.1 %all-to-all-start.2 = ((bf16[8,768,256]{2,1,0:T(8,128)(2,1)}), bf16[8,768,256]{2,1,0:T(8,128)(2,1)}, u32[]{:S(2)}, u32[]{:S(2)}) async-start(bf16[8,768,256]{2,1,0:T(8,128)(2,1)} %pack.3), calls=%async_computation.2 | async-start | bytes 6291456 | tf_op jit(solution)/shard_map/all_to_all | solution.py:508
  20.8 68.9 %copy-start.10 = (bf16[1,64,2048]{2,1,0:T(8,128)(2,1)S(1)}, bf16[1,64,2048]{2,1,0:T(8,128)(2,1)}, u32[]{:S(2)}) copy-start(bf16[1,64,2048]{2,1,0:T(8,128)(2,1)} %param.31) | copy-start | bytes 786436
  20.8 68.9 %copy-start.11 = (bf16[1,64,2048]{2,1,0:T(8,128)(2,1)S(1)}, bf16[1,64,2048]{2,1,0:T(8,128)(2,1)}, u32[]{:S(2)}) copy-start(bf16[1,64,2048]{2,1,0:T(8,128)(2,1)} %param.30) | copy-start | bytes 786436
  20.8 71.7 %copy-start.12 = (s32[1,64]{1,0:T(1,128)S(1)}, s32[1,64]{1,0:T(1,128)}, u32[]{:S(2)}) copy-start(s32[1,64]{1,0:T(1,128)} %param.32) | copy-start | bytes 772
  20.8 169.0 %copy-start.9 = (bf16[1,64,2048]{2,1,0:T(8,128)(2,1)S(1)}, bf16[1,64,2048]{2,1,0:T(8,128)(2,1)}, u32[]{:S(2)}) copy-start(bf16[1,64,2048]{2,1,0:T(8,128)(2,1)} %param.26) | copy-start | bytes 786436
  85.0 104.7 %all-to-all-start = ((bf16[8,960,256]{2,1,0:T(8,128)(2,1)}), bf16[8,960,256]{2,1,0:T(8,128)(2,1)}, u32[]{:S(2)}, u32[]{:S(2)}) async-start(bf16[8,960,256]{2,1,0:T(8,128)(2,1)} %pack.2), calls=%async_computation | async-start | bytes 7864320 | tf_op jit(solution)/shard_map/all_to_all | solution.py:508
  89.6 167.6 %collective-permute-start.1 = (bf16[8,768,256]{2,1,0:T(8,128)(2,1)}, bf16[8,768,256]{2,1,0:T(8,128)(2,1)}, u32[]{:S(2)}, u32[]{:S(2)}) collective-permute-start(bf16[8,768,256]{2,1,0:T(8,128)(2,1)} %all-to-all-done.2.refs_0_.refs_1_.refs_2_), channel_id=1, source_target_pairs={{0,1},{1,0},{2,3},{3,2},{4,5},{5,4},{6,7},{7,6},{8,9},{9,8},{10,11... | collective-permute-start | bytes 9437192 | tf_op jit(solution)/shard_map/ppermute | solution.py:26
  89.7 123.7 %copy-start.3 = (bf16[64,4096]{1,0:T(8,128)(2,1)}, bf16[64,4096]{1,0:T(8,128)(2,1)S(1)}, u32[]{:S(2)}) copy-start(bf16[64,4096]{1,0:T(8,128)(2,1)S(1)} %pad_maximum_fusion.a_ref) | copy-start | bytes 1572868
  89.7 123.7 %collective-permute-start.12 = (bf16[64,4096]{1,0:T(8,128)(2,1)S(1)}, bf16[64,4096]{1,0:T(8,128)(2,1)S(1)}, u32[]{:S(2)}, u32[]{:S(2)}) collective-permute-start(bf16[64,4096]{1,0:T(8,128)(2,1)S(1)} %pad_maximum_fusion.a_ref), channel_id=1, source_target_pairs={{0,8},{2,10},{4,12},{6,14},{8,0},{10,2},{12,4},{14,6},{1,9},{3,11}... | collective-permute-start | bytes 1572872 | tf_op jit(solution)/shard_map/ppermute | solution.py:26
  189.7 123.0 %collective-permute-start = (bf16[8,960,256]{2,1,0:T(8,128)(2,1)}, bf16[8,960,256]{2,1,0:T(8,128)(2,1)}, u32[]{:S(2)}, u32[]{:S(2)}) collective-permute-start(bf16[8,960,256]{2,1,0:T(8,128)(2,1)} %all-to-all-done.refs_0_.refs_1_.refs_2_.refs_6_.refs_7_.refs_8_), channel_id=1, source_target_pairs={{0,1},{1,0},{2,3},{3,2},{4,5},{5,4},{6,7},{7,6},{8,9},{9,8},{10,11... | collective-permute-start | bytes 11796488 | tf_op jit(solution)/shard_map/ppermute | solution.py:26
  189.8 21.0 %copy-start.4 = (bf16[64,2176]{1,0:T(8,128)(2,1)}, bf16[64,2176]{1,0:T(8,128)(2,1)S(1)}, u32[]{:S(2)}) copy-start(bf16[64,2176]{1,0:T(8,128)(2,1)S(1)} %pad_maximum_fusion.1.a_ref) | copy-start | bytes 835588
  189.8 21.0 %collective-permute-start.2 = (bf16[64,2176]{1,0:T(8,128)(2,1)S(1)}, bf16[64,2176]{1,0:T(8,128)(2,1)S(1)}, u32[]{:S(2)}, u32[]{:S(2)}) collective-permute-start(bf16[64,2176]{1,0:T(8,128)(2,1)S(1)} %pad_maximum_fusion.1.a_ref), channel_id=1, source_target_pairs={{0,8},{2,10},{4,12},{6,14},{8,0},{10,2},{12,4},{14,6},{1,9},{3,11}... | collective-permute-start | bytes 835592 | tf_op jit(solution)/shard_map/ppermute | solution.py:26
  210.8 0.7 copy-start.8
  213.4 15.7 %collective-permute-start.3 = (bf16[128,2176]{1,0:T(8,128)(2,1)}, bf16[128,2176]{1,0:T(8,128)(2,1)S(1)}, u32[]{:S(2)}, u32[]{:S(2)}) collective-permute-start(bf16[128,2176]{1,0:T(8,128)(2,1)} %stack_rows.4.a_ref), channel_id=1, source_target_pairs={{0,4},{2,6},{4,0},{6,2},{8,12},{10,14},{12,8},{14,10},{1,5},{3,7},... | collective-permute-start | bytes 1671176 | tf_op jit(solution)/shard_map/ppermute | solution.py:26
  213.4 0.8 copy-start.7
  216.5 32.3 %collective-permute-start.13 = (bf16[128,4096]{1,0:T(8,128)(2,1)}, bf16[128,4096]{1,0:T(8,128)(2,1)S(1)}, u32[]{:S(2)}, u32[]{:S(2)}) collective-permute-start(bf16[128,4096]{1,0:T(8,128)(2,1)} %stack_rows.6.a_ref), channel_id=1, source_target_pairs={{0,4},{2,6},{4,0},{6,2},{8,12},{10,14},{12,8},{14,10},{1,5},{3,7},... | collective-permute-start | bytes 3145736 | tf_op jit(solution)/shard_map/ppermute | solution.py:26
  229.1 0.8 copy-start.6
  232.2 24.4 %collective-permute-start.4 = (bf16[256,2176]{1,0:T(8,128)(2,1)}, bf16[256,2176]{1,0:T(8,128)(2,1)}, u32[]{:S(2)}, u32[]{:S(2)}) collective-permute-start(bf16[256,2176]{1,0:T(8,128)(2,1)} %stack_rows.5.refs_0_.refs_4_.refs_2_), channel_id=1, source_target_pairs={{0,2},{2,0},{4,6},{6,4},{8,10},{10,8},{12,14},{14,12},{1,3},{3,1},... | collective-permute-start | bytes 3342344 | tf_op jit(solution)/shard_map/ppermute | solution.py:26
  234.3 22.3 %copy-start.2 = (bf16[256,2176]{1,0:T(8,128)(2,1)S(1)}, bf16[256,2176]{1,0:T(8,128)(2,1)}, u32[]{:S(2)}) copy-start(bf16[256,2176]{1,0:T(8,128)(2,1)} %stack_rows.5.refs_0_.refs_4_.refs_2_) | copy-start | bytes 3342340
  248.8 1.0 copy-start.5
  252.8 59.9 %collective-permute-start.14 = (bf16[256,4096]{1,0:T(8,128)(2,1)}, bf16[256,4096]{1,0:T(8,128)(2,1)}, u32[]{:S(2)}, u32[]{:S(2)}) collective-permute-start(bf16[256,4096]{1,0:T(8,128)(2,1)} %stack_rows.7.refs_0_.refs_1_), channel_id=1, source_target_pairs={{0,2},{2,0},{4,6},{6,4},{8,10},{10,8},{12,14},{14,12},{1,3},{3,1},... | collective-permute-start | bytes 6291464 | tf_op jit(solution)/shard_map/ppermute | solution.py:26
  256.6 32.5 %collective-permute-start.5 = (bf16[256,2176]{1,0:T(8,128)(2,1)S(1)}, bf16[256,2176]{1,0:T(8,128)(2,1)}, u32[]{:S(2)}, u32[]{:S(2)}) collective-permute-start(bf16[256,2176]{1,0:T(8,128)(2,1)S(1)} %copy-done.2), channel_id=1, source_target_pairs={{0,1},{1,0},{2,3},{3,2},{4,5},{5,4},{6,7},{7,6},{8,9},{9,8},{10,11... | collective-permute-start | bytes 3342344 | tf_op jit(solution)/shard_map/ppermute | solution.py:26
  256.6 32.5 %collective-permute-start.6 = (bf16[256,2176]{1,0:T(8,128)(2,1)}, bf16[256,2176]{1,0:T(8,128)(2,1)}, u32[]{:S(2)}, u32[]{:S(2)}) collective-permute-start(bf16[256,2176]{1,0:T(8,128)(2,1)} %collective-permute-done.4.refs_1_.refs_5_), channel_id=1, source_target_pairs={{0,1},{1,0},{2,3},{3,2},{4,5},{5,4},{6,7},{7,6},{8,9},{9,8},{10,11... | collective-permute-start | bytes 3342344 | tf_op jit(solution)/shard_map/ppermute | solution.py:26
  283.1 5.9 %copy-start = (bf16[256,4096]{1,0:T(8,128)(2,1)S(1)}, bf16[256,4096]{1,0:T(8,128)(2,1)}, u32[]{:S(2)}) copy-start(bf16[256,4096]{1,0:T(8,128)(2,1)} %stack_rows.7.refs_0_.refs_1_) | copy-start | bytes 6291460
  283.1 59.1 %all-to-all-start.3 = ((bf16[8,256,256]{2,1,0:T(8,128)(2,1)}), bf16[8,256,256]{2,1,0:T(8,128)(2,1)}, u32[]{:S(2)}, u32[]{:S(2)}) async-start(bf16[8,256,256]{2,1,0:T(8,128)(2,1)} %self_attention.3), calls=%async_computation.3 | async-start | bytes 2097152 | tf_op jit(solution)/shard_map/all_to_all | solution.py:508
  289.1 123.6 %collective-permute-start.15 = (bf16[256,4096]{1,0:T(8,128)(2,1)S(1)}, bf16[256,4096]{1,0:T(8,128)(2,1)}, u32[]{:S(2)}, u32[]{:S(2)}) collective-permute-start(bf16[256,4096]{1,0:T(8,128)(2,1)S(1)} %copy-done), channel_id=1, source_target_pairs={{0,1},{1,0},{2,3},{3,2},{4,5},{5,4},{6,7},{7,6},{8,9},{9,8},{10,11... | collective-permute-start | bytes 6291464 | tf_op jit(solution)/shard_map/ppermute | solution.py:26
  312.1 36.3 %collective-permute-start.8 = (bf16[256,2176]{1,0:T(8,128)(2,1)}, bf16[256,2176]{1,0:T(8,128)(2,1)}, u32[]{:S(2)}, u32[]{:S(2)}) collective-permute-start(bf16[256,2176]{1,0:T(8,128)(2,1)} %get-tuple-element.19), channel_id=1, source_target_pairs={{0,1},{1,0},{2,3},{3,2},{4,5},{5,4},{6,7},{7,6},{8,9},{9,8},{10,11... | collective-permute-start | bytes 3342344 | tf_op jit(solution)/shard_map/ppermute | solution.py:26
  312.7 100.0 %collective-permute-start.16 = (bf16[256,4096]{1,0:T(8,128)(2,1)}, bf16[256,4096]{1,0:T(8,128)(2,1)}, u32[]{:S(2)}, u32[]{:S(2)}) collective-permute-start(bf16[256,4096]{1,0:T(8,128)(2,1)} %collective-permute-done.14.refs_3_.refs_4_), channel_id=1, source_target_pairs={{0,1},{1,0},{2,3},{3,2},{4,5},{5,4},{6,7},{7,6},{8,9},{9,8},{10,11... | collective-permute-start | bytes 6291464 | tf_op jit(solution)/shard_map/ppermute | solution.py:26
  342.3 97.1 %all-to-all-start.1 = ((bf16[8,320,256]{2,1,0:T(8,128)(2,1)}), bf16[8,320,256]{2,1,0:T(8,128)(2,1)S(1)}, u32[]{:S(2)}, u32[]{:S(2)}) async-start(bf16[8,320,256]{2,1,0:T(8,128)(2,1)} %self_attention.2), calls=%async_computation.1 | async-start | bytes 2621440 | tf_op jit(solution)/shard_map/all_to_all | solution.py:508
  348.3 5.7 %collective-permute-start.7 = (bf16[256,2176]{1,0:T(8,128)(2,1)}, bf16[256,2176]{1,0:T(8,128)(2,1)}, u32[]{:S(2)}, u32[]{:S(2)}) collective-permute-start(bf16[256,2176]{1,0:T(8,128)(2,1)} %get-tuple-element.17), channel_id=1, source_target_pairs={{0,1},{1,0},{2,3},{3,2},{4,5},{5,4},{6,7},{7,6},{8,9},{9,8},{10,11... | collective-permute-start | bytes 3342344 | tf_op jit(solution)/shard_map/ppermute | solution.py:26
  352.1 37.2 %collective-permute-start.9 = (bf16[256,2176]{1,0:T(8,128)(2,1)}, bf16[256,2176]{1,0:T(8,128)(2,1)}, u32[]{:S(2)}, u32[]{:S(2)}) collective-permute-start(bf16[256,2176]{1,0:T(8,128)(2,1)} %merge.6), channel_id=1, source_target_pairs={{0,2},{2,0},{4,6},{6,4},{8,10},{10,8},{12,14},{14,12},{1,3},{3,1},... | collective-permute-start | bytes 3342344 | tf_op jit(solution)/shard_map/ppermute | solution.py:26
  392.8 14.8 %collective-permute-start.10 = (bf16[128,2176]{1,0:T(8,128)(2,1)}, bf16[128,2176]{1,0:T(8,128)(2,1)}, u32[]{:S(2)}, u32[]{:S(2)}) collective-permute-start(bf16[128,2176]{1,0:T(8,128)(2,1)} %get-tuple-element.21), channel_id=1, source_target_pairs={{0,4},{2,6},{4,0},{6,2},{8,12},{10,14},{12,8},{14,10},{1,5},{3,7},... | collective-permute-start | bytes 1671176 | tf_op jit(solution)/shard_map/ppermute | solution.py:26
  410.2 26.9 %collective-permute-start.11 = (bf16[64,2176]{1,0:T(8,128)(2,1)}, bf16[64,2176]{1,0:T(8,128)(2,1)}, u32[]{:S(2)}, u32[]{:S(2)}) collective-permute-start(bf16[64,2176]{1,0:T(8,128)(2,1)} %get-tuple-element.23), channel_id=1, source_target_pairs={{0,8},{2,10},{4,12},{6,14},{8,0},{10,2},{12,4},{14,6},{1,9},{3,11}... | collective-permute-start | bytes 835592 | tf_op jit(solution)/shard_map/ppermute | solution.py:26
  439.4 1.1 copy-start.1

commit v3 on v2

--- a/solution.py
+++ b/solution.py
@@ -15,6 +15,7 @@
 LANES = 128
 LOG2E = 1.4426950408889634
 VIDEO_PARTS = 2
+WIDE = 512
 
 
 BF16 = jnp.bfloat16
@@ -77,12 +78,16 @@
             outs.append(jnp.stack(cut, axis=2).reshape(r, tok_count * len(entry) * w))
         return outs
 
+    each = math.gcd(tok_count, 2)
+
     def body(*refs):
         at = 0
         for e, (w, count) in enumerate(zip(wides, parts)):
             out = refs[sum(parts) + e]
             for p in range(count):
-                out[:, p * w : (p + 1) * w] = refs[at][0]
+                for m in range(each):
+                    here = (m * count + p) * w
+                    out[:, here : here + w] = refs[at][m]
                 at += 1
 
     flat = [(array, at, r) for entry, r in zip(sources, rows) for array, at in entry]
@@ -90,17 +95,17 @@
         assert at % r == 0
     return pl.pallas_call(
         body,
-        grid=(tok_count,),
+        grid=(tok_count // each,),
         out_shape=[
             jax.ShapeDtypeStruct((r, tok_count * w * count), BF16)
             for r, w, count in zip(rows, wides, parts)
         ],
         in_specs=[
-            pl.BlockSpec((1, r, array.shape[2]), lambda m, k=at // r: (m, k, 0))
+            pl.BlockSpec((each, r, array.shape[2]), lambda m, k=at // r: (m, k, 0))
             for array, at, r in flat
         ],
         out_specs=[
-            pl.BlockSpec((r, w * count), lambda m: (0, m))
+            pl.BlockSpec((r, each * w * count), lambda m: (0, m))
             for r, w, count in zip(rows, wides, parts)
         ],
         cost_estimate=cost(0, 0, 4 * sum(r * w for r, w in zip(rows, wides)) * tok_count),
@@ -108,19 +113,20 @@
     )(*[array for array, _, _ in flat])
 
 
-def stack_rows(first, second):
-    rows, wide = first.shape
-
-    def body(a_ref, b_ref, out_ref):
-        out_ref[:rows] = a_ref[...]
-        out_ref[rows:] = b_ref[...]
+def stack_rows(*arrays):
+    rows, wide = arrays[0].shape
+    count = len(arrays)
+
+    def body(*refs):
+        for m in range(count):
+            refs[count][m * rows : (m + 1) * rows] = refs[m][...]
 
     return pl.pallas_call(
         body,
-        out_shape=jax.ShapeDtypeStruct((2 * rows, wide), BF16),
-        cost_estimate=cost(0, 0, 8 * rows * wide),
+        out_shape=jax.ShapeDtypeStruct((count * rows, wide), BF16),
+        cost_estimate=cost(0, 0, 4 * count * rows * wide),
         name="stack_rows",
-    )(first, second)
+    )(*arrays)
 
 
 def lane_of(shape):
@@ -224,58 +230,70 @@
     counted, columns = queries.shape
     keyed = pieces[0].shape[0]
     n = len(pieces)
-    steps = columns // LANES
+    block = WIDE if columns % WIDE == 0 else LANES
+    steps = columns // block
     heads = LANES // DHA
     factor = LOG2E / math.sqrt(DHA)
 
     def body(slope_ref, place_ref, q_ref, *refs):
         gate_ref, out_ref = refs[3 * n :]
         i = pl.program_id(0)
-        q = q_ref[...]
         at = place_ref[0]
         if span % counted == 0:
             mine = (at // span).astype(F32)
         else:
             col = lax.broadcasted_iota(jnp.int32, (1, counted), 1)
             mine = ((at + col) // span).astype(F32)
-        gaps, turned = [], []
+        gaps = []
         for p in range(n):
             frame = refs[3 * p + 2][...].astype(F32)
-            if counted > LANES:
+            if span % counted != 0 and counted > LANES:
                 frame = jnp.concatenate([frame] * (counted // LANES), axis=1)
-            gaps.append(jnp.abs(frame[:, :counted] - mine))
-            turned.append(jnp.transpose(refs[3 * p + 1][...]))
-        results = []
-        for head in range(heads):
-            slope = slope_ref[i * heads + head] * LOG2E
-            scores = [
-                nt(pick(LANES, DHA, refs[3 * p][...], head), q) * factor - gaps[p] * slope
-                for p in range(n)
-            ]
-            top = jnp.max(scores[0], axis=0, keepdims=True)
-            for one in scores[1:]:
-                top = jnp.maximum(top, jnp.max(one, axis=0, keepdims=True))
-            total = summed = None
-            for p in range(n):
-                exps = jnp.exp2(scores[p] - top)
-                sums = jnp.sum(exps, axis=0, keepdims=True)
-                part = jnp.dot(
-                    turned[p][head * DHA : (head + 1) * DHA],
-                    exps.astype(BF16),
-                    preferred_element_type=F32,
-                )
-                total = sums if total is None else total + sums
-                summed = part if summed is None else summed + part
-            results.append(summed / total)
-        result = jnp.transpose(jnp.concatenate(results, axis=0))
-        out_ref[...] = (result * gate_ref[...]).astype(BF16)
-
-    piece = [
-        pl.BlockSpec((keyed, LANES), lambda i: (0, i)),
-        pl.BlockSpec((keyed, LANES), lambda i: (0, steps + i)),
-        pl.BlockSpec((keyed, LANES), lambda i: (0, steps)),
-    ]
-    scores = counted * keyed * n * steps * heads
+            if counted < LANES:
+                frame = frame[:, :counted]
+            gaps.append(jnp.abs(frame - mine))
+        for j in range(block // LANES):
+            here = slice(j * LANES, (j + 1) * LANES)
+            q = q_ref[:, here]
+            turned = [jnp.transpose(refs[3 * p + 1][:, here]) for p in range(n)]
+            results = []
+            for head in range(heads):
+                slope = slope_ref[(i * (block // LANES) + j) * heads + head] * LOG2E
+                scores = []
+                for p in range(n):
+                    bias = gaps[p] * slope
+                    if bias.shape[1] < counted:
+                        bias = jnp.concatenate([bias] * (counted // LANES), axis=1)
+                    keys = pick(LANES, DHA, refs[3 * p][:, here], head)
+                    scores.append(nt(keys, q) * factor - bias)
+                top = jnp.max(scores[0], axis=0, keepdims=True)
+                for one in scores[1:]:
+                    top = jnp.maximum(top, jnp.max(one, axis=0, keepdims=True))
+                total = summed = None
+                for p in range(n):
+                    exps = jnp.exp2(scores[p] - top)
+                    sums = jnp.sum(exps, axis=0, keepdims=True)
+                    part = jnp.dot(
+                        turned[p][head * DHA : (head + 1) * DHA],
+                        exps.astype(BF16),
+                        preferred_element_type=F32,
+                    )
+                    total = sums if total is None else total + sums
+                    summed = part if summed is None else summed + part
+                results.append(summed * (1.0 / total))
+            result = jnp.transpose(jnp.concatenate(results, axis=0))
+            out_ref[:, here] = (result * gate_ref[:, here]).astype(BF16)
+
+    each = marks[0].shape[0] // keyed
+    pairs = [pl.BlockSpec((keyed, block), lambda i, k=k: (0, k * steps + i)) for k in (0, 1)]
+    specs, operands = [], []
+    for p in range(n):
+        specs += pairs
+        specs.append(
+            pl.BlockSpec((keyed, LANES), lambda i, r=p % each: (r, columns // LANES))
+        )
+        operands += [pieces[p], pieces[p], marks[p // each]]
+    scores = counted * keyed * n * columns // DHA
     return pl.pallas_call(
         body,
         grid=(steps,),
@@ -283,14 +301,14 @@
         in_specs=[
             pl.BlockSpec(memory_space=pltpu.SMEM),
             pl.BlockSpec(memory_space=pltpu.SMEM),
-            pl.BlockSpec((counted, LANES), lambda i: (0, i)),
+            pl.BlockSpec((counted, block), lambda i: (0, i)),
         ]
-        + piece * n
-        + [pl.BlockSpec((1, LANES), lambda i: (0, i))],
-        out_specs=pl.BlockSpec((counted, LANES), lambda i: (0, i)),
+        + specs
+        + [pl.BlockSpec((1, block), lambda i: (0, i))],
+        out_specs=pl.BlockSpec((counted, block), lambda i: (0, i)),
         cost_estimate=cost(scores * 4 * LANES, scores, 4 * columns * (counted + n * keyed)),
         name="video_cross",
-    )(slopes, place, queries, *[a for k, f in zip(pieces, marks) for a in (k, k, f)], gate)
+    )(slopes, place, queries, *operands, gate)
 
 
 def audio_cross_local(pieces, keys, values, slopes, place, span):
@@ -441,10 +459,8 @@
 
     if form == "halves":
         shapes = [jax.ShapeDtypeStruct((half, wide), BF16)] * 2
-    elif form == "last":
+    else:
         shapes = jax.ShapeDtypeStruct((rows, columns), BF16)
-    else:
-        shapes = jax.ShapeDtypeStruct((rows, wide), BF16)
     extra = () if gate is None else (gate,)
     return pl.pallas_call(
         body,
@@ -504,6 +520,15 @@
                 own = stack_rows(own, received)
         return [own, received, swap(own, "head", 1), swap(received, "head", 1)]
 
+    def collect_soon(own):
+        for mask in masks[:-2]:
+            received = swap(own, "tok", mask)
+            own = stack_rows(own, received)
+        ends = masks[-2:] + ([3] if len(masks) > 1 else [])
+        received = [swap(own, "tok", mask) for mask in ends]
+        own = stack_rows(own, *received)
+        return [own, swap(own, "head", 1)]
+
     def across(blocks):
         return lax.all_to_all(blocks, "tok", split_axis=0, concat_axis=0, tiled=True)
 
@@ -524,14 +549,13 @@
         frames = jnp.broadcast_to(
             audio_frames[s][:, None].astype(F32), (audio_rows, LANES)
         ).astype(BF16)
-        asked = collect(jnp.concatenate((cross_audio_query[s], frames), axis=1))
+        asked = collect_soon(jnp.concatenate((cross_audio_query[s], frames), axis=1))
         kept = collect(jnp.concatenate((cross_audio_key[s], cross_audio_value[s]), axis=1))
         partial = audio_cross_local(
             asked, cross_video_key[s], cross_video_value[s], into_audio_slope, place, patches
         )
-        got = [swap(partial[2], "head", 1), swap(partial[3], "head", 1)]
-        mine = merge(partial[0], got[0], "whole")
-        send = merge(partial[1], got[1], "whole")
+        received = swap(partial[1], "head", 1)
+        mine, send = merge(partial[0], received, "halves")
         for step, mask in enumerate(reversed(masks)):
             received = swap(send, "tok", mask)
             if step < len(masks) - 1:

time: 448 us -> 467 us (1.042)
  waiting for transfers between devices: 250 us -> 274 us
  Pallas kernels: 147 us -> 139 us
    ppermute x17 -> x16, waiting for transfers between devices: 88.2 us -> 210 us  [swap(): return lax.ppermute(value, axis, [(j, j ^ mask) for j in range(count)])]
    all_to_all x4, waiting for transfers between devices: 161 us -> 64.2 us  [across(): lax.all_to_all(blocks, 'tok', split_axis=0, concat_axis=0, tiled=True)]
    pallas_call x5 -> x4, Pallas kernels: 15.7 us -> 13.8 us  [merge(): pl.pallas_call(body, out_shape=shapes, cost_estimate=cost(0, rows * wide,...]
    ppermute x17 -> x16, starting transfers between devices: 15.9 us -> 16.9 us  [swap(): return lax.ppermute(value, axis, [(j, j ^ mask) for j in range(count)])]
  transfers between devices with their start and end apart: 21 -> 20, of which waited for: 7 -> 9; matrix products, arithmetic and copies ran while one was open for 1% -> 1% of each run, Pallas kernels for 30% -> 28%
where the time goes in v3:
time: 467 us; the launch traced here: 466 us
  waiting for transfers between devices  274 us (59%)
  Pallas kernels  139 us (30%)
  starting transfers between devices  39.2 us (8%)
  local copies, waits for them, and re-layouts  7.46 us (2%)
  other arithmetic  4.97 us (1%)
    ppermute x16, waiting for transfers between devices, swap(): return lax.ppermute(value, axis, [(j, j ^ mask) for j in range(count)])  210 us
    all_to_all x4, waiting for transfers between devices, across(): lax.all_to_all(blocks, 'tok', split_axis=0, concat_axis=0, tiled=True)  64.2 us
    pallas_call x2, Pallas kernels, self_attention(): pl.pallas_call(body, grid=(columns // lanes,), out_shape=jax.ShapeDtypeSt...  55.6 us
    pallas_call x1, Pallas kernels, audio_cross_local(): pl.pallas_call(body, grid=(steps + 1,), out_shape=[jax.ShapeDtypeStruct((...  22.7 us
    all_to_all x4, starting transfers between devices, across(): lax.all_to_all(blocks, 'tok', split_axis=0, concat_axis=0, tiled=True)  22.3 us
    pallas_call x1, Pallas kernels, video_cross_local(): pl.pallas_call(body, grid=(steps,), out_shape=jax.ShapeDtypeStruct((count...  19.9 us
    ppermute x16, starting transfers between devices, swap(): return lax.ppermute(value, axis, [(j, j ^ mask) for j in range(count)])  16.9 us
    pallas_call x4, Pallas kernels, merge(): pl.pallas_call(body, out_shape=shapes, cost_estimate=cost(0, rows * wide,...  13.8 us
  transfers between devices with their start and end apart: 20, of which 9 were waited for; matrix products, arithmetic and copies ran while one was open for 1% of the time, Pallas kernels for 28%

profile of v3, /device:TPU:0, one launch (start us, length us, event | category | flops | bytes accessed | tf_op | source)
XLA Modules:
  0.0 466.3 jit_solution(7301359878476563781)
XLA Ops:
  0.6 6.3 %pack.3 = bf16[8,768,256]{2,1,0:T(8,128)(2,1)} custom-call(bf16[256,4096]{1,0:T(8,128)(2,1)} %bitcast.23, bf16[256,4096]{1,0:T(8,128)(2,1)} %bitcast.25, bf16[256,4096]{1,0:T(8,128)(2,1)} %bitcast.27), custom_call_target="tpu_custom_call" | custom-call | bytes 6291456 | tf_op jit(solution)/shard_map/pack/pallas_call | solution.py:56
  6.9 7.3 %all-to-all-start.2 = ((bf16[8,768,256]{2,1,0:T(8,128)(2,1)}), bf16[8,768,256]{2,1,0:T(8,128)(2,1)}, u32[]{:S(2)}, u32[]{:S(2)}) async-start(bf16[8,768,256]{2,1,0:T(8,128)(2,1)} %pack.3), calls=%async_computation.2 | async-start | bytes 6291456 | tf_op jit(solution)/shard_map/all_to_all | solution.py:533
  14.2 6.6 %pack.2 = bf16[8,960,256]{2,1,0:T(8,128)(2,1)} custom-call(bf16[256,4096]{1,0:T(8,128)(2,1)} %bitcast.24, bf16[256,4096]{1,0:T(8,128)(2,1)} %bitcast.26, bf16[256,4096]{1,0:T(8,128)(2,1)} %bitcast.28, bf16[64,2048]{1,0:T(8,128)(2,1)} %bitcast.31, bf16[64,2048]{1,0:T(8,128)(2,1)} %bitcast.32, bf16[64,2048]{1,0:T(8,128)(2,1)} %bitcast.33), custom_call_target="tpu_custom_call" | custom-call | bytes 7864320 | tf_op jit(solution)/shard_map/pack/pallas_call | solution.py:56
  20.8 64.2 %all-to-all-done.2.refs_0_.refs_1_.refs_2_ = bf16[8,768,256]{2,1,0:T(8,128)(2,1)} async-done(((bf16[8,768,256]{2,1,0:T(8,128)(2,1)}), bf16[8,768,256]{2,1,0:T(8,128)(2,1)}, u32[]{:S(2)}, u32[]{:S(2)}) %all-to-all-start.2) | async-done | bytes 3145760 | tf_op jit(solution)/shard_map/all_to_all | solution.py:533
  85.0 4.5 all-to-all-start
  89.5 0.1 broadcast_in_dim.2
  89.7 0.0 copy-start.5
  89.7 2.9 collective-permute-start.2
  92.5 95.8 %collective-permute-done.2.refs_1_ = bf16[64,2176]{1,0:T(8,128)(2,1)S(1)} collective-permute-done((bf16[64,2176]{1,0:T(8,128)(2,1)S(1)}, bf16[64,2176]{1,0:T(8,128)(2,1)S(1)}, u32[]{:S(2)}, u32[]{:S(2)}) %collective-permute-start.2) | collective-permute-done | bytes 278560 | tf_op jit(solution)/shard_map/ppermute | solution.py:27
  188.3 0.7 copy-done.11
  189.0 1.9 stack_rows.4.refs_0_
  190.9 0.0 collective-permute-start.5
  190.9 1.5 collective-permute-start.4
  192.5 2.0 collective-permute-start.3
  194.4 0.0 collective-permute-start.1
  194.4 13.1 %collective-permute-done.5.refs_3_ = bf16[128,2176]{1,0:T(8,128)(2,1)S(1)} collective-permute-done((bf16[128,2176]{1,0:T(8,128)(2,1)}, bf16[128,2176]{1,0:T(8,128)(2,1)S(1)}, u32[]{:S(2)}, u32[]{:S(2)}) %collective-permute-start.5) | collective-permute-done | bytes 557088 | tf_op jit(solution)/shard_map/ppermute | solution.py:27
  207.5 9.1 %collective-permute-done.4.refs_2_ = bf16[128,2176]{1,0:T(8,128)(2,1)S(1)} collective-permute-done((bf16[128,2176]{1,0:T(8,128)(2,1)}, bf16[128,2176]{1,0:T(8,128)(2,1)S(1)}, u32[]{:S(2)}, u32[]{:S(2)}) %collective-permute-start.4) | collective-permute-done | bytes 557088 | tf_op jit(solution)/shard_map/ppermute | solution.py:27
  216.7 1.0 collective-permute-done.3.refs_1_
  217.7 0.8 copy-done.9
  218.5 3.1 stack_rows.5.refs_0_.refs_2_.refs_5_
  221.5 0.0 collective-permute-start.6
  221.5 0.5 collective-permute-start
  222.1 0.0 copy-start.4
  222.1 2.0 collective-permute-start.11
  224.1 24.1 %collective-permute-done.11.refs_1_ = bf16[64,4096]{1,0:T(8,128)(2,1)S(1)} collective-permute-done((bf16[64,4096]{1,0:T(8,128)(2,1)S(1)}, bf16[64,4096]{1,0:T(8,128)(2,1)S(1)}, u32[]{:S(2)}, u32[]{:S(2)}) %collective-permute-start.11) | collective-permute-done | bytes 524320 | tf_op jit(solution)/shard_map/ppermute | solution.py:27
  248.2 0.8 copy-done.10
  249.0 2.2 stack_rows.6.refs_0_
  251.2 0.0 collective-permute-start.12
  251.9 0.9 dynamic-slice_convert_fusion
  252.8 0.6 constant_dynamic-slice_fusion
  253.4 22.6 %collective-permute-done.12.refs_1_ = bf16[128,4096]{1,0:T(8,128)(2,1)S(1)} collective-permute-done((bf16[128,4096]{1,0:T(8,128)(2,1)}, bf16[128,4096]{1,0:T(8,128)(2,1)S(1)}, u32[]{:S(2)}, u32[]{:S(2)}) %collective-permute-start.12) | collective-permute-done | bytes 1048608 | tf_op jit(solution)/shard_map/ppermute | solution.py:27
  276.0 1.0 copy-done.6
  277.0 3.0 stack_rows.7.refs_0_.refs_1_
  280.0 1.8 collective-permute-start.13
  281.7 0.0 collective-permute-done.6.refs_1_.refs_3_.refs_8_.refs_11_
  281.7 1.4 copy-done.2
  283.1 22.7 %audio_cross.1 = (bf16[512,2176]{1,0:T(8,128)(2,1)}, bf16[512,2176]{1,0:T(8,128)(2,1)}) custom-call(f32[32]{0:T(128)} %slope_ref.2, s32[1]{0:T(128)} %bitcast.9.place_ref, bf16[256,2048]{1,0:T(8,128)(2,1)} %bitcast.39, bf16[256,2048]{1,0:T(8,128)(2,1)} %bitcast.40, bf16[512,2176]{1,0:T(8,128)(2,1)} %stack_rows.5.refs_0_.refs_2_.refs_5_, ...), custom_call_target="tpu_custom_call" | custom-call | flops 4294967296 | bytes 10485760 | tf_op jit(solution)/shard_map/audio_cross/pallas_call | solution.py:382
  305.8 26.0 %self_attention.3 = bf16[8,256,256]{2,1,0:T(8,128)(2,1)} custom-call(bf16[8,768,256]{2,1,0:T(8,128)(2,1)} %all-to-all-done.2.refs_0_.refs_1_.refs_2_, bf16[8,768,256]{2,1,0:T(8,128)(2,1)} %all-to-all-done.2.refs_0_.refs_1_.refs_2_, bf16[8,768,256]{2,1,0:T(8,128)(2,1)} %all-to-all-done.2.refs_0_.refs_1_.refs_2_, ...), custom_call_target="tpu_custom_call" | custom-call | flops 8589934592 | bytes 15728640 | tf_op jit(solution)/shard_map/self_attention/pallas_call | solution.py:218
  331.8 4.5 all-to-all-start.3
  336.4 1.3 dynamic-slice_convert_fusion.3.refs_11_
  337.7 0.2 collective-permute-start.14
  337.9 0.0 collective-permute-done.13.refs_3_.refs_4_
  337.9 0.3 collective-permute-start.15
  338.2 0.0 collective-permute-done.refs_3_.refs_4_.refs_9_.refs_10_
  338.2 29.5 %self_attention.2 = bf16[8,320,256]{2,1,0:T(8,128)(2,1)} custom-call(bf16[8,960,256]{2,1,0:T(8,128)(2,1)} %all-to-all-done.refs_0_.refs_1_.refs_2_.refs_6_.refs_7_.refs_8_, bf16[8,960,256]{2,1,0:T(8,128)(2,1)} %all-to-all-done.refs_0_.refs_1_.refs_2_.refs_6_.refs_7_.refs_8_, ...), custom_call_target="tpu_custom_call" | custom-call | flops 9663676416 | bytes 19660800 | tf_op jit(solution)/shard_map/self_attention/pallas_call | solution.py:218
  367.8 1.0 copy-done.3
  368.7 6.0 %all-to-all-start.1 = ((bf16[8,320,256]{2,1,0:T(8,128)(2,1)}), bf16[8,320,256]{2,1,0:T(8,128)(2,1)S(1)}, u32[]{:S(2)}, u32[]{:S(2)}) async-start(bf16[8,320,256]{2,1,0:T(8,128)(2,1)} %self_attention.2), calls=%async_computation.1 | async-start | bytes 2621440 | tf_op jit(solution)/shard_map/all_to_all | solution.py:533
  374.7 0.0 collective-permute-done.7.b_ref
  374.7 5.4 %merge.4 = (bf16[256,2176]{1,0:T(8,128)(2,1)}, bf16[256,2176]{1,0:T(8,128)(2,1)}) custom-call(bf16[512,2176]{1,0:T(8,128)(2,1)} %get-tuple-element.16.a_ref, bf16[512,2176]{1,0:T(8,128)(2,1)} %collective-permute-done.7.b_ref), custom_call_target="tpu_custom_call" | custom-call | bytes 6684672 | tf_op jit(solution)/shard_map/merge/pallas_call | solution.py:465
  380.1 2.0 collective-permute-start.8
  382.1 33.6 %collective-permute-done.8.b_ref = bf16[256,2176]{1,0:T(8,128)(2,1)} collective-permute-done((bf16[256,2176]{1,0:T(8,128)(2,1)}, bf16[256,2176]{1,0:T(8,128)(2,1)}, u32[]{:S(2)}, u32[]{:S(2)}) %collective-permute-start.8) | collective-permute-done | bytes 1114144 | tf_op jit(solution)/shard_map/ppermute | solution.py:27
  415.7 3.6 merge.5
  419.3 1.1 collective-permute-start.9
  420.4 1.4 dynamic-slice_convert_fusion.2.refs_0_
  421.7 1.4 dynamic-slice_convert_fusion.1.refs_12_
  423.1 10.8 %collective-permute-done.9.b_ref = bf16[128,2176]{1,0:T(8,128)(2,1)} collective-permute-done((bf16[128,2176]{1,0:T(8,128)(2,1)}, bf16[128,2176]{1,0:T(8,128)(2,1)}, u32[]{:S(2)}, u32[]{:S(2)}) %collective-permute-start.9) | collective-permute-done | bytes 557088 | tf_op jit(solution)/shard_map/ppermute | solution.py:27
  433.9 2.6 merge.6
  436.6 2.5 collective-permute-start.10
  439.1 0.0 collective-permute-done.14.refs_6_.refs_7_
  439.1 19.9 %video_cross.1 = bf16[256,2048]{1,0:T(8,128)(2,1)} custom-call(f32[32]{0:T(128)} %slope_ref.3, s32[1]{0:T(128)} %bitcast.9.place_ref, bf16[256,2048]{1,0:T(8,128)(2,1)} %bitcast.29, bf16[256,4096]{1,0:T(8,128)(2,1)} %stack_rows.7.refs_0_.refs_1_, bf16[256,4096]{1,0:T(8,128)(2,1)} %stack_rows.7.refs_0_.refs_1_, ...), custom_call_target="tpu_custom_call" | custom-call | flops 4294967296 | bytes 10485760 | tf_op jit(solution)/shard_map/video_cross/pallas_call | solution.py:297
  459.1 2.2 merge.7
  461.3 0.0 all-to-all-done.1.refs_0_.refs_2_
  461.3 1.1 copy-done.1
  462.4 3.8 unpack.1
  (32 shorter events, 0.1 us)
Async XLA Ops:
  6.9 78.1 %all-to-all-start.2 = ((bf16[8,768,256]{2,1,0:T(8,128)(2,1)}), bf16[8,768,256]{2,1,0:T(8,128)(2,1)}, u32[]{:S(2)}, u32[]{:S(2)}) async-start(bf16[8,768,256]{2,1,0:T(8,128)(2,1)} %pack.3), calls=%async_computation.2 | async-start | bytes 6291456 | tf_op jit(solution)/shard_map/all_to_all | solution.py:533
  20.8 68.8 %copy-start.15 = (s32[1,64]{1,0:T(1,128)S(1)}, s32[1,64]{1,0:T(1,128)}, u32[]{:S(2)}) copy-start(s32[1,64]{1,0:T(1,128)} %param.32) | copy-start | bytes 772
  20.8 68.8 %copy-start.12 = (bf16[1,64,2048]{2,1,0:T(8,128)(2,1)S(1)}, bf16[1,64,2048]{2,1,0:T(8,128)(2,1)}, u32[]{:S(2)}) copy-start(bf16[1,64,2048]{2,1,0:T(8,128)(2,1)} %param.26) | copy-start | bytes 786436
  85.0 136.5 %all-to-all-start = ((bf16[8,960,256]{2,1,0:T(8,128)(2,1)}), bf16[8,960,256]{2,1,0:T(8,128)(2,1)}, u32[]{:S(2)}, u32[]{:S(2)}) async-start(bf16[8,960,256]{2,1,0:T(8,128)(2,1)} %pack.2), calls=%async_computation | async-start | bytes 7864320 | tf_op jit(solution)/shard_map/all_to_all | solution.py:533
  89.7 98.7 %copy-start.5 = (bf16[64,2176]{1,0:T(8,128)(2,1)}, bf16[64,2176]{1,0:T(8,128)(2,1)S(1)}, u32[]{:S(2)}) copy-start(bf16[64,2176]{1,0:T(8,128)(2,1)S(1)} %pad_maximum_fusion.1.refs_0_) | copy-start | bytes 835588
  89.7 98.7 %collective-permute-start.2 = (bf16[64,2176]{1,0:T(8,128)(2,1)S(1)}, bf16[64,2176]{1,0:T(8,128)(2,1)S(1)}, u32[]{:S(2)}, u32[]{:S(2)}) collective-permute-start(bf16[64,2176]{1,0:T(8,128)(2,1)S(1)} %pad_maximum_fusion.1.refs_0_), channel_id=1, source_target_pairs={{0,8},{2,10},{4,12},{6,14},{8,0},{10,2},{12,4},{14,6},{1,9},{3,11}... | collective-permute-start | bytes 835592 | tf_op jit(solution)/shard_map/ppermute | solution.py:27
  188.3 0.7 copy-start.11
  190.9 31.1 %copy-start.13 = (bf16[1,64,2048]{2,1,0:T(8,128)(2,1)S(1)}, bf16[1,64,2048]{2,1,0:T(8,128)(2,1)}, u32[]{:S(2)}) copy-start(bf16[1,64,2048]{2,1,0:T(8,128)(2,1)} %param.31) | copy-start | bytes 786436
  190.9 31.1 %copy-start.14 = (bf16[1,64,2048]{2,1,0:T(8,128)(2,1)S(1)}, bf16[1,64,2048]{2,1,0:T(8,128)(2,1)}, u32[]{:S(2)}) copy-start(bf16[1,64,2048]{2,1,0:T(8,128)(2,1)} %param.30) | copy-start | bytes 786436
  190.9 16.6 %collective-permute-start.5 = (bf16[128,2176]{1,0:T(8,128)(2,1)}, bf16[128,2176]{1,0:T(8,128)(2,1)S(1)}, u32[]{:S(2)}, u32[]{:S(2)}) collective-permute-start(bf16[128,2176]{1,0:T(8,128)(2,1)} %stack_rows.4.refs_0_), channel_id=1, source_target_pairs={{0,6},{2,4},{4,2},{6,0},{8,14},{10,12},{12,10},{14,8},{1,7},{3,5},... | collective-permute-start | bytes 1671176 | tf_op jit(solution)/shard_map/ppermute | solution.py:27
  190.9 25.7 %collective-permute-start.4 = (bf16[128,2176]{1,0:T(8,128)(2,1)}, bf16[128,2176]{1,0:T(8,128)(2,1)S(1)}, u32[]{:S(2)}, u32[]{:S(2)}) collective-permute-start(bf16[128,2176]{1,0:T(8,128)(2,1)} %stack_rows.4.refs_0_), channel_id=1, source_target_pairs={{0,2},{2,0},{4,6},{6,4},{8,10},{10,8},{12,14},{14,12},{1,3},{3,1},... | collective-permute-start | bytes 1671176 | tf_op jit(solution)/shard_map/ppermute | solution.py:27
  192.5 25.2 %collective-permute-start.3 = (bf16[128,2176]{1,0:T(8,128)(2,1)}, bf16[128,2176]{1,0:T(8,128)(2,1)S(1)}, u32[]{:S(2)}, u32[]{:S(2)}) collective-permute-start(bf16[128,2176]{1,0:T(8,128)(2,1)} %stack_rows.4.refs_0_), channel_id=1, source_target_pairs={{0,4},{2,6},{4,0},{6,2},{8,12},{10,14},{12,8},{14,10},{1,5},{3,7},... | collective-permute-start | bytes 1671176 | tf_op jit(solution)/shard_map/ppermute | solution.py:27
  194.4 111.4 %collective-permute-start.1 = (bf16[8,768,256]{2,1,0:T(8,128)(2,1)}, bf16[8,768,256]{2,1,0:T(8,128)(2,1)}, u32[]{:S(2)}, u32[]{:S(2)}) collective-permute-start(bf16[8,768,256]{2,1,0:T(8,128)(2,1)} %all-to-all-done.2.refs_0_.refs_1_.refs_2_), channel_id=1, source_target_pairs={{0,1},{1,0},{2,3},{3,2},{4,5},{5,4},{6,7},{7,6},{8,9},{9,8},{10,11... | collective-permute-start | bytes 9437192 | tf_op jit(solution)/shard_map/ppermute | solution.py:27
  207.5 10.1 %copy-start.7 = (bf16[128,2176]{1,0:T(8,128)(2,1)}, bf16[128,2176]{1,0:T(8,128)(2,1)S(1)}, u32[]{:S(2)}) copy-start(bf16[128,2176]{1,0:T(8,128)(2,1)S(1)} %collective-permute-done.5.refs_3_) | copy-start | bytes 1671172
  216.7 1.0 copy-start.8
  217.7 0.8 copy-start.9
  221.5 60.2 %collective-permute-start.6 = (bf16[512,2176]{1,0:T(8,128)(2,1)}, bf16[512,2176]{1,0:T(8,128)(2,1)S(1)}, u32[]{:S(2)}, u32[]{:S(2)}) collective-permute-start(bf16[512,2176]{1,0:T(8,128)(2,1)} %stack_rows.5.refs_0_.refs_2_.refs_5_), channel_id=1, source_target_pairs={{0,1},{1,0},{2,3},{3,2},{4,5},{5,4},{6,7},{7,6},{8,9},{9,8},{10,11... | collective-permute-start | bytes 6684680 | tf_op jit(solution)/shard_map/ppermute | solution.py:27
  221.5 116.7 %collective-permute-start = (bf16[8,960,256]{2,1,0:T(8,128)(2,1)}, bf16[8,960,256]{2,1,0:T(8,128)(2,1)}, u32[]{:S(2)}, u32[]{:S(2)}) collective-permute-start(bf16[8,960,256]{2,1,0:T(8,128)(2,1)} %all-to-all-done.refs_0_.refs_1_.refs_2_.refs_6_.refs_7_.refs_8_), channel_id=1, source_target_pairs={{0,1},{1,0},{2,3},{3,2},{4,5},{5,4},{6,7},{7,6},{8,9},{9,8},{10,11... | collective-permute-start | bytes 11796488 | tf_op jit(solution)/shard_map/ppermute | solution.py:27
  222.1 26.1 %copy-start.4 = (bf16[64,4096]{1,0:T(8,128)(2,1)}, bf16[64,4096]{1,0:T(8,128)(2,1)S(1)}, u32[]{:S(2)}) copy-start(bf16[64,4096]{1,0:T(8,128)(2,1)S(1)} %pad_maximum_fusion.refs_0_) | copy-start | bytes 1572868
  222.1 26.1 %collective-permute-start.11 = (bf16[64,4096]{1,0:T(8,128)(2,1)S(1)}, bf16[64,4096]{1,0:T(8,128)(2,1)S(1)}, u32[]{:S(2)}, u32[]{:S(2)}) collective-permute-start(bf16[64,4096]{1,0:T(8,128)(2,1)S(1)} %pad_maximum_fusion.refs_0_), channel_id=1, source_target_pairs={{0,8},{2,10},{4,12},{6,14},{8,0},{10,2},{12,4},{14,6},{1,9},{3,11}... | collective-permute-start | bytes 1572872 | tf_op jit(solution)/shard_map/ppermute | solution.py:27
  248.2 0.8 copy-start.10
  251.2 24.7 %collective-permute-start.12 = (bf16[128,4096]{1,0:T(8,128)(2,1)}, bf16[128,4096]{1,0:T(8,128)(2,1)S(1)}, u32[]{:S(2)}, u32[]{:S(2)}) collective-permute-start(bf16[128,4096]{1,0:T(8,128)(2,1)} %stack_rows.6.refs_0_), channel_id=1, source_target_pairs={{0,4},{2,6},{4,0},{6,2},{8,12},{10,14},{12,8},{14,10},{1,5},{3,7},... | collective-permute-start | bytes 3145736 | tf_op jit(solution)/shard_map/ppermute | solution.py:27
  276.0 1.0 copy-start.6
  280.0 57.9 %collective-permute-start.13 = (bf16[256,4096]{1,0:T(8,128)(2,1)}, bf16[256,4096]{1,0:T(8,128)(2,1)}, u32[]{:S(2)}, u32[]{:S(2)}) collective-permute-start(bf16[256,4096]{1,0:T(8,128)(2,1)} %stack_rows.7.refs_0_.refs_1_), channel_id=1, source_target_pairs={{0,2},{2,0},{4,6},{6,4},{8,10},{10,8},{12,14},{14,12},{1,3},{3,1},... | collective-permute-start | bytes 6291464 | tf_op jit(solution)/shard_map/ppermute | solution.py:27
  281.7 1.4 copy-start.2
  305.8 68.9 %collective-permute-start.7 = (bf16[512,2176]{1,0:T(8,128)(2,1)}, bf16[512,2176]{1,0:T(8,128)(2,1)}, u32[]{:S(2)}, u32[]{:S(2)}) collective-permute-start(bf16[512,2176]{1,0:T(8,128)(2,1)} %get-tuple-element.17), channel_id=1, source_target_pairs={{0,1},{1,0},{2,3},{3,2},{4,5},{5,4},{6,7},{7,6},{8,9},{9,8},{10,11... | collective-permute-start | bytes 6684680 | tf_op jit(solution)/shard_map/ppermute | solution.py:27
  331.8 5.8 %copy-start = (bf16[256,4096]{1,0:T(8,128)(2,1)S(1)}, bf16[256,4096]{1,0:T(8,128)(2,1)}, u32[]{:S(2)}) copy-start(bf16[256,4096]{1,0:T(8,128)(2,1)} %stack_rows.7.refs_0_.refs_1_) | copy-start | bytes 6291460
  331.8 35.9 %all-to-all-start.3 = ((bf16[8,256,256]{2,1,0:T(8,128)(2,1)}), bf16[8,256,256]{2,1,0:T(8,128)(2,1)S(1)}, u32[]{:S(2)}, u32[]{:S(2)}) async-start(bf16[8,256,256]{2,1,0:T(8,128)(2,1)} %self_attention.3), calls=%async_computation.3 | async-start | bytes 2097152 | tf_op jit(solution)/shard_map/all_to_all | solution.py:533
  337.7 101.4 %collective-permute-start.14 = (bf16[256,4096]{1,0:T(8,128)(2,1)S(1)}, bf16[256,4096]{1,0:T(8,128)(2,1)}, u32[]{:S(2)}, u32[]{:S(2)}) collective-permute-start(bf16[256,4096]{1,0:T(8,128)(2,1)S(1)} %copy-done), channel_id=1, source_target_pairs={{0,1},{1,0},{2,3},{3,2},{4,5},{5,4},{6,7},{7,6},{8,9},{9,8},{10,11... | collective-permute-start | bytes 6291464 | tf_op jit(solution)/shard_map/ppermute | solution.py:27
  337.9 101.2 %collective-permute-start.15 = (bf16[256,4096]{1,0:T(8,128)(2,1)}, bf16[256,4096]{1,0:T(8,128)(2,1)}, u32[]{:S(2)}, u32[]{:S(2)}) collective-permute-start(bf16[256,4096]{1,0:T(8,128)(2,1)} %collective-permute-done.13.refs_3_.refs_4_), channel_id=1, source_target_pairs={{0,1},{1,0},{2,3},{3,2},{4,5},{5,4},{6,7},{7,6},{8,9},{9,8},{10,11... | collective-permute-start | bytes 6291464 | tf_op jit(solution)/shard_map/ppermute | solution.py:27
  367.7 1.0 copy-start.3
  368.7 92.6 %all-to-all-start.1 = ((bf16[8,320,256]{2,1,0:T(8,128)(2,1)}), bf16[8,320,256]{2,1,0:T(8,128)(2,1)S(1)}, u32[]{:S(2)}, u32[]{:S(2)}) async-start(bf16[8,320,256]{2,1,0:T(8,128)(2,1)} %self_attention.2), calls=%async_computation.1 | async-start | bytes 2621440 | tf_op jit(solution)/shard_map/all_to_all | solution.py:533
  380.1 35.6 %collective-permute-start.8 = (bf16[256,2176]{1,0:T(8,128)(2,1)}, bf16[256,2176]{1,0:T(8,128)(2,1)}, u32[]{:S(2)}, u32[]{:S(2)}) collective-permute-start(bf16[256,2176]{1,0:T(8,128)(2,1)} %get-tuple-element.19), channel_id=1, source_target_pairs={{0,2},{2,0},{4,6},{6,4},{8,10},{10,8},{12,14},{14,12},{1,3},{3,1},... | collective-permute-start | bytes 3342344 | tf_op jit(solution)/shard_map/ppermute | solution.py:27
  419.3 14.7 %collective-permute-start.9 = (bf16[128,2176]{1,0:T(8,128)(2,1)}, bf16[128,2176]{1,0:T(8,128)(2,1)}, u32[]{:S(2)}, u32[]{:S(2)}) collective-permute-start(bf16[128,2176]{1,0:T(8,128)(2,1)} %get-tuple-element.21), channel_id=1, source_target_pairs={{0,4},{2,6},{4,0},{6,2},{8,12},{10,14},{12,8},{14,10},{1,5},{3,7},... | collective-permute-start | bytes 1671176 | tf_op jit(solution)/shard_map/ppermute | solution.py:27
  436.6 22.5 %collective-permute-start.10 = (bf16[64,2176]{1,0:T(8,128)(2,1)}, bf16[64,2176]{1,0:T(8,128)(2,1)}, u32[]{:S(2)}, u32[]{:S(2)}) collective-permute-start(bf16[64,2176]{1,0:T(8,128)(2,1)} %get-tuple-element.23), channel_id=1, source_target_pairs={{0,8},{2,10},{4,12},{6,14},{8,0},{10,2},{12,4},{14,6},{1,9},{3,11}... | collective-permute-start | bytes 835592 | tf_op jit(solution)/shard_map/ppermute | solution.py:27
  461.3 1.1 copy-start.1
